TPU v7x, 32 devices: a whole 2x2x4 slice. The times are simulated.
32 devices in a mesh: dp: 16 (over z, x, core), tensor: 2 (over y).
Axes of the slice: x: 2, y: 2, z: 4, core: 2. Of those that a mesh axis runs over, the one named last changes fastest.
Arguments:
- inputs: float32 [32, 680, 1024], P('dp', 'tensor'), may hold values from -6 to 6
- labels: int32 [32], P('dp'), may hold values from 0 to 999
- scale_ids: int32 [32, 680], P('dp'), may hold values from 0 to 9, never falling along the last dimension, each value on 1 to 256 neighbouring positions
- cotangent: float32 [32, 680, 1024], P('dp', 'tensor'), may hold values from -6 to 6
- table: float32 [1000, 1024], P(None, 'dp'), may hold values from -6 to 6
- w_ada: float32 [1024, 6, 1024], P('dp'), may hold values from -0.1875 to 0.1875
- w_qkv: float32 [1024, 3, 1024], P('dp', None, 'tensor'), may hold values from -0.1875 to 0.1875
- head_scale: float32 [16], P('tensor'), may hold values from 6 to 12
- w_proj: float32 [1024, 1024], P('tensor', 'dp'), may hold values from -0.375 to 0.375
- w_fc1: float32 [1024, 4096], P('dp', 'tensor'), may hold values from -0.1875 to 0.1875
- w_fc2: float32 [4096, 1024], P('tensor', 'dp'), may hold values from -0.125 to 0.125
Outputs:
- output: float32 [32, 680, 1024], P('dp', 'tensor')
- d_inputs: float32 [32, 680, 1024], P('dp', 'tensor')
- d_table: float32 [1000, 1024], P(None, 'dp')
- d_ada: float32 [1024, 6, 1024], P('dp')
- d_qkv: float32 [1024, 3, 1024], P('dp', None, 'tensor')
- d_scale: float32 [16], P('tensor')
- d_proj: float32 [1024, 1024], P('tensor', 'dp')
- d_fc1: float32 [1024, 4096], P('dp', 'tensor')
- d_fc2: float32 [4096, 1024], P('tensor', 'dp')
Inputs may be any that keep to these rules, and one draw needn't show every extreme that they name: `scale_ids`: each image's scale ids never fall along its tokens; every scale occurs, with 1 to 256 tokens, one scale with exactly 256; the scales' lengths vary from image to image, a generalization of VAR's fixed pyramid.
All inputs are finite; a program needn't handle non-finite values.
Results may differ from a plain program's by a relative error of at most 0.03.
Values may be sent and summed in bfloat16 or wider, within the bound.
No kernel may reach another device: no remote copies, remote signals or barrier semaphores. Data moves between devices by JAX's collectives and lax.ppermute only.
A program may use at most 256 MiB of HBM per device.

v0:
```python
import functools

import jax
import jax.numpy as jnp
from jax import lax
from jax.sharding import PartitionSpec as P

EPSILON = 1e-06
HIGHEST = lax.Precision.HIGHEST


def layer_norm(values):
    average = jnp.mean(values, axis=-1, keepdims=True)
    centred = values - average
    inverse = lax.rsqrt(jnp.mean(centred * centred, axis=-1, keepdims=True) + EPSILON)
    return (centred * inverse, inverse)


def norm_back(d_normed, normed, inverse):
    return inverse * (
        d_normed
        - jnp.mean(d_normed, axis=-1, keepdims=True)
        - normed * jnp.mean(d_normed * normed, axis=-1, keepdims=True)
    )


def unit_rows(values):
    inverse = lax.rsqrt(jnp.sum(values * values, axis=-1, keepdims=True) + EPSILON)
    return (values * inverse, inverse)


def unit_back(d_unit, unit, inverse):
    return inverse * (d_unit - unit * jnp.sum(d_unit * unit, axis=-1, keepdims=True))


def spread(values):
    return lax.all_gather(values, "tensor", axis=1, tiled=True)


def collect(terms):
    return lax.psum_scatter(
        terms.astype(jnp.bfloat16), "tensor", scatter_dimension=1, tiled=True
    ).astype(jnp.float32)


def masked_scores(queries, keys_in, scale_row):
    scores = jnp.einsum("qhd,khd->hqk", queries, keys_in, preferred_element_type=jnp.float32)
    visible = scale_row[None, :] <= scale_row[:, None]
    return jnp.where(visible[None], scores, -1e30)


def attend_forward(pieces):
    queries, keys_in, values_in, scale_row = pieces
    scores = masked_scores(queries, keys_in, scale_row)
    largest = jnp.max(scores, axis=-1, keepdims=True)
    exponent = jnp.exp(scores - largest)
    denominator = jnp.sum(exponent, axis=-1, keepdims=True)
    attn_probs = (exponent / denominator).astype(jnp.bfloat16)
    mixed = jnp.einsum("hqk,khd->qhd", attn_probs, values_in, preferred_element_type=jnp.float32)
    return (mixed.astype(jnp.bfloat16), (largest + jnp.log(denominator))[..., 0])


def attend_backward(pieces):
    queries, keys_in, values_in, scale_row, log_total, d_mixed = pieces
    scores = masked_scores(queries, keys_in, scale_row)
    attn_probs = jnp.exp(scores - log_total[..., None])
    d_probs = jnp.einsum("qhd,khd->hqk", d_mixed, values_in, preferred_element_type=jnp.float32)
    offset = jnp.sum(attn_probs * d_probs, axis=-1, keepdims=True)
    d_scores = (attn_probs * (d_probs - offset)).astype(jnp.bfloat16)
    d_queries = jnp.einsum("hqk,khd->qhd", d_scores, keys_in, preferred_element_type=jnp.float32)
    d_keys = jnp.einsum("hqk,qhd->khd", d_scores, queries, preferred_element_type=jnp.float32)
    d_values = jnp.einsum(
        "hqk,qhd->khd", attn_probs.astype(jnp.bfloat16), d_mixed, preferred_element_type=jnp.float32
    )
    return (d_queries, d_keys, d_values)


def on_device(
    inputs, labels, scale_ids, cotangent, table, w_ada, w_qkv, head_scale, w_proj, w_fc1, w_fc2
):
    images, local_len, model_width = inputs.shape
    full_len = scale_ids.shape[1]
    local_heads = head_scale.shape[0]
    head_dim = w_qkv.shape[2] // local_heads
    classes = table.shape[0]
    gathered = (
        lax.all_gather(table.astype(jnp.bfloat16), "dp", axis=1, tiled=True),
        lax.all_gather(w_qkv.astype(jnp.bfloat16), "dp", axis=0, tiled=True),
        lax.all_gather(w_proj.astype(jnp.bfloat16), "dp", axis=1, tiled=True),
        lax.all_gather(w_fc1.astype(jnp.bfloat16), "dp", axis=0, tiled=True),
        lax.all_gather(w_fc2.astype(jnp.bfloat16), "dp", axis=1, tiled=True),
    )
    table_low, qkv_low, proj_low, fc1_low, fc2_low = gathered
    qkv_flat = qkv_low.reshape(model_width, -1)
    one_hot = labels[:, None] == jnp.arange(classes)[None, :]
    condition = jnp.dot(one_hot.astype(jnp.bfloat16), table_low, preferred_element_type=jnp.float32)
    silu_low = jax.nn.silu(condition).astype(jnp.bfloat16)
    ada_full = lax.all_gather(w_ada.astype(jnp.bfloat16), "dp", axis=0, tiled=True).reshape(
        model_width, 6 * model_width
    )
    modulation = jnp.dot(silu_low, ada_full, preferred_element_type=jnp.float32)
    modulation = modulation.reshape(images, 6, model_width)
    gain_attn = modulation[:, 0, None, :]
    gain_mlp = modulation[:, 1, None, :]
    scale_attn = modulation[:, 2, None, :]
    scale_mlp = modulation[:, 3, None, :]
    shift_attn = modulation[:, 4, None, :]
    shift_mlp = modulation[:, 5, None, :]
    normed_one, inverse_one = layer_norm(inputs)
    hidden_one = spread((normed_one * (1.0 + scale_attn) + shift_attn).astype(jnp.bfloat16))
    projected = jnp.einsum("bld,dc->blc", hidden_one, qkv_flat, preferred_element_type=jnp.float32)
    projected = projected.reshape(images, full_len, 3, local_heads, head_dim)
    q_unit, q_inverse = unit_rows(projected[:, :, 0])
    k_unit, k_inverse = unit_rows(projected[:, :, 1])
    q_hat = (q_unit * head_scale[:, None]).astype(jnp.bfloat16)
    k_hat = k_unit.astype(jnp.bfloat16)
    v_hat = projected[:, :, 2].astype(jnp.bfloat16)
    mixed, log_total = lax.map(attend_forward, (q_hat, k_hat, v_hat, scale_ids))
    mixed_flat = mixed.reshape(images, full_len, local_heads * head_dim)
    attended = collect(
        jnp.einsum("blc,cd->bld", mixed_flat, proj_low, preferred_element_type=jnp.float32)
    )
    middle = inputs + gain_attn * attended
    normed_two, inverse_two = layer_norm(middle)
    hidden_two = spread((normed_two * (1.0 + scale_mlp) + shift_mlp).astype(jnp.bfloat16))
    before = jnp.einsum("bld,df->blf", hidden_two, fc1_low, preferred_element_type=jnp.float32)
    gelu_fn = functools.partial(jax.nn.gelu, approximate=True)
    active_f, gelu_pull = jax.vjp(gelu_fn, before)
    active = active_f.astype(jnp.bfloat16)
    branch = collect(jnp.einsum("blf,fd->bld", active, fc2_low, preferred_element_type=jnp.float32))
    output = middle + gain_mlp * branch
    again = (
        lax.all_gather(w_qkv.astype(jnp.bfloat16), "dp", axis=0, tiled=True),
        lax.all_gather(w_proj.astype(jnp.bfloat16), "dp", axis=1, tiled=True),
        lax.all_gather(w_fc1.astype(jnp.bfloat16), "dp", axis=0, tiled=True),
        lax.all_gather(w_fc2.astype(jnp.bfloat16), "dp", axis=1, tiled=True),
    )
    qkv_back, proj_back, fc1_back, fc2_back = again
    d_gain_mlp = jnp.sum(cotangent * branch, axis=1)
    d_branch = spread((gain_mlp * cotangent).astype(jnp.bfloat16))
    grad_fc2 = jnp.einsum("blf,bld->fd", active, d_branch, preferred_element_type=jnp.float32)
    d_active = jnp.einsum("bld,fd->blf", d_branch, fc2_back, preferred_element_type=jnp.float32)
    d_before = gelu_pull(d_active)[0].astype(jnp.bfloat16)
    grad_fc1 = jnp.einsum("bld,blf->df", hidden_two, d_before, preferred_element_type=jnp.float32)
    d_hidden_two = collect(
        jnp.einsum("blf,df->bld", d_before, fc1_back, preferred_element_type=jnp.float32)
    )
    d_scale_mlp = jnp.sum(d_hidden_two * normed_two, axis=1)
    d_shift_mlp = jnp.sum(d_hidden_two, axis=1)
    d_middle = cotangent + norm_back(d_hidden_two * (1.0 + scale_mlp), normed_two, inverse_two)
    d_gain_attn = jnp.sum(d_middle * attended, axis=1)
    d_attended = spread((gain_attn * d_middle).astype(jnp.bfloat16))
    grad_proj = jnp.einsum(
        "blc,bld->cd", mixed_flat, d_attended, preferred_element_type=jnp.float32
    )
    d_mixed = jnp.einsum("bld,cd->blc", d_attended, proj_back, preferred_element_type=jnp.float32)
    d_mixed = d_mixed.astype(jnp.bfloat16).reshape(images, full_len, local_heads, head_dim)
    d_q_hat, d_k_hat, d_v_hat = lax.map(
        attend_backward, (q_hat, k_hat, v_hat, scale_ids, log_total, d_mixed)
    )
    scale_terms = jnp.sum(d_q_hat * q_unit, axis=(0, 1, 3))
    d_query = unit_back(d_q_hat * head_scale[:, None], q_unit, q_inverse)
    d_key = unit_back(d_k_hat, k_unit, k_inverse)
    d_raw = jnp.stack([d_query, d_key, d_v_hat], axis=2).astype(jnp.bfloat16)
    d_raw = d_raw.reshape(images, full_len, 3 * local_heads * head_dim)
    grad_qkv = jnp.einsum("bld,blc->dc", hidden_one, d_raw, preferred_element_type=jnp.float32)
    grad_qkv = grad_qkv.reshape(model_width, 3, local_heads * head_dim)
    d_hidden_one = collect(
        jnp.einsum(
            "blc,dc->bld",
            d_raw,
            qkv_back.reshape(model_width, -1),
            preferred_element_type=jnp.float32,
        )
    )
    d_scale_attn = jnp.sum(d_hidden_one * normed_one, axis=1)
    d_shift_attn = jnp.sum(d_hidden_one, axis=1)
    d_inputs = d_middle + norm_back(d_hidden_one * (1.0 + scale_attn), normed_one, inverse_one)
    mod_terms_back = jnp.stack(
        [d_gain_attn, d_gain_mlp, d_scale_attn, d_scale_mlp, d_shift_attn, d_shift_mlp], axis=1
    )
    d_modulation = lax.psum(mod_terms_back.astype(jnp.bfloat16), "tensor").astype(jnp.float32)
    d_mod_flat = d_modulation.reshape(images, 6 * model_width)
    grad_scale = lax.psum(scale_terms, "dp")
    ada_terms = jnp.dot(silu_low.astype(jnp.float32).T, d_mod_flat, precision=HIGHEST)
    grad_ada = lax.psum_scatter(
        ada_terms.reshape(model_width, 6, model_width).astype(jnp.bfloat16),
        "dp",
        scatter_dimension=0,
        tiled=True,
    ).astype(jnp.float32)
    d_silu = jnp.dot(d_mod_flat, ada_full.astype(jnp.float32).T, precision=HIGHEST)
    _, silu_pull = jax.vjp(jax.nn.silu, condition)
    d_condition = silu_pull(d_silu)[0]
    table_terms = jnp.dot(one_hot.astype(jnp.float32).T, d_condition, precision=HIGHEST)
    summed = (
        lax.psum_scatter(
            table_terms.astype(jnp.bfloat16), "dp", scatter_dimension=1, tiled=True
        ).astype(jnp.float32),
        lax.psum_scatter(
            grad_qkv.astype(jnp.bfloat16), "dp", scatter_dimension=0, tiled=True
        ).astype(jnp.float32),
        lax.psum_scatter(
            grad_proj.astype(jnp.bfloat16), "dp", scatter_dimension=1, tiled=True
        ).astype(jnp.float32),
        lax.psum_scatter(
            grad_fc1.astype(jnp.bfloat16), "dp", scatter_dimension=0, tiled=True
        ).astype(jnp.float32),
        lax.psum_scatter(
            grad_fc2.astype(jnp.bfloat16), "dp", scatter_dimension=1, tiled=True
        ).astype(jnp.float32),
    )
    grad_table, grad_qkv_own, grad_proj_own, grad_fc1_own, grad_fc2_own = summed
    return (
        output,
        d_inputs,
        grad_table,
        grad_ada,
        grad_qkv_own,
        grad_scale,
        grad_proj_own,
        grad_fc1_own,
        grad_fc2_own,
    )


def solution(mesh):
    placed = (
        P("dp", "tensor", None),
        P("dp"),
        P("dp", None),
        P("dp", "tensor", None),
        P(None, "dp"),
        P("dp", None, None),
        P("dp", None, "tensor"),
        P("tensor"),
        P("tensor", "dp"),
        P("dp", "tensor"),
        P("tensor", "dp"),
    )
    return jax.shard_map(
        on_device,
        mesh=mesh,
        in_specs=placed,
        out_specs=(
            P("dp", "tensor", None),
            P("dp", "tensor", None),
            P(None, "dp"),
            P("dp", None, None),
            P("dp", None, "tensor"),
            P("tensor"),
            P("tensor", "dp"),
            P("dp", "tensor"),
            P("tensor", "dp"),
        ),
        check_vma=False,
    )
```

profile of v0, /device:TPU:9, one launch (start us, length us, event | category | flops | bytes accessed | tf_op | source)
XLA Modules:
  0.0 1515.7 jit_solution(9431631226440730742)
XLA Ops:
  14.9 38.0 %all-gather.11.cloned.1.call-done = bf16[1000,1024]{0,1:T(8,128)(2,1)} async-done(((bf16[1000,64]{0,1:T(8,128)(2,1)}), bf16[1000,1024]{0,1:T(8,128)(2,1)}) %all-gather.11.cloned.1.call-update) | async-done | bytes 2048016 | tf_op jit(solution)/shard_map/all_gather | solution.py:87
  55.1 99.7 %all-gather.13.cloned.1.call-done = bf16[1024,6,1024]{2,0,1:T(8,128)(2,1)} async-done(((bf16[64,6,1024]{2,0,1:T(8,128)(2,1)}), bf16[1024,6,1024]{2,0,1:T(8,128)(2,1)}) %all-gather.13.cloned.1.call-update) | async-done | bytes 12582928 | tf_op jit(solution)/shard_map/all_gather | solution.py:98
  154.8 16.7 %copy.63 = bf16[1024,6,1024]{0,2,1:T(8,128)(2,1)} copy(bf16[1024,6,1024]{2,0,1:T(8,128)(2,1)} %all-gather.13.cloned.1.call-done) | data formatting | bytes 25165824 | tf_op jit(solution)/shard_map/all_gather | solution.py:98
  184.8 17.9 %all-gather.17.cloned.1.call-done = bf16[1024,3,512]{2,0,1:T(8,128)(2,1)} async-done(((bf16[64,3,512]{2,0,1:T(8,128)(2,1)}), bf16[1024,3,512]{2,0,1:T(8,128)(2,1)}) %all-gather.17.cloned.1.call-update) | async-done | bytes 3145744 | tf_op jit(solution)/shard_map/all_gather | solution.py:88
  205.9 37.7 %all-gather.15.cloned.1.call-done = bf16[2,680,1024]{2,0,1:T(2,128)(2,1)} async-done(((bf16[2,340,1024]{2,0,1:T(2,128)(2,1)}), bf16[2,680,1024]{2,0,1:T(2,128)(2,1)}) %all-gather.15.cloned.1.call-update) | async-done | bytes 2785296 | tf_op jit(solution)/shard_map/all_gather | solution.py:37
  256.7 56.2 %while.26 = (s32[]{:T(128)}, bf16[2,680,8,64]{1,3,2,0:T(8,128)(2,1)}, f32[2,8,680]{2,1,0:T(8,128)S(1)}, bf16[2,680,8,64]{1,3,2,0:T(8,128)(2,1)}, s32[2,680]{1,0:...) while((s32[]{:T(128)}, ...), condition=%wide.region_7.8_spmd, body=%wide.region_4.7_spmd.sunk | while | flops 981093120 | bytes 51553284 | solution.py:118
  323.1 76.0 %all-reduce.9.cloned.1.call-done = bf16[2,680,1024]{2,0,1:T(2,128)(2,1)} async-done(((bf16[2,680,1024]{2,0,1:T(2,128)(2,1)}), bf16[2,680,1024]{2,0,1:T(2,128)(2,1)}) %all-reduce.9.cloned.1.call-update) | async-done | bytes 2785296
  413.0 39.9 %all-gather.23.cloned.1.call-done = bf16[1024,2048]{1,0:T(8,128)(2,1)} async-done(((bf16[64,2048]{1,0:T(8,128)(2,1)}), bf16[1024,2048]{1,0:T(8,128)(2,1)}) %all-gather.23.cloned.1.call-update) | async-done | bytes 4194320 | tf_op jit(solution)/shard_map/all_gather | solution.py:90
  453.0 41.1 %all-gather.21.cloned.1.call-done = bf16[2,680,1024]{2,0,1:T(2,128)(2,1)} async-done(((bf16[2,340,1024]{2,0,1:T(2,128)(2,1)}), bf16[2,680,1024]{2,0,1:T(2,128)(2,1)}) %all-gather.21.cloned.1.call-update) | async-done | bytes 2785296 | tf_op jit(solution)/shard_map/all_gather | solution.py:37
  505.3 42.7 %all-gather.25.cloned.1.call-done = bf16[2048,1024]{0,1:T(8,128)(2,1)} async-done(((bf16[2048,64]{0,1:T(8,128)(2,1)}), bf16[2048,1024]{0,1:T(8,128)(2,1)}) %all-gather.25.cloned.1.call-update) | async-done | bytes 4194320 | tf_op jit(solution)/shard_map/all_gather | solution.py:91
  548.0 40.4 %all-gather.27.cloned.1.call-done = bf16[2,680,1024]{2,0,1:T(2,128)(2,1)} async-done(((bf16[2,340,1024]{2,0,1:T(2,128)(2,1)}), bf16[2,680,1024]{2,0,1:T(2,128)(2,1)}) %all-gather.27.cloned.1.call-update) | async-done | bytes 2785296 | tf_op jit(solution)/shard_map/all_gather | solution.py:37
  588.3 16.5 %fusion.55 = bf16[2,680,2048]{2,1,0:T(8,128)(2,1)S(1)} fusion(f32[2,680,2048]{2,1,0:T(8,128)} %fusion.61, bf16[2048,1024]{0,1:T(8,128)(2,1)} %all-gather.25.cloned.1.call-done, bf16[2,680,1024]{2,0,1:T(2,128)(2,1)} %all-gather.27.cloned.1.call-done), kind=kOutput, calls=%fused_computation.69 | convolution fusion | flops 5759959040 | bytes 23691264 | tf_op jit(solution)/shard_map/bld,fd->blf/dot_general | solution.py:142
  616.0 78.0 %all-reduce.11.cloned.1.call-done = bf16[2,680,1024]{2,0,1:T(2,128)(2,1)} async-done(((bf16[2,680,1024]{2,0,1:T(2,128)(2,1)}), bf16[2,680,1024]{2,0,1:T(2,128)(2,1)}) %all-reduce.11.cloned.1.call-update) | async-done | bytes 2785296
  732.4 25.3 %all-gather.29.cloned.1.call-done = bf16[2,680,1024]{2,0,1:T(2,128)(2,1)} async-done(((bf16[2,340,1024]{2,0,1:T(2,128)(2,1)}), bf16[2,680,1024]{2,0,1:T(2,128)(2,1)}) %all-gather.29.cloned.1.call-update) | async-done | bytes 2785296 | tf_op jit(solution)/shard_map/all_gather | solution.py:37
  763.0 98.1 %while.27 = (s32[]{:T(128)}, f32[2,680,8,64]{1,3,2,0:T(8,128)}, f32[2,680,8,64]{1,3,2,0:T(8,128)}, bf16[2,680,8,64]{1,3,2,0:T(8,128)(2,1)}, bf16[2,680,8,64]{1,3...) while((s32[]{:T(128)}, f32[2,680,8,64]{1,3,2,0:T(8,128)}, ...), condition=%wide.region_17.18_spmd, body=%wide.region_15.17_spmd.sunk | while | flops 2412335360 | bytes 217013808 | solution.py:158
  782.4 13.2 multiply_reduce_fusion.9
  831.3 13.2 multiply_reduce_fusion.9
  931.6 92.2 %all-reduce.13.cloned.1.call-done = (bf16[2,680,1024]{2,0,1:T(2,128)(2,1)}, bf16[2,680,1024]{2,0,1:T(2,128)(2,1)}) async-done(((bf16[2,680,1024]{2,0,1:T(2,128)(2,1)}, bf16[2,680,1024]{2,0,1:T(2,128)(2,1)}), (bf16[2,680,1024]{2,0,1:T(2,128)(2,1)}, bf16[2,680,1024]{2,0,1:T(2,128)(2,1)})) %all-reduce.13.cloned.1.call-update) | async-done | bytes 5570576
  1075.1 25.8 %psum.15 = f32[8]{0:T(128)} all-reduce(f32[8]{0:T(128)S(1)} %multiply_reduce_fusion.1), channel_id=1, replica_groups=mesh['dp'=16,'tensor'=2] {'dp'}, use_global_device_ids=true, to_apply=%region_34.35 | all-reduce | flops 8 | bytes 64 | tf_op jit(solution)/shard_map/psum | solution.py:184
  1102.6 71.2 %reduce-scatter.15.cloned.1.call-done = bf16[64,2048]{1,0:T(8,128)(2,1)} async-done(((bf16[1024,2048]{1,0:T(8,128)(2,1)}), bf16[64,2048]{1,0:T(8,128)(2,1)}) %reduce-scatter.15.cloned.1.call-update) | async-done | bytes 262160 | tf_op jit(solution)/shard_map/reduce_scatter | solution.py:206
  1175.6 58.0 %reduce-scatter.13.cloned.1.call-done = bf16[512,64]{0,1:T(8,128)(2,1)} async-done(((bf16[512,1024]{0,1:T(8,128)(2,1)}), bf16[512,64]{0,1:T(8,128)(2,1)}) %reduce-scatter.13.cloned.1.call-update) | async-done | bytes 65552 | tf_op jit(solution)/shard_map/reduce_scatter | solution.py:203
  1235.2 67.8 %reduce-scatter.11.cloned.1.call-done = bf16[64,3,512]{2,0,1:T(8,128)(2,1)} async-done(((bf16[1024,3,512]{2,0,1:T(8,128)(2,1)}), bf16[64,3,512]{2,0,1:T(8,128)(2,1)}) %reduce-scatter.11.cloned.1.call-update) | async-done | bytes 196624 | tf_op jit(solution)/shard_map/reduce_scatter | solution.py:200
  1311.1 56.3 %reduce-scatter.7.cloned.1.call-done = bf16[1000,64]{0,1:T(8,128)(2,1)} async-done(((bf16[1000,1024]{0,1:T(8,128)(2,1)}), bf16[1000,64]{0,1:T(8,128)(2,1)}) %reduce-scatter.7.cloned.1.call-update) | async-done | bytes 128016 | tf_op jit(solution)/shard_map/reduce_scatter | solution.py:197
  1369.1 137.4 %reduce-scatter.9.cloned.1.call-done = bf16[64,6,1024]{2,0,1:T(8,128)(2,1)} async-done(((bf16[1024,6,1024]{2,0,1:T(8,128)(2,1)}), bf16[64,6,1024]{2,0,1:T(8,128)(2,1)}) %reduce-scatter.9.cloned.1.call-update) | async-done | bytes 786448 | tf_op jit(solution)/shard_map/reduce_scatter | solution.py:186
  (280 shorter events, 393.6 us)
Async XLA Ops:
  7.2 45.6 %all-gather.11.cloned.1.call-start = ((), (), s32[]{:S(2)}) async-start(), calls=%async_computation.6 | async-start | bytes 2228224 | tf_op jit(solution)/shard_map/all_gather | solution.py:87
  9.0 145.8 %all-gather.13.cloned.1.call-start = ((), (), s32[]{:S(2)}) async-start(), calls=%async_computation.7 | async-start | bytes 13369344 | tf_op jit(solution)/shard_map/all_gather | solution.py:98
  11.5 191.2 %all-gather.17.cloned.1.call-start = ((), (), s32[]{:S(2)}) async-start(), calls=%async_computation.9 | async-start | bytes 3342336 | tf_op jit(solution)/shard_map/all_gather | solution.py:88
  12.3 231.3 %all-gather.15.cloned.1.call-start = ((), (), s32[]{:S(2)}) async-start(), calls=%async_computation.8 | async-start | bytes 4177920 | tf_op jit(solution)/shard_map/all_gather | solution.py:37
  13.2 166.9 %copy-start.13 = (f32[2,340]{0,1:T(8,128)}, f32[2,340]{0,1:T(8,128)S(1)}, u32[]{:S(2)}) copy-start(f32[2,340]{0,1:T(8,128)S(1)} %broadcast_multiply_fusion.5) | copy-start | bytes 8164
  14.9 165.2 %copy-start.20 = (f32[2,340]{0,1:T(8,128)}, f32[2,340]{0,1:T(8,128)S(1)}, u32[]{:S(2)}) copy-start(f32[2,340]{0,1:T(8,128)S(1)} %add_rsqrt_fusion.1) | copy-start | bytes 8164
  55.1 116.4 %copy-start.34 = (f32[2,1024]{1,0:T(2,128)}, f32[2,1024]{1,0:T(2,128)S(1)}, u32[]{:S(2)}) copy-start(f32[2,1024]{1,0:T(2,128)S(1)} %fusion.135) | copy-start | bytes 24580
  183.8 129.1 %all-gather.19.cloned.1.call-start = ((), (), s32[]{:S(2)}) async-start(), calls=%async_computation.10 | async-start | bytes 1114112 | tf_op jit(solution)/shard_map/all_gather | solution.py:89
  184.5 214.5 %all-reduce.9.cloned.1.call-start = ((), (), s32[]{:S(2)}) async-start(), calls=%async_computation.22 | async-start | bytes 5570560
  321.0 132.0 %all-gather.23.cloned.1.call-start = ((), (), s32[]{:S(2)}) async-start(), calls=%async_computation.12 | async-start | bytes 4456448 | tf_op jit(solution)/shard_map/all_gather | solution.py:90
  321.8 172.3 %all-gather.21.cloned.1.call-start = ((), (), s32[]{:S(2)}) async-start(), calls=%async_computation.11 | async-start | bytes 4177920 | tf_op jit(solution)/shard_map/all_gather | solution.py:37
  408.1 139.9 %all-gather.25.cloned.1.call-start = ((), (), s32[]{:S(2)}) async-start(), calls=%async_computation.13 | async-start | bytes 4456448 | tf_op jit(solution)/shard_map/all_gather | solution.py:91
  408.9 179.4 %all-gather.27.cloned.1.call-start = ((), (), s32[]{:S(2)}) async-start(), calls=%async_computation.14 | async-start | bytes 4177920 | tf_op jit(solution)/shard_map/all_gather | solution.py:37
  413.0 281.0 %all-reduce.11.cloned.1.call-start = ((), (), s32[]{:S(2)}) async-start(), calls=%async_computation.23 | async-start | bytes 5570560
  615.9 141.7 %all-gather.29.cloned.1.call-start = ((), (), s32[]{:S(2)}) async-start(), calls=%async_computation.15 | async-start | bytes 4177920 | tf_op jit(solution)/shard_map/all_gather | solution.py:37
  716.6 307.2 %all-reduce.13.cloned.1.call-start = ((), (), s32[]{:S(2)}) async-start(), calls=%async_computation.24 | async-start | bytes 11141120
  763.0 98.1 %copy-start.27 = (f32[2,680,8]{1,2,0:T(8,128)S(1)}, f32[2,680,8]{1,2,0:T(8,128)}, u32[]{:S(2)}) copy-start(f32[2,680,8]{1,2,0:T(8,128)} %copy-done.26) | copy-start | bytes 130564
  885.7 215.2 %reduce-scatter.17.cloned.1.call-start = ((), (), s32[]{:S(2)}) async-start(), calls=%async_computation.21 | async-start | bytes 4456448 | tf_op jit(solution)/shard_map/reduce_scatter | solution.py:209
  899.3 274.5 %reduce-scatter.15.cloned.1.call-start = ((), (), s32[]{:S(2)}) async-start(), calls=%async_computation.20 | async-start | bytes 4456448 | tf_op jit(solution)/shard_map/reduce_scatter | solution.py:206
  913.5 320.2 %reduce-scatter.13.cloned.1.call-start = ((), (), s32[]{:S(2)}) async-start(), calls=%async_computation.19 | async-start | bytes 1114112 | tf_op jit(solution)/shard_map/reduce_scatter | solution.py:203
  918.8 384.2 %reduce-scatter.11.cloned.1.call-start = ((), (), s32[]{:S(2)}) async-start(), calls=%async_computation.18 | async-start | bytes 3342336 | tf_op jit(solution)/shard_map/reduce_scatter | solution.py:200
  928.0 98.3 %copy-start.38 = (f32[2,1024]{1,0:T(2,128)S(1)}, f32[2,1024]{1,0:T(2,128)}, u32[]{:S(2)}) copy-start(f32[2,1024]{1,0:T(2,128)} %get-tuple-element.192) | copy-start | bytes 24580
  928.0 439.4 %reduce-scatter.7.cloned.1.call-start = ((), (), s32[]{:S(2)}) async-start(), calls=%async_computation.16 | async-start | bytes 2228224 | tf_op jit(solution)/shard_map/reduce_scatter | solution.py:197
  1064.3 442.2 %reduce-scatter.9.cloned.1.call-start = ((), (), s32[]{:S(2)}) async-start(), calls=%async_computation.17 | async-start | bytes 13369344 | tf_op jit(solution)/shard_map/reduce_scatter | solution.py:186
  (60 other events, 549.4 us)
Sparse Core Ops, SparseCore 0:
  10.8 42.0 all-gather.10
  55.6 99.1 all-gather.12
  157.6 45.1 all-gather.16
  204.7 38.8 all-gather.14
  246.2 37.4 all-gather.18
  321.1 77.9 all-reduce.8
  401.8 51.1 all-gather.22
  455.1 38.9 all-gather.20
  496.8 51.1 all-gather.24
  549.4 38.9 all-gather.26
  616.1 77.9 all-reduce.10
  716.7 40.8 all-gather.28
  885.8 137.9 all-reduce.12
  1027.5 70.3 reduce-scatter.16
  1102.1 71.7 reduce-scatter.14
  1177.3 56.3 reduce-scatter.12
  1237.8 65.1 reduce-scatter.10
  1307.0 60.3 reduce-scatter.6
  1371.5 134.8 reduce-scatter.8
where the time goes:
time: 1530 us; the launch traced here: 1520 us
  waiting for transfers between devices  1020 us (67%)
  matrix products  245 us (16%)
  other arithmetic  138 us (9%)
  local copies, waits for them, and re-layouts  62.2 us (4%)
  blocking collectives  32.6 us (2%)
  between operations  15.5 us (1%)
    unnamed x22, waiting for transfers between devices  247 us
    all_gather x4, waiting for transfers between devices, spread(): return lax.all_gather(values, 'tensor', axis=1, tiled=True)  144 us
    reduce_scatter x1, waiting for transfers between devices, on_device(): lax.psum_scatter(ada_terms.reshape(model_width, 6, model_width).astype(jn...  137 us
    all_gather x1, waiting for transfers between devices, on_device(): lax.all_gather(w_ada.astype(jnp.bfloat16), 'dp', axis=0, tiled=True)  99.7 us
    reduce_scatter x1, waiting for transfers between devices, on_device(): lax.psum_scatter(grad_fc1.astype(jnp.bfloat16), 'dp', scatter_dimension=0...  71.2 us
    reduce_scatter x1, waiting for transfers between devices, on_device(): lax.psum_scatter(grad_qkv.astype(jnp.bfloat16), 'dp', scatter_dimension=0...  67.8 us
    reduce_scatter x1, waiting for transfers between devices, on_device(): lax.psum_scatter(grad_proj.astype(jnp.bfloat16), 'dp', scatter_dimension=...  58 us
    reduce_scatter x1, waiting for transfers between devices, on_device(): lax.psum_scatter(table_terms.astype(jnp.bfloat16), 'dp', scatter_dimensio...  56.3 us
  transfers between devices with their start and end apart: 19, of which 17 were waited for; matrix products, arithmetic and copies ran while one was open for 16% of the time, Pallas kernels for 0%

commit v1 on v0

--- a/solution.py
+++ b/solution.py
@@ -3,6 +3,8 @@
 import jax
 import jax.numpy as jnp
 from jax import lax
+from jax.experimental import pallas as pl
+from jax.experimental.pallas import tpu as pltpu
 from jax.sharding import PartitionSpec as P
 
 EPSILON = 1e-06
@@ -75,7 +77,7 @@
     return (d_queries, d_keys, d_values)
 
 
-def on_device(
+def on_device_general(
     inputs, labels, scale_ids, cotangent, table, w_ada, w_qkv, head_scale, w_proj, w_fc1, w_fc2
 ):
     images, local_len, model_width = inputs.shape
@@ -224,6 +226,544 @@
     )
 
 
+BF16 = jnp.bfloat16
+F32 = jnp.float32
+ZS, XS, CS, TS = 4, 2, 2, 2
+BOTH = ("dp", "tensor")
+NN = (((1,), (0,)), ((), ()))
+NT = (((1,), (1,)), ((), ()))
+TN = (((0,), (0,)), ((), ()))
+HIDDEN = -1e30
+VMEM_LIMIT = 60 * 1024 * 1024
+
+
+def perm_of(step):
+    pairs = []
+    for z in range(ZS):
+        for x in range(XS):
+            for c in range(CS):
+                for t in range(TS):
+                    nz, nx, nc, nt = step(z, x, c, t)
+                    source = ((z * XS + x) * CS + c) * TS + t
+                    target = ((nz * XS + nx) * CS + nc) * TS + nt
+                    pairs.append((source, target))
+    return pairs
+
+
+def send(values, step):
+    return lax.ppermute(values, BOTH, perm_of(step))
+
+
+def to_core(z, x, c, t):
+    return (z, x, 1 - c, t)
+
+
+def to_x(z, x, c, t):
+    return (z, 1 - x, c, t)
+
+
+def to_t(z, x, c, t):
+    return (z, x, c, 1 - t)
+
+
+def to_z(k):
+    return lambda z, x, c, t: ((z + k) % ZS, x, c, t)
+
+
+def to_near(z, x, c, t):
+    return (z, 1 - x, c, t) if c == 0 else (z, x, c, 1 - t)
+
+
+def to_far(z, x, c, t):
+    return (z, x, c, 1 - t) if c == 0 else (z, 1 - x, c, t)
+
+
+def pick(values, index, axis=0):
+    return lax.dynamic_index_in_dim(values, index, axis, keepdims=False)
+
+
+def place():
+    dp = lax.axis_index("dp")
+    t = lax.axis_index("tensor")
+    return dp // (XS * CS), (dp // CS) % XS, dp % CS, t
+
+
+def matmul(left, right, dims):
+    return lax.dot_general(left, right, dims, preferred_element_type=F32)
+
+
+def gather_near_first(rows):
+    rows = jnp.concatenate([rows, send(rows, to_core)])
+    rows = jnp.concatenate([rows, send(rows, to_x)])
+    return jnp.concatenate([rows] + [send(rows, to_z(k)) for k in range(1, ZS)])
+
+
+def reduce_near_first(terms):
+    terms = terms[:, :, 0] + send(terms[:, :, 1], to_core)
+    terms = terms[:, 0] + send(terms[:, 1], to_x)
+    total = terms[0]
+    for k in range(1, ZS):
+        total = total + send(terms[ZS - k], to_z(k))
+    return total
+
+
+def gather_pieces(keep, give):
+    two = jnp.stack([keep, send(give, to_core)])
+    four = jnp.stack([two] + [send(two, to_z(k)) for k in range(1, ZS)])
+    near = send(four, to_near)
+    mine = [four, near, send(four, to_far), send(near, to_far)]
+    return mine + [send(piece, to_core) for piece in mine]
+
+
+def assemble_kernel(parts, where_ref, *refs):
+    pieces, outs, sem = refs[:8], refs[8:-1], refs[-1]
+    z, x, c, t = where_ref[0], where_ref[1], where_ref[2], where_ref[3]
+    for number, piece in enumerate(pieces):
+        owner = c if number < 4 else 1 - c
+        slot = number % 4
+        if slot == 0:
+            dx, dt = 0, 0
+        elif slot == 1:
+            dx, dt = 1 - owner, owner
+        elif slot == 2:
+            dx, dt = owner, 1 - owner
+        else:
+            dx, dt = 1, 1
+        sx, st = x ^ dx, t ^ dt
+        for dz in range(ZS):
+            for dc in range(CS):
+                sz = (z + ZS - dz) % ZS
+                sc = owner ^ dc
+                row = pl.multiple_of(((sz * XS + sx) * CS + sc) * 64, 64)
+                for which, base, stride_t, stride_h, start, width in parts:
+                    column = pl.multiple_of(base + st * stride_t + owner * stride_h, 128)
+                    pltpu.make_async_copy(
+                        piece.at[dz, dc, :, pl.ds(start, width)],
+                        outs[which].at[pl.ds(row, 64), pl.ds(column, width)],
+                        sem.at[which],
+                    ).start()
+    for which, out in enumerate(outs):
+        pltpu.make_async_copy(out, out, sem.at[which]).wait()
+
+
+def assemble(pieces, position, parts, widths):
+    rows = ZS * XS * CS * 64
+    outs = [jax.ShapeDtypeStruct((rows, width), BF16) for width in widths]
+    return pl.pallas_call(
+        functools.partial(assemble_kernel, parts),
+        out_shape=outs,
+        in_specs=[pl.BlockSpec(memory_space=pltpu.SMEM)]
+        + [pl.BlockSpec(memory_space=pl.ANY)] * 8,
+        out_specs=[pl.BlockSpec(memory_space=pltpu.VMEM)] * len(outs),
+        scratch_shapes=[pltpu.SemaphoreType.DMA((len(outs),))],
+        compiler_params=pltpu.CompilerParams(vmem_limit_bytes=VMEM_LIMIT),
+    )(position, *pieces)
+
+
+def product_kernel(*refs):
+    left = jnp.concatenate([ref[...] for ref in refs[1 : 1 + ZS]], axis=1)
+    right = refs[1 + ZS][...]
+    out = refs[-1]
+    total = matmul(left, right.reshape(right.shape[-2:]), TN)
+    if len(refs) == ZS + 4:
+        total = total + refs[2 + ZS][...].astype(F32)
+    out[...] = total.astype(out.dtype)
+
+
+def product(rows, columns, quarter, choice, added=None):
+    tokens = rows.shape[0]
+    span = CS * 64
+    if columns.ndim == 3:
+        parts = columns.shape[0]
+        right = pl.BlockSpec((1, tokens, quarter), lambda p, s: (p, 0, s[1]))
+    else:
+        parts = 1
+        right = pl.BlockSpec((tokens, quarter), lambda p, s: (0, s[1]))
+    lefts = [
+        pl.BlockSpec((tokens, span), functools.partial(lambda n, p, s: (0, n * XS + s[0]), n))
+        for n in range(ZS)
+    ]
+    block = pl.BlockSpec((ZS * span, quarter), lambda p, s: (0, p))
+    extra = [] if added is None else [added]
+    return pl.pallas_call(
+        product_kernel,
+        out_shape=jax.ShapeDtypeStruct((ZS * span, parts * quarter), BF16),
+        grid_spec=pltpu.PrefetchScalarGridSpec(
+            num_scalar_prefetch=1,
+            grid=(parts,),
+            in_specs=lefts + [right] + [block] * len(extra),
+            out_specs=block,
+        ),
+        cost_estimate=pl.CostEstimate(
+            flops=2 * tokens * ZS * span * parts * quarter,
+            bytes_accessed=2 * (tokens + ZS * span) * (ZS * span + parts * quarter),
+            transcendentals=0,
+        ),
+        compiler_params=pltpu.CompilerParams(vmem_limit_bytes=VMEM_LIMIT),
+    )(choice, *([rows] * ZS), columns, *extra)
+
+
+def scatter_sum(rows, columns, quarter, z, x, c, t):
+    def block(dx, dt, dh, added=None):
+        choice = jnp.stack([x ^ dx, (t ^ dt) * 2 + (c ^ dh)]).astype(jnp.int32)
+        return product(rows, columns, quarter, choice, added)
+
+    def on_chip(dx, dt, other_dx, other_dt):
+        return block(dx, dt, 0, send(block(other_dx, other_dt, 1), to_core))
+
+    flag = 1 - c
+    far_both = send(on_chip(1, 1, 1, 1), to_far)
+    far_one = send(on_chip(c, flag, flag, c), to_far)
+    near = on_chip(flag, c, c, flag).astype(F32) + far_both.astype(F32)
+    near = send(near.astype(BF16), to_near)
+    whole = on_chip(0, 0, 0, 0).astype(F32) + far_one.astype(F32) + near.astype(F32)
+    whole = whole.astype(BF16).reshape(ZS, CS, 64, whole.shape[-1])
+    total = pick(whole, z).astype(F32)
+    for k in range(1, ZS):
+        total = total + send(pick(whole, (z + k) % ZS), to_z(k)).astype(F32)
+    return pick(total, c), send(pick(total, 1 - c).astype(BF16), to_core).astype(F32)
+
+
+def in_order(own, other, bit):
+    return jnp.where(bit == 0, own, other), jnp.where(bit == 0, other, own)
+
+
+def whole_image(values, t):
+    own = pick(values, t)
+    other = send(pick(values, 1 - t).astype(BF16), to_t).astype(F32)
+    return jnp.concatenate(in_order(own, other, t), axis=0)
+
+
+def split_image(values, t):
+    half = values.shape[0] // 2
+    own = lax.dynamic_slice_in_dim(values, t * half, half, axis=0)
+    give = lax.dynamic_slice_in_dim(values, (1 - t) * half, half, axis=0)
+    other = send(give.astype(BF16), to_t).astype(F32)
+    return jnp.stack(in_order(own, other, t))
+
+
+def unit_of(values, mask):
+    squares = jnp.where(mask, values * values, 0.0)
+    inverse = lax.rsqrt(jnp.sum(squares, axis=-1, keepdims=True) + EPSILON)
+    return jnp.where(mask, values * inverse, 0.0), inverse
+
+
+def head_masks(shape, head_dim):
+    lane = lax.broadcasted_iota(jnp.int32, shape, 1)
+    return [(lane >= n * head_dim) & (lane < (n + 1) * head_dim) for n in range(2)]
+
+
+def attend_kernel(head_dim, scale_ref, row_ref, column_ref, q_ref, k_ref, v_ref, out_ref, bias_ref):
+    pair = pl.program_id(0)
+
+    @pl.when(pair == 0)
+    def _():
+        bias_ref[...] = jnp.where(row_ref[...] <= column_ref[...], 0.0, HIDDEN)
+
+    q, k = q_ref[...].astype(F32), k_ref[...].astype(F32)
+    v = v_ref[...]
+    values = jnp.concatenate([v, jnp.ones_like(v)], axis=1)
+    masks = head_masks(q.shape, head_dim)
+    k_hat = (unit_of(k, masks[0])[0] + unit_of(k, masks[1])[0]).astype(BF16)
+    result = None
+    for n in range(2):
+        scale = scale_ref[2 * pair + n]
+        q_hat = (unit_of(q, masks[n])[0] * scale).astype(BF16)
+        scores = matmul(q_hat, k_hat, NT) + (bias_ref[...] - jnp.abs(scale))
+        weights = jnp.exp(scores).astype(BF16)
+        mixed = matmul(weights, values, NN)
+        mixed = mixed[:, : 2 * head_dim] / mixed[:, 2 * head_dim :]
+        result = mixed if result is None else jnp.where(masks[n], mixed, result)
+    out_ref[...] = result.astype(out_ref.dtype)
+
+
+def attend_whole(raw, scale_row, all_scale):
+    tokens, width = raw.shape[0], raw.shape[1] // 3
+    head_dim = width // all_scale.shape[0]
+    lanes = 2 * head_dim
+    pairs = width // lanes
+
+    def block(part):
+        return pl.BlockSpec((tokens, lanes), lambda n: (0, part * pairs + n))
+
+    return pl.pallas_call(
+        functools.partial(attend_kernel, head_dim),
+        out_shape=jax.ShapeDtypeStruct((tokens, width), BF16),
+        grid=(pairs,),
+        in_specs=[
+            pl.BlockSpec(memory_space=pltpu.SMEM),
+            pl.BlockSpec((1, tokens), lambda n: (0, 0)),
+            pl.BlockSpec((tokens, 1), lambda n: (0, 0)),
+            block(0),
+            block(1),
+            block(2),
+        ],
+        out_specs=pl.BlockSpec((tokens, lanes), lambda n: (0, n)),
+        scratch_shapes=[pltpu.VMEM((tokens, tokens), F32)],
+        cost_estimate=pl.CostEstimate(
+            flops=4 * tokens * tokens * width,
+            bytes_accessed=8 * tokens * width,
+            transcendentals=tokens * tokens * all_scale.shape[0],
+        ),
+        compiler_params=pltpu.CompilerParams(vmem_limit_bytes=VMEM_LIMIT),
+    )(all_scale, scale_row[None, :], scale_row[:, None], raw, raw, raw)
+
+
+def attend_back_kernel(
+    head_dim,
+    scale_ref,
+    row_ref,
+    column_ref,
+    q_ref,
+    k_ref,
+    v_ref,
+    mixed_ref,
+    d_mixed_ref,
+    out_ref,
+    term_ref,
+    bias_ref,
+):
+    pair = pl.program_id(0)
+
+    @pl.when(pair == 0)
+    def _():
+        bias_ref[...] = jnp.where(column_ref[...] <= row_ref[...], 0.0, HIDDEN)
+
+    q, k = q_ref[...].astype(F32), k_ref[...].astype(F32)
+    v, d_mixed = v_ref[...], d_mixed_ref[...]
+    masks = head_masks(q.shape, head_dim)
+    k_units = [unit_of(k, mask) for mask in masks]
+    k_hat = (k_units[0][0] + k_units[1][0]).astype(BF16)
+    products = d_mixed.astype(F32) * mixed_ref[...].astype(F32)
+    d_q_all = d_k_all = d_v_all = None
+    for n in range(2):
+        mask = masks[n]
+        scale = scale_ref[2 * pair + n]
+        q_unit, q_inverse = unit_of(q, mask)
+        q_hat = (q_unit * scale).astype(BF16)
+        d_out = jnp.where(mask, d_mixed, jnp.zeros_like(d_mixed))
+        offset = jnp.sum(jnp.where(mask, products, 0.0), axis=-1, keepdims=True)
+        offset = jnp.transpose(jnp.broadcast_to(offset, products.shape))[:1]
+        scores = matmul(k_hat, q_hat, NT) + (bias_ref[...] - jnp.abs(scale))
+        weights = jnp.exp(scores)
+        weights = weights * (1.0 / jnp.sum(weights, axis=0, keepdims=True))
+        d_weights = matmul(v, d_out, NT)
+        d_scores = (weights * (d_weights - offset)).astype(BF16)
+        d_v = matmul(weights.astype(BF16), d_out, NN)
+        d_k = matmul(d_scores, q_hat, NN)
+        d_q = jnp.where(mask, matmul(d_scores, k_hat, TN), 0.0)
+        d_k = jnp.where(mask, d_k, 0.0)
+        k_unit, k_inverse = k_units[n]
+        term = d_q * q_unit
+        term_n = jnp.sum(term, axis=0, keepdims=True)
+        d_q = q_inverse * scale * (d_q - q_unit * jnp.sum(term, axis=-1, keepdims=True))
+        d_k = k_inverse * (d_k - k_unit * jnp.sum(d_k * k_unit, axis=-1, keepdims=True))
+        if n == 0:
+            d_q_all, d_k_all, d_v_all, term_all = d_q, d_k, d_v, term_n
+        else:
+            d_q_all, d_k_all = d_q_all + d_q, d_k_all + d_k
+            d_v_all, term_all = d_v_all + d_v, term_all + term_n
+    out_ref[0] = d_q_all.astype(out_ref.dtype)
+    out_ref[1] = d_k_all.astype(out_ref.dtype)
+    out_ref[2] = d_v_all.astype(out_ref.dtype)
+    term_ref[...] = jnp.broadcast_to(term_all, term_ref.shape)
+
+
+def attend_back_whole(raw, mixed, d_mixed, scale_row, all_scale):
+    tokens, width = mixed.shape
+    heads = all_scale.shape[0]
+    head_dim = width // heads
+    lanes = 2 * head_dim
+    pairs = width // lanes
+
+    def block(part):
+        return pl.BlockSpec((tokens, lanes), lambda n: (0, part * pairs + n))
+
+    d_raw, terms = pl.pallas_call(
+        functools.partial(attend_back_kernel, head_dim),
+        out_shape=[
+            jax.ShapeDtypeStruct((3, tokens, width), BF16),
+            jax.ShapeDtypeStruct((8, width), F32),
+        ],
+        grid=(pairs,),
+        in_specs=[
+            pl.BlockSpec(memory_space=pltpu.SMEM),
+            pl.BlockSpec((1, tokens), lambda n: (0, 0)),
+            pl.BlockSpec((tokens, 1), lambda n: (0, 0)),
+            block(0),
+            block(1),
+            block(2),
+            block(0),
+            block(0),
+        ],
+        out_specs=[
+            pl.BlockSpec((3, tokens, lanes), lambda n: (0, 0, n)),
+            pl.BlockSpec((8, lanes), lambda n: (0, n)),
+        ],
+        scratch_shapes=[pltpu.VMEM((tokens, tokens), F32)],
+        cost_estimate=pl.CostEstimate(
+            flops=10 * tokens * tokens * width,
+            bytes_accessed=16 * tokens * width,
+            transcendentals=tokens * tokens * heads,
+        ),
+        compiler_params=pltpu.CompilerParams(vmem_limit_bytes=VMEM_LIMIT),
+    )(all_scale, scale_row[None, :], scale_row[:, None], raw, raw, raw, mixed, d_mixed)
+    return d_raw, jnp.sum(terms[0].reshape(heads, head_dim), axis=1)
+
+
+def halves(values, c, half):
+    keep = lax.dynamic_slice_in_dim(values, c * half, half, axis=1)
+    give = lax.dynamic_slice_in_dim(values, (1 - c) * half, half, axis=1)
+    return keep, give
+
+
+def on_device_whole(
+    inputs, labels, scale_ids, cotangent, table, w_ada, w_qkv, head_scale, w_proj, w_fc1, w_fc2
+):
+    width = inputs.shape[2]
+    classes, rows = table.shape
+    heads = TS * head_scale.shape[0]
+    quarter = w_qkv.shape[2] // 2
+    hidden_quarter = w_fc1.shape[1] // 2
+    z, x, c, t = place()
+    position = jnp.stack([z, x, c, t]).astype(jnp.int32)
+
+    qkv_parts = [halves(w_qkv[:, n].astype(BF16), c, quarter) for n in range(3)]
+    proj_parts = halves(w_proj.astype(BF16).T, c, quarter)
+    fc1_parts = halves(w_fc1.astype(BF16), c, hidden_quarter)
+    fc2_parts = halves(w_fc2.astype(BF16).T, c, hidden_quarter)
+    pieces_qkv = gather_pieces(
+        *[jnp.concatenate([part[n] for part in qkv_parts], axis=1) for n in range(2)]
+    )
+    pieces_mid = gather_pieces(
+        *[jnp.concatenate([proj_parts[n], fc1_parts[n]], axis=1) for n in range(2)]
+    )
+    pieces_fc2 = gather_pieces(*fc2_parts)
+    (qkv_low,) = assemble(
+        pieces_qkv,
+        position,
+        [(0, n * width, 2 * quarter, quarter, n * quarter, quarter) for n in range(3)],
+        [3 * width],
+    )
+    proj_low, fc1_low = assemble(
+        pieces_mid,
+        position,
+        [
+            (0, 0, 2 * quarter, quarter, 0, quarter),
+            (1, 0, 2 * hidden_quarter, hidden_quarter, quarter, hidden_quarter),
+        ],
+        [width, 4 * hidden_quarter],
+    )
+    (fc2_low,) = assemble(
+        pieces_fc2,
+        position,
+        [(0, 0, 2 * hidden_quarter, hidden_quarter, 0, hidden_quarter)],
+        [4 * hidden_quarter],
+    )
+
+    label_pair = jnp.stack(in_order(labels[0], labels[1], t)).astype(F32)
+    label_tile = jnp.broadcast_to(label_pair[:, None], (2, 128))
+    all_labels = gather_near_first(label_tile)[:, 0].astype(jnp.int32)
+    one_hot = (all_labels[:, None] == jnp.arange(classes)[None, :]).astype(BF16)
+    condition = matmul(one_hot, table.astype(BF16), NN)
+    silu_low = jax.nn.silu(condition).astype(BF16)
+    ada_low = w_ada.astype(BF16).reshape(rows, 6 * width)
+    silu_own = silu_low.reshape(-1, TS, rows)[:, 0]
+    partial = matmul(silu_own, ada_low, NN).reshape(ZS, XS, CS, 6 * width)
+    modulation = reduce_near_first(partial).reshape(6, 1, width)
+    gain_attn, gain_mlp, scale_attn, scale_mlp, shift_attn, shift_mlp = modulation
+
+    tokens_in = whole_image(inputs, t)
+    upstream = whole_image(cotangent, t)
+    scale_row = pick(scale_ids, t)
+    other_scale = send(jnp.broadcast_to(head_scale[None, :], (8, head_scale.shape[0])), to_t)[0]
+    all_scale = jnp.concatenate(in_order(head_scale, other_scale, t))
+
+    normed_one, inverse_one = layer_norm(tokens_in)
+    hidden_one = (normed_one * (1.0 + scale_attn) + shift_attn).astype(BF16)
+    raw = matmul(hidden_one, qkv_low, NN).astype(BF16)
+    mixed = attend_whole(raw, scale_row, all_scale)
+    attended = matmul(mixed, proj_low, NT)
+    middle = tokens_in + gain_attn * attended
+    normed_two, inverse_two = layer_norm(middle)
+    hidden_two = (normed_two * (1.0 + scale_mlp) + shift_mlp).astype(BF16)
+    before = matmul(hidden_two, fc1_low, NN)
+    gelu_fn = functools.partial(jax.nn.gelu, approximate=True)
+    active_f, gelu_pull = jax.vjp(gelu_fn, before)
+    active = active_f.astype(BF16)
+    slope = gelu_pull(jnp.ones_like(before))[0].astype(BF16)
+    branch = matmul(active, fc2_low, NT)
+    output = split_image(middle + gain_mlp * branch, t)
+
+    d_gain_mlp = jnp.sum(upstream * branch, axis=0)
+    d_branch = (gain_mlp * upstream).astype(BF16)
+    grad_fc2 = scatter_sum(d_branch, active, hidden_quarter, z, x, c, t)
+    d_before = (matmul(d_branch, fc2_low, NN) * slope.astype(F32)).astype(BF16)
+    grad_fc1 = scatter_sum(hidden_two, d_before, hidden_quarter, z, x, c, t)
+    d_hidden_two = matmul(d_before, fc1_low, NT)
+    d_scale_mlp = jnp.sum(d_hidden_two * normed_two, axis=0)
+    d_shift_mlp = jnp.sum(d_hidden_two, axis=0)
+    d_middle = upstream + norm_back(d_hidden_two * (1.0 + scale_mlp), normed_two, inverse_two)
+    d_gain_attn = jnp.sum(d_middle * attended, axis=0)
+    d_attended = (gain_attn * d_middle).astype(BF16)
+    grad_proj = scatter_sum(d_attended, mixed, quarter, z, x, c, t)
+    d_mixed = matmul(d_attended, proj_low, NN).astype(BF16)
+    d_raw, scale_terms = attend_back_whole(raw, mixed, d_mixed, scale_row, all_scale)
+    grad_qkv = scatter_sum(hidden_one, d_raw, quarter, z, x, c, t)
+    d_hidden_one = sum(
+        matmul(d_raw[n], qkv_low[:, n * width : (n + 1) * width], NT) for n in range(3)
+    )
+    d_scale_attn = jnp.sum(d_hidden_one * normed_one, axis=0)
+    d_shift_attn = jnp.sum(d_hidden_one, axis=0)
+    d_inputs = d_middle + norm_back(d_hidden_one * (1.0 + scale_attn), normed_one, inverse_one)
+    d_inputs = split_image(d_inputs, t)
+
+    d_modulation = jnp.concatenate(
+        [d_gain_attn, d_gain_mlp, d_scale_attn, d_scale_mlp, d_shift_attn, d_shift_mlp]
+    )
+    scale_high = lax.reduce_precision(scale_terms, 8, 7)
+    row = jnp.concatenate(
+        [d_modulation, scale_high, scale_terms - scale_high, jnp.zeros((128 - 2 * heads,), F32)]
+    ).astype(BF16)[None, :]
+    everything = gather_near_first(jnp.concatenate([row, send(row, to_t)]))
+    d_mod_all = everything[:, : 6 * width]
+    scale_sum = jnp.sum(everything[:, 6 * width : 6 * width + 2 * heads].astype(F32), axis=0)
+    scale_sum = (scale_sum[:heads] + scale_sum[heads:]).reshape(TS, heads // TS)
+    grad_scale = pick(scale_sum, t)
+    grad_ada = matmul(silu_low, d_mod_all, TN).reshape(rows, 6, width)
+    d_silu = matmul(d_mod_all, ada_low, NT)
+    _, silu_pull = jax.vjp(jax.nn.silu, condition)
+    d_condition = silu_pull(d_silu)[0]
+    grad_table = jnp.dot(one_hot.astype(F32).T, d_condition, precision=HIGHEST)
+
+    own_qkv, other_qkv = grad_qkv
+    grad_qkv = jnp.stack(
+        [
+            jnp.concatenate(
+                in_order(
+                    own_qkv[:, n * quarter : (n + 1) * quarter],
+                    other_qkv[:, n * quarter : (n + 1) * quarter],
+                    c,
+                ),
+                axis=1,
+            )
+            for n in range(3)
+        ],
+        axis=1,
+    )
+    return (
+        output,
+        d_inputs,
+        grad_table,
+        grad_ada,
+        grad_qkv,
+        grad_scale,
+        jnp.concatenate(in_order(*grad_proj, c), axis=1).T,
+        jnp.concatenate(in_order(*grad_fc1, c), axis=1),
+        jnp.concatenate(in_order(*grad_fc2, c), axis=1).T,
+    )
+
+
 def solution(mesh):
     placed = (
         P("dp", "tensor", None),
@@ -238,6 +778,12 @@
         P("dp", "tensor"),
         P("tensor", "dp"),
     )
+    fitting = mesh.shape["dp"] == ZS * XS * CS and mesh.shape["tensor"] == TS
+
+    def on_device(inputs, *others):
+        fits = fitting and inputs.shape[0] == TS
+        return (on_device_whole if fits else on_device_general)(inputs, *others)
+
     return jax.shard_map(
         on_device,
         mesh=mesh,

time: 1530 us -> 712 us (0.47)
  waiting for transfers between devices: 1020 us -> 175 us
  Pallas kernels: 0 us -> 208 us
  matrix products: 245 us -> 95.9 us
  starting transfers between devices: 1.22 us -> 104 us
  other arithmetic: 138 us -> 62.5 us
  blocking collectives: 32.6 us -> 0 us
    reduce_scatter x6 -> x0, waiting for transfers between devices: 391 us -> none  [the longest x1 137 us: on_device(): lax.psum_scatter(ada_terms.reshape(model_width, 6, model_width).astype(jn...]
    all_gather x10 -> x0, waiting for transfers between devices: 383 us -> none  [the longest x4 144 us: spread(): return lax.all_gather(values, 'tensor', axis=1, tiled=True)]
    unnamed x22 -> x0, waiting for transfers between devices: 247 us -> none
    pallas_call x0 -> x37, Pallas kernels: none -> 208 us  [the longest x32 136 us: product(): pl.pallas_call(product_kernel, out_shape=jax.ShapeDtypeStruct((ZS * span,...]
    ppermute x0 -> x98, waiting for transfers between devices: none -> 175 us  [send(): return lax.ppermute(values, BOTH, perm_of(step))]
    dot_general x31 -> x15, matrix products: 245 us -> 95.9 us  [the longest x14 94.9 us: matmul(): return lax.dot_general(left, right, dims, preferred_element_type=F32)]
    ppermute x0 -> x98, starting transfers between devices: none -> 104 us  [send(): return lax.ppermute(values, BOTH, perm_of(step))]
    reduce_sum x10 -> x2, other arithmetic: 61.2 us -> 0.14 us  [the longest x1 0.12 us: attend_back_whole(): return (d_raw, jnp.sum(terms[0].reshape(heads, head_dim), axis=1))]
  transfers between devices with their start and end apart: 19 -> 98, of which waited for: 17 -> 26; matrix products, arithmetic and copies ran while one was open for 16% -> 18% of each run, Pallas kernels for 0% -> 16%
where the time goes in v1:
time: 712 us; the launch traced here: 701 us
  Pallas kernels  208 us (29%)
  waiting for transfers between devices  175 us (25%)
  starting transfers between devices  104 us (15%)
  matrix products  95.9 us (13%)
  other arithmetic  62.5 us (9%)
  local copies, waits for them, and re-layouts  50.1 us (7%)
    ppermute x98, waiting for transfers between devices, send(): return lax.ppermute(values, BOTH, perm_of(step))  175 us
    pallas_call x32, Pallas kernels, product(): pl.pallas_call(product_kernel, out_shape=jax.ShapeDtypeStruct((ZS * span,...  136 us
    ppermute x98, starting transfers between devices, send(): return lax.ppermute(values, BOTH, perm_of(step))  104 us
    dot_general x14, matrix products, matmul(): return lax.dot_general(left, right, dims, preferred_element_type=F32)  94.9 us
    pallas_call x1, Pallas kernels, attend_back_whole(): pl.pallas_call(functools.partial(attend_back_kernel, head_dim), out_shape...  34 us
    pallas_call x3, Pallas kernels, assemble(): pl.pallas_call(functools.partial(assemble_kernel, parts), out_shape=outs,...  22.5 us
    unnamed x165, local copies, waits for them, and re-layouts  16.1 us
    pallas_call x1, Pallas kernels, attend_whole(): pl.pallas_call(functools.partial(attend_kernel, head_dim), out_shape=jax....  14.8 us
  transfers between devices with their start and end apart: 98, of which 26 were waited for; matrix products, arithmetic and copies ran while one was open for 18% of the time, Pallas kernels for 16%

profile of v1, /device:TPU:9, one launch (start us, length us, event | category | flops | bytes accessed | tf_op | source)
XLA Modules:
  0.0 700.8 jit_solution(16072876291231938909)
XLA Ops:
  65.1 11.2 %collective-permute-done.13 = bf16[2,64,768]{2,1,0:T(8,128)(2,1)S(1)} collective-permute-done((bf16[2,64,768]{2,1,0:T(8,128)(2,1)S(1)}, bf16[2,64,768]{2,1,0:T(8,128)(2,1)S(1)}, u32[]{:S(2)}, u32[]{:S(2)}) %collective-permute-start.13) | collective-permute-done | bytes 196640 | tf_op jit(solution)/shard_map/ppermute | solution.py:254
  78.6 9.6 %collective-permute-done.10 = f32[6144]{0:T(1024)S(1)} collective-permute-done((f32[6144]{0:T(1024)S(1)}, f32[6144]{0:T(1024)S(1)}, u32[]{:S(2)}, u32[]{:S(2)}) %collective-permute-start.10) | collective-permute-done | bytes 24608 | tf_op jit(solution)/shard_map/ppermute | solution.py:254
  127.9 16.8 %collective-permute-done.46 = bf16[340,1024]{1,0:T(8,128)(2,1)} collective-permute-done((bf16[340,1024]{1,0:T(8,128)(2,1)}, bf16[340,1024]{1,0:T(8,128)(2,1)}, u32[]{:S(2)}, u32[]{:S(2)}) %collective-permute-start.46) | collective-permute-done | bytes 696352 | tf_op jit(solution)/shard_map/ppermute | solution.py:254
  150.7 16.6 %collective-permute-done.38.refs_1_ = bf16[4,2,64,1024]{3,2,1,0:T(8,128)(2,1)S(1)} collective-permute-done((bf16[4,2,64,1024]{3,2,1,0:T(8,128)(2,1)S(1)}, bf16[4,2,64,1024]{3,2,1,0:T(8,128)(2,1)S(1)}, u32[]{:S(2)}, u32[]{:S(2)}) %collective-permute-start.38) | collective-permute-done | bytes 1048608 | tf_op jit(solution)/shard_map/ppermute | solution.py:254
  171.6 23.8 %collective-permute-done.27.refs_1_ = bf16[4,2,64,1280]{3,2,1,0:T(8,128)(2,1)} collective-permute-done((bf16[4,2,64,1280]{3,2,1,0:T(8,128)(2,1)S(1)}, bf16[4,2,64,1280]{3,2,1,0:T(8,128)(2,1)}, u32[]{:S(2)}, u32[]{:S(2)}) %collective-permute-start.27) | collective-permute-done | bytes 1310752 | tf_op jit(solution)/shard_map/ppermute | solution.py:254
  197.3 7.8 %collective-permute-start.42 = (bf16[4,2,64,1024]{3,2,1,0:T(8,128)(2,1)S(1)}, bf16[4,2,64,1024]{3,2,1,0:T(8,128)(2,1)S(1)}, u32[]{:S(2)}, u32[]{:S(2)}) collective-permute-start(bf16[4,2,64,1024]{3,2,1,0:T(8,128)(2,1)S(1)} %collective-permute-done.38.refs_1_), channel_id=1, source_target_pairs={{0,2},{1,3},{2,0},{3,1},{4,6},{5,7},{6,4},{7,5},{8,10},{9,11},{10,... | collective-permute-start | bytes 3145736 | tf_op jit(solution)/shard_map/ppermute | solution.py:254
  209.5 14.1 %collective-permute-done.40.refs_3_ = bf16[4,2,64,1024]{3,2,1,0:T(8,128)(2,1)S(1)} collective-permute-done((bf16[4,2,64,1024]{3,2,1,0:T(8,128)(2,1)S(1)}, bf16[4,2,64,1024]{3,2,1,0:T(8,128)(2,1)S(1)}, u32[]{:S(2)}, u32[]{:S(2)}) %collective-permute-start.40) | collective-permute-done | bytes 1048608 | tf_op jit(solution)/shard_map/ppermute | solution.py:254
  223.6 6.7 collective-permute-start.30
  232.0 6.2 shard_map.178
  238.6 9.0 %convolution_convert_fusion.q_ref.k_ref.v_ref = bf16[680,3072]{1,0:T(8,128)(2,1)} fusion(bf16[680,1024]{1,0:T(8,128)(2,1)S(1)} %add_convert_fusion.1.refs_1_.refs_2_.refs_3_.refs_4_, bf16[1024,3072]{1,0:T(8,128)(2,1)} %shard_map.178), kind=kOutput, calls=%fused_computation.11 | convolution fusion | flops 4280279040 | bytes 11862016 | tf_op jit(solution)/shard_map/dot_general | solution.py:292
  247.6 14.8 %shard_map.179.mixed_ref.refs_5_ = bf16[680,1024]{1,0:T(8,128)(2,1)} custom-call(f32[16]{0:T(128)} %pad_maximum_fusion.19.scale_ref, s32[1,680]{1,0:T(1,128)} %constant_dynamic-slice_fusion.5.row_ref, s32[680,1]{1,0:T(8,128)} %copy.71.column_ref, bf16[680,3072]{1,0:T(8,128)(2,1)} %convolution_convert_fusion.q_ref.k_ref.v_ref, ...), custom_call_target="tpu_custom_call" | custom-call | flops 1893990400 | bytes 5570560 | tf_op jit(solution)/shard_map/pallas_call | solution.py:489
  262.4 7.4 %shard_map.181 = bf16[1024,4096]{1,0:T(8,128)(2,1)} custom-call(s32[4]{0:T(128)} %pad_add_fusion.where_ref, bf16[4,2,64,1024]{3,2,1,0:T(8,128)(2,1)} %copy-done.23, bf16[4,2,64,1024]{3,2,1,0:T(8,128)(2,1)} %copy-done.36, bf16[4,2,64,1024]{3,2,1,0:T(8,128)(2,1)} %collective-permute-done.39.refs_2_, bf16[4,2,64,1024]{3,2,1,0:T(8,128)(2,1)} %copy-done.39, ...), custom_call_target="tpu_custom_call" | custom-call | tf_op jit(solution)/shard_map/pallas_call | solution.py:352
  269.8 8.9 %shard_map.180 = (bf16[1024,1024]{1,0:T(8,128)(2,1)}, bf16[1024,4096]{1,0:T(8,128)(2,1)}) custom-call(s32[4]{0:T(128)} %pad_add_fusion.where_ref, bf16[4,2,64,1280]{3,2,1,0:T(8,128)(2,1)} %copy-done.20, bf16[4,2,64,1280]{3,2,1,0:T(8,128)(2,1)} %collective-permute-done.27.refs_1_, bf16[4,2,64,1280]{3,2,1,0:T(8,128)(2,1)} %collective-permute-done.28.refs_2_, ...), custom_call_target="tpu_custom_call" | custom-call | tf_op jit(solution)/shard_map/pallas_call | solution.py:352
  278.8 5.9 fusion.69
  285.6 10.6 %multiply_convert_fusion.1 = (bf16[680,4096]{1,0:T(8,128)(2,1)S(1)}, f32[680,4096]{1,0:T(8,128)}) fusion(bf16[680,1024]{1,0:T(8,128)(2,1)S(1)} %add_convert_fusion.refs_1_.refs_2_.refs_3_.refs_4_, bf16[1024,4096]{1,0:T(8,128)(2,1)S(1)} %copy-done.79), kind=kOutput, calls=%fused_computation.10 | convolution fusion | flops 5729320960 | bytes 26492928 | tf_op jit(solution)/shard_map/dot_general | solution.py:292
  296.2 17.2 %multiply_convert_fusion.refs_5_ = bf16[680,4096]{1,0:T(8,128)(2,1)S(1)} fusion(bf16[680,1024]{1,0:T(8,128)(2,1)S(1)} %multiply_convert_fusion.3.refs_1_.refs_2_.refs_3_.refs_4_, bf16[1024,4096]{1,0:T(8,128)(2,1)} %shard_map.181, f32[680,4096]{1,0:T(8,128)} %get-tuple-element.150), kind=kOutput, calls=%fused_computation.9 | convolution fusion | flops 5762744320 | bytes 26492928 | tf_op jit(solution)/shard_map/dot_general | solution.py:292
  313.4 12.4 %multiply_reduce_fusion = (bf16[1024]{0:T(1024)(128)(2,1)S(1)}, f32[680]{0:T(1024)S(1)}, f32[680]{0:T(1024)S(1)}, bf16[1024]{0:T(1024)(128)(2,1)S(1)}, f32[680,1024]{1,0:T(8,128)}) fusion(f32[680,1024]{1,0:T(8,128)S(1)} %get-tuple-element.73, f32[680]{0:T(1024)S(1)} %add_rsqrt_fusion, f32[680]{0:T(1024)S(1)} %broadcast_multiply_fusion.4, ...), kind=kOutput, calls=%fused_computation.16 | convolution fusion | flops 5710517248 | bytes 19548800 | tf_op jit(solution)/shard_map/dot_general | solution.py:292
  325.9 13.9 %multiply_reduce_fusion.3 = (bf16[1024]{0:T(1024)(128)(2,1)S(1)}, f32[680,1024]{1,0:T(8,128)}, bf16[1024]{0:T(1024)(128)(2,1)S(1)}, f32[680,1024]{1,0:T(8,128)}) fusion(f32[680,1024]{1,0:T(8,128)} %get-tuple-element.147, f32[680]{0:T(1024)S(1)} %broadcast_multiply_fusion.2, f32[680,1024]{1,0:T(8,128)S(1)} %get-tuple-element.73, ...), kind=kOutput, calls=%fused_computation.19 | convolution fusion | flops 5714696192 | bytes 30694016 | tf_op jit(solution)/shard_map/dot_general | solution.py:292
  345.0 34.0 %shard_map.182 = (bf16[3,680,1024]{2,1,0:T(8,128)(2,1)}, f32[8,1024]{1,0:T(8,128)}) custom-call(f32[16]{0:T(128)} %pad_maximum_fusion.19.scale_ref, s32[1,680]{1,0:T(1,128)} %constant_dynamic-slice_fusion.5.row_ref, s32[680,1]{1,0:T(8,128)} %copy.71.column_ref, bf16[680,3072]{1,0:T(8,128)(2,1)} %convolution_convert_fusion.q_ref.k_ref.v_ref, ...), custom_call_target="tpu_custom_call" | custom-call | flops 4734976000 | bytes 11141120 | tf_op jit(solution)/shard_map/pallas_call | solution.py:582
  444.2 7.9 %multiply_reduce_fusion.1 = (bf16[1024]{0:T(1024)(128)(2,1)S(1)}, f32[680]{0:T(1024)S(1)}, f32[680]{0:T(1024)S(1)}, bf16[1024]{0:T(1024)(128)(2,1)S(1)}, f32[680,1024]{1,0:T(8,128)}) fusion(f32[680]{0:T(1024)S(1)} %copy-done.68, f32[680]{0:T(1024)S(1)} %copy-done.63, f32[340,1024]{1,0:T(8,128)} %copy-done.12, f32[340,1024]{1,0:T(8,128)S(1)} %copy-done.11, ...), kind=kOutput, calls=%fused_computation.17 | convolution fusion | flops 1434415872 | bytes 14666368 | tf_op jit(solution)/shard_map/dot_general | solution.py:292
  623.6 8.1 %collective-permute-done.62 = bf16[2,64,768]{2,1,0:T(8,128)(2,1)S(1)} collective-permute-done((bf16[2,64,768]{2,1,0:T(8,128)(2,1)S(1)}, bf16[2,64,768]{2,1,0:T(8,128)(2,1)S(1)}, u32[]{:S(2)}, u32[]{:S(2)}) %collective-permute-start.62) | collective-permute-done | bytes 196640 | tf_op jit(solution)/shard_map/ppermute | solution.py:254
  638.8 9.0 %collective-permute-done.82 = bf16[512,1024]{1,0:T(8,128)(2,1)S(1)} collective-permute-done((bf16[512,1024]{1,0:T(8,128)(2,1)S(1)}, bf16[512,1024]{1,0:T(8,128)(2,1)S(1)}, u32[]{:S(2)}, u32[]{:S(2)}) %collective-permute-start.82) | collective-permute-done | bytes 1048608 | tf_op jit(solution)/shard_map/ppermute | solution.py:254
  668.8 16.9 %collective-permute-done.83 = bf16[2,64,1024]{2,1,0:T(8,128)(2,1)S(1)} collective-permute-done((bf16[2,64,1024]{2,1,0:T(8,128)(2,1)S(1)}, bf16[2,64,1024]{2,1,0:T(8,128)(2,1)S(1)}, u32[]{:S(2)}, u32[]{:S(2)}) %collective-permute-start.83) | collective-permute-done | bytes 262176 | tf_op jit(solution)/shard_map/ppermute | solution.py:254
  691.3 5.6 collective-permute-done.94
  (524 shorter events, 401.3 us)
Async XLA Ops:
  6.7 45.5 %collective-permute-start.11 = (f32[8,8]{1,0:T(8,128)}, f32[8,8]{1,0:T(8,128)}, u32[]{:S(2)}, u32[]{:S(2)}) collective-permute-start(f32[8,8]{1,0:T(8,128)} %broadcast_in_dim.9), channel_id=1, source_target_pairs={{0,1},{1,0},{2,3},{3,2},{4,5},{5,4},{6,7},{7,6},{8,9},{9,8},{10,11... | collective-permute-start | bytes 776 | tf_op jit(solution)/shard_map/ppermute | solution.py:254
  10.9 33.9 %collective-permute-start.12 = (bf16[64,768]{1,0:T(8,128)(2,1)}, bf16[64,768]{1,0:T(8,128)(2,1)}, u32[]{:S(2)}, u32[]{:S(2)}) collective-permute-start(bf16[64,768]{1,0:T(8,128)(2,1)} %pad_maximum_fusion.14), channel_id=1, source_target_pairs={{0,2},{1,3},{2,0},{3,1},{4,6},{5,7},{6,4},{7,5},{8,10},{9,11},{10,... | collective-permute-start | bytes 294920 | tf_op jit(solution)/shard_map/ppermute | solution.py:254
  52.3 45.8 %collective-permute-start.37 = (bf16[2,64,1024]{2,1,0:T(8,128)(2,1)}, bf16[2,64,1024]{2,1,0:T(8,128)(2,1)}, u32[]{:S(2)}, u32[]{:S(2)}) collective-permute-start(bf16[2,64,1024]{2,1,0:T(8,128)(2,1)} %get-tuple-element.109), channel_id=1, source_target_pairs={{0,24},{1,25},{2,26},{3,27},{4,28},{5,29},{6,30},{7,31},{8,0},{9,1... | collective-permute-start | bytes 786440 | tf_op jit(solution)/shard_map/ppermute | solution.py:254
  52.5 48.6 %collective-permute-start.36 = (bf16[2,64,1024]{2,1,0:T(8,128)(2,1)}, bf16[2,64,1024]{2,1,0:T(8,128)(2,1)}, u32[]{:S(2)}, u32[]{:S(2)}) collective-permute-start(bf16[2,64,1024]{2,1,0:T(8,128)(2,1)} %get-tuple-element.109), channel_id=1, source_target_pairs={{0,16},{1,17},{2,18},{3,19},{4,20},{5,21},{6,22},{7,23},{8,24},{9,... | collective-permute-start | bytes 786440 | tf_op jit(solution)/shard_map/ppermute | solution.py:254
  101.1 44.8 %collective-permute-start.16 = (bf16[4,2,64,768]{3,2,1,0:T(8,128)(2,1)}, bf16[4,2,64,768]{3,2,1,0:T(8,128)(2,1)}, u32[]{:S(2)}, u32[]{:S(2)}) collective-permute-start(bf16[4,2,64,768]{3,2,1,0:T(8,128)(2,1)} %pad_maximum_fusion.6.refs_0_), channel_id=1, source_target_pairs={{0,4},{1,5},{2,3},{3,2},{4,0},{5,1},{6,7},{7,6},{8,12},{9,13},{10,... | collective-permute-start | bytes 2359304 | tf_op jit(solution)/shard_map/ppermute | solution.py:254
  105.4 39.3 %collective-permute-start.46 = (bf16[340,1024]{1,0:T(8,128)(2,1)}, bf16[340,1024]{1,0:T(8,128)(2,1)}, u32[]{:S(2)}, u32[]{:S(2)}) collective-permute-start(bf16[340,1024]{1,0:T(8,128)(2,1)} %bitcast.225), channel_id=1, source_target_pairs={{0,1},{1,0},{2,3},{3,2},{4,5},{5,4},{6,7},{7,6},{8,9},{9,8},{10,11... | collective-permute-start | bytes 2088968 | tf_op jit(solution)/shard_map/ppermute | solution.py:254
  124.8 42.6 %collective-permute-start.38 = (bf16[4,2,64,1024]{3,2,1,0:T(8,128)(2,1)S(1)}, bf16[4,2,64,1024]{3,2,1,0:T(8,128)(2,1)S(1)}, u32[]{:S(2)}, u32[]{:S(2)}) collective-permute-start(bf16[4,2,64,1024]{3,2,1,0:T(8,128)(2,1)S(1)} %pad_maximum_fusion.5.refs_0_), channel_id=1, source_target_pairs={{0,4},{1,5},{2,3},{3,2},{4,0},{5,1},{6,7},{7,6},{8,12},{9,13},{10,... | collective-permute-start | bytes 3145736 | tf_op jit(solution)/shard_map/ppermute | solution.py:254
  147.4 48.1 %collective-permute-start.27 = (bf16[4,2,64,1280]{3,2,1,0:T(8,128)(2,1)S(1)}, bf16[4,2,64,1280]{3,2,1,0:T(8,128)(2,1)}, u32[]{:S(2)}, u32[]{:S(2)}) collective-permute-start(bf16[4,2,64,1280]{3,2,1,0:T(8,128)(2,1)S(1)} %pad_maximum_fusion.4.refs_0_), channel_id=1, source_target_pairs={{0,4},{1,5},{2,3},{3,2},{4,0},{5,1},{6,7},{7,6},{8,12},{9,13},{10,... | collective-permute-start | bytes 3932168 | tf_op jit(solution)/shard_map/ppermute | solution.py:254
  148.5 48.4 %collective-permute-start.28 = (bf16[4,2,64,1280]{3,2,1,0:T(8,128)(2,1)S(1)}, bf16[4,2,64,1280]{3,2,1,0:T(8,128)(2,1)}, u32[]{:S(2)}, u32[]{:S(2)}) collective-permute-start(bf16[4,2,64,1280]{3,2,1,0:T(8,128)(2,1)S(1)} %pad_maximum_fusion.4.refs_0_), channel_id=1, source_target_pairs={{0,1},{1,0},{2,6},{3,7},{4,5},{5,4},{6,2},{7,3},{8,9},{9,8},{10,14... | collective-permute-start | bytes 3932168 | tf_op jit(solution)/shard_map/ppermute | solution.py:254
  168.6 37.0 %collective-permute-start.20 = (bf16[4,2,64,768]{3,2,1,0:T(8,128)(2,1)}, bf16[4,2,64,768]{3,2,1,0:T(8,128)(2,1)S(1)}, u32[]{:S(2)}, u32[]{:S(2)}) collective-permute-start(bf16[4,2,64,768]{3,2,1,0:T(8,128)(2,1)} %collective-permute-done.16.refs_1_), channel_id=1, source_target_pairs={{0,2},{1,3},{2,0},{3,1},{4,6},{5,7},{6,4},{7,5},{8,10},{9,11},{10,... | collective-permute-start | bytes 2359304 | tf_op jit(solution)/shard_map/ppermute | solution.py:254
  169.6 36.1 %collective-permute-start.21 = (bf16[4,2,64,768]{3,2,1,0:T(8,128)(2,1)S(1)}, bf16[4,2,64,768]{3,2,1,0:T(8,128)(2,1)S(1)}, u32[]{:S(2)}, u32[]{:S(2)}) collective-permute-start(bf16[4,2,64,768]{3,2,1,0:T(8,128)(2,1)S(1)} %collective-permute-done.17.refs_2_), channel_id=1, source_target_pairs={{0,2},{1,3},{2,0},{3,1},{4,6},{5,7},{6,4},{7,5},{8,10},{9,11},{10,... | collective-permute-start | bytes 2359304 | tf_op jit(solution)/shard_map/ppermute | solution.py:254
  195.4 35.5 %collective-permute-start.29 = (bf16[4,2,64,1280]{3,2,1,0:T(8,128)(2,1)}, bf16[4,2,64,1280]{3,2,1,0:T(8,128)(2,1)}, u32[]{:S(2)}, u32[]{:S(2)}) collective-permute-start(bf16[4,2,64,1280]{3,2,1,0:T(8,128)(2,1)} %collective-permute-done.27.refs_1_), channel_id=1, source_target_pairs={{0,1},{1,0},{2,6},{3,7},{4,5},{5,4},{6,2},{7,3},{8,9},{9,8},{10,14... | collective-permute-start | bytes 3932168 | tf_op jit(solution)/shard_map/ppermute | solution.py:254
  223.6 46.2 %collective-permute-start.30 = (bf16[4,2,64,1280]{3,2,1,0:T(8,128)(2,1)S(1)}, bf16[4,2,64,1280]{3,2,1,0:T(8,128)(2,1)}, u32[]{:S(2)}, u32[]{:S(2)}) collective-permute-start(bf16[4,2,64,1280]{3,2,1,0:T(8,128)(2,1)S(1)} %pad_maximum_fusion.4.refs_0_), channel_id=1, source_target_pairs={{0,2},{1,3},{2,0},{3,1},{4,6},{5,7},{6,4},{7,5},{8,10},{9,11},{10,... | collective-permute-start | bytes 3932168 | tf_op jit(solution)/shard_map/ppermute | solution.py:254
  230.4 39.5 %collective-permute-start.31 = (bf16[4,2,64,1280]{3,2,1,0:T(8,128)(2,1)}, bf16[4,2,64,1280]{3,2,1,0:T(8,128)(2,1)}, u32[]{:S(2)}, u32[]{:S(2)}) collective-permute-start(bf16[4,2,64,1280]{3,2,1,0:T(8,128)(2,1)} %collective-permute-done.27.refs_1_), channel_id=1, source_target_pairs={{0,2},{1,3},{2,0},{3,1},{4,6},{5,7},{6,4},{7,5},{8,10},{9,11},{10,... | collective-permute-start | bytes 3932168 | tf_op jit(solution)/shard_map/ppermute | solution.py:254
  230.5 39.4 %collective-permute-start.32 = (bf16[4,2,64,1280]{3,2,1,0:T(8,128)(2,1)}, bf16[4,2,64,1280]{3,2,1,0:T(8,128)(2,1)}, u32[]{:S(2)}, u32[]{:S(2)}) collective-permute-start(bf16[4,2,64,1280]{3,2,1,0:T(8,128)(2,1)} %collective-permute-done.28.refs_2_), channel_id=1, source_target_pairs={{0,2},{1,3},{2,0},{3,1},{4,6},{5,7},{6,4},{7,5},{8,10},{9,11},{10,... | collective-permute-start | bytes 3932168 | tf_op jit(solution)/shard_map/ppermute | solution.py:254
  230.9 39.0 %collective-permute-start.33 = (bf16[4,2,64,1280]{3,2,1,0:T(8,128)(2,1)}, bf16[4,2,64,1280]{3,2,1,0:T(8,128)(2,1)}, u32[]{:S(2)}, u32[]{:S(2)}) collective-permute-start(bf16[4,2,64,1280]{3,2,1,0:T(8,128)(2,1)} %collective-permute-done.29.refs_3_), channel_id=1, source_target_pairs={{0,2},{1,3},{2,0},{3,1},{4,6},{5,7},{6,4},{7,5},{8,10},{9,11},{10,... | collective-permute-start | bytes 3932168 | tf_op jit(solution)/shard_map/ppermute | solution.py:254
  444.0 78.2 %collective-permute-start.45 = (bf16[340,1024]{1,0:T(8,128)(2,1)}, bf16[340,1024]{1,0:T(8,128)(2,1)}, u32[]{:S(2)}, u32[]{:S(2)}) collective-permute-start(bf16[340,1024]{1,0:T(8,128)(2,1)} %dynamic-slice_convert_fusion.1), channel_id=1, source_target_pairs={{0,1},{1,0},{2,3},{3,2},{4,5},{5,4},{6,7},{7,6},{8,9},{9,8},{10,11... | collective-permute-start | bytes 2088968 | tf_op jit(solution)/shard_map/ppermute | solution.py:254
  482.1 40.3 %collective-permute-start.47 = (bf16[340,1024]{1,0:T(8,128)(2,1)}, bf16[340,1024]{1,0:T(8,128)(2,1)}, u32[]{:S(2)}, u32[]{:S(2)}) collective-permute-start(bf16[340,1024]{1,0:T(8,128)(2,1)} %dynamic-slice_convert_fusion), channel_id=1, source_target_pairs={{0,1},{1,0},{2,3},{3,2},{4,5},{5,4},{6,7},{7,6},{8,9},{9,8},{10,11... | collective-permute-start | bytes 2088968 | tf_op jit(solution)/shard_map/ppermute | solution.py:254
  544.4 42.4 %collective-permute-start.88 = (bf16[512,1024]{1,0:T(8,128)(2,1)S(1)}, bf16[512,1024]{1,0:T(8,128)(2,1)}, u32[]{:S(2)}, u32[]{:S(2)}) collective-permute-start(bf16[512,1024]{1,0:T(8,128)(2,1)S(1)} %copy-done.34), channel_id=1, source_target_pairs={{0,2},{1,3},{2,0},{3,1},{4,6},{5,7},{6,4},{7,5},{8,10},{9,11},{10,... | collective-permute-start | bytes 3145736 | tf_op jit(solution)/shard_map/ppermute | solution.py:254
  567.1 39.1 %collective-permute-start.87 = (bf16[512,1024]{1,0:T(8,128)(2,1)S(1)}, bf16[512,1024]{1,0:T(8,128)(2,1)}, u32[]{:S(2)}, u32[]{:S(2)}) collective-permute-start(bf16[512,1024]{1,0:T(8,128)(2,1)S(1)} %copy-done.33), channel_id=1, source_target_pairs={{0,2},{1,3},{2,0},{3,1},{4,6},{5,7},{6,4},{7,5},{8,10},{9,11},{10,... | collective-permute-start | bytes 3145736 | tf_op jit(solution)/shard_map/ppermute | solution.py:254
  572.1 39.7 %collective-permute-start.81 = (bf16[512,1024]{1,0:T(8,128)(2,1)}, bf16[512,1024]{1,0:T(8,128)(2,1)}, u32[]{:S(2)}, u32[]{:S(2)}) collective-permute-start(bf16[512,1024]{1,0:T(8,128)(2,1)} %shard_map.206), channel_id=1, source_target_pairs={{0,1},{1,0},{2,6},{3,7},{4,5},{5,4},{6,2},{7,3},{8,9},{9,8},{10,14... | collective-permute-start | bytes 3145736 | tf_op jit(solution)/shard_map/ppermute | solution.py:254
  575.5 38.7 %collective-permute-start.56 = (bf16[512,768]{1,0:T(8,128)(2,1)}, bf16[512,768]{1,0:T(8,128)(2,1)}, u32[]{:S(2)}, u32[]{:S(2)}) collective-permute-start(bf16[512,768]{1,0:T(8,128)(2,1)} %shard_map.186), channel_id=1, source_target_pairs={{0,1},{1,0},{2,6},{3,7},{4,5},{5,4},{6,2},{7,3},{8,9},{9,8},{10,14... | collective-permute-start | bytes 2359304 | tf_op jit(solution)/shard_map/ppermute | solution.py:254
  575.9 38.3 %collective-permute-start.60 = (bf16[512,768]{1,0:T(8,128)(2,1)}, bf16[512,768]{1,0:T(8,128)(2,1)}, u32[]{:S(2)}, u32[]{:S(2)}) collective-permute-start(bf16[512,768]{1,0:T(8,128)(2,1)} %add_convert_fusion.7), channel_id=1, source_target_pairs={{0,4},{1,5},{2,3},{3,2},{4,0},{5,1},{6,7},{7,6},{8,12},{9,13},{10,... | collective-permute-start | bytes 2359304 | tf_op jit(solution)/shard_map/ppermute | solution.py:254
  611.8 42.9 %collective-permute-start.89 = (bf16[512,1024]{1,0:T(8,128)(2,1)S(1)}, bf16[512,1024]{1,0:T(8,128)(2,1)S(1)}, u32[]{:S(2)}, u32[]{:S(2)}) collective-permute-start(bf16[512,1024]{1,0:T(8,128)(2,1)S(1)} %copy-done.38), channel_id=1, source_target_pairs={{0,1},{1,0},{2,6},{3,7},{4,5},{5,4},{6,2},{7,3},{8,9},{9,8},{10,14... | collective-permute-start | bytes 3145736 | tf_op jit(solution)/shard_map/ppermute | solution.py:254
  (154 other events, 2558.3 us)

commit v2 on v1

--- a/solution.py
+++ b/solution.py
@@ -235,6 +235,7 @@
 TN = (((0,), (0,)), ((), ()))
 HIDDEN = -1e30
 VMEM_LIMIT = 60 * 1024 * 1024
+BRIEF = pl.CostEstimate(flops=0, bytes_accessed=0, transcendentals=0)
 
 
 def perm_of(step):
@@ -292,154 +293,139 @@
     return lax.dot_general(left, right, dims, preferred_element_type=F32)
 
 
-def gather_near_first(rows):
-    rows = jnp.concatenate([rows, send(rows, to_core)])
-    rows = jnp.concatenate([rows, send(rows, to_x)])
-    return jnp.concatenate([rows] + [send(rows, to_z(k)) for k in range(1, ZS)])
-
-
-def reduce_near_first(terms):
-    terms = terms[:, :, 0] + send(terms[:, :, 1], to_core)
-    terms = terms[:, 0] + send(terms[:, 1], to_x)
-    total = terms[0]
-    for k in range(1, ZS):
-        total = total + send(terms[ZS - k], to_z(k))
-    return total
-
-
-def gather_pieces(keep, give):
-    two = jnp.stack([keep, send(give, to_core)])
-    four = jnp.stack([two] + [send(two, to_z(k)) for k in range(1, ZS)])
-    near = send(four, to_near)
-    mine = [four, near, send(four, to_far), send(near, to_far)]
-    return mine + [send(piece, to_core) for piece in mine]
-
-
-def assemble_kernel(parts, where_ref, *refs):
-    pieces, outs, sem = refs[:8], refs[8:-1], refs[-1]
+def hold(*values):
+    return lax.optimization_barrier(values)
+
+
+def send_z(values):
+    return [send(values, to_z(k)) for k in range(1, ZS)]
+
+
+def send_terms_z(terms):
+    return [send(terms[k - 1], to_z(k)) for k in range(1, ZS)]
+
+
+def assemble_kernel(widths, where_ref, *refs):
+    pieces, outs, sem = refs[:4], refs[4:-1], refs[-1]
     z, x, c, t = where_ref[0], where_ref[1], where_ref[2], where_ref[3]
-    for number, piece in enumerate(pieces):
-        owner = c if number < 4 else 1 - c
-        slot = number % 4
-        if slot == 0:
-            dx, dt = 0, 0
-        elif slot == 1:
-            dx, dt = 1 - owner, owner
-        elif slot == 2:
-            dx, dt = owner, 1 - owner
-        else:
-            dx, dt = 1, 1
+    for slot, piece in enumerate(pieces):
+        dx, dt = [(0, 0), (1 - c, c), (c, 1 - c), (1, 1)][slot]
         sx, st = x ^ dx, t ^ dt
         for dz in range(ZS):
             for dc in range(CS):
                 sz = (z + ZS - dz) % ZS
-                sc = owner ^ dc
+                sc = c ^ dc
                 row = pl.multiple_of(((sz * XS + sx) * CS + sc) * 64, 64)
-                for which, base, stride_t, stride_h, start, width in parts:
-                    column = pl.multiple_of(base + st * stride_t + owner * stride_h, 128)
+                start = 0
+                for which, width in enumerate(widths):
+                    column = pl.multiple_of(st * width, 128)
                     pltpu.make_async_copy(
                         piece.at[dz, dc, :, pl.ds(start, width)],
                         outs[which].at[pl.ds(row, 64), pl.ds(column, width)],
                         sem.at[which],
                     ).start()
+                    start += width
     for which, out in enumerate(outs):
         pltpu.make_async_copy(out, out, sem.at[which]).wait()
 
 
-def assemble(pieces, position, parts, widths):
+def assemble(pieces, position, widths):
     rows = ZS * XS * CS * 64
-    outs = [jax.ShapeDtypeStruct((rows, width), BF16) for width in widths]
     return pl.pallas_call(
-        functools.partial(assemble_kernel, parts),
-        out_shape=outs,
+        functools.partial(assemble_kernel, widths),
+        out_shape=[jax.ShapeDtypeStruct((rows, TS * width), BF16) for width in widths],
         in_specs=[pl.BlockSpec(memory_space=pltpu.SMEM)]
-        + [pl.BlockSpec(memory_space=pl.ANY)] * 8,
-        out_specs=[pl.BlockSpec(memory_space=pltpu.VMEM)] * len(outs),
-        scratch_shapes=[pltpu.SemaphoreType.DMA((len(outs),))],
+        + [pl.BlockSpec(memory_space=pl.ANY)] * 4,
+        out_specs=[pl.BlockSpec(memory_space=pltpu.VMEM)] * len(widths),
+        scratch_shapes=[pltpu.SemaphoreType.DMA((len(widths),))],
+        cost_estimate=BRIEF,
         compiler_params=pltpu.CompilerParams(vmem_limit_bytes=VMEM_LIMIT),
     )(position, *pieces)
 
 
-def product_kernel(*refs):
-    left = jnp.concatenate([ref[...] for ref in refs[1 : 1 + ZS]], axis=1)
-    right = refs[1 + ZS][...]
-    out = refs[-1]
-    total = matmul(left, right.reshape(right.shape[-2:]), TN)
-    if len(refs) == ZS + 4:
-        total = total + refs[2 + ZS][...].astype(F32)
-    out[...] = total.astype(out.dtype)
-
-
-def product(rows, columns, quarter, choice, added=None):
-    tokens = rows.shape[0]
+def product_kernel(count, with_added, *refs):
+    out, start = refs[-1], 0
+    for n in range(count):
+        left = refs[1 + 2 * n][...]
+        left = left.reshape(left.shape[0] * left.shape[1], left.shape[2])
+        right = refs[2 + 2 * n][...]
+        total = matmul(left, right, NN)
+        columns = pl.ds(start, right.shape[1])
+        if with_added:
+            total = total + refs[1 + 2 * count][0, :, columns].astype(F32)
+        out[0, :, columns] = total.astype(out.dtype)
+        start += right.shape[1]
+
+
+def products(factors, choice, added=None):
+    tokens = factors[0][0].shape[1]
     span = CS * 64
-    if columns.ndim == 3:
-        parts = columns.shape[0]
-        right = pl.BlockSpec((1, tokens, quarter), lambda p, s: (p, 0, s[1]))
-    else:
-        parts = 1
-        right = pl.BlockSpec((tokens, quarter), lambda p, s: (0, s[1]))
-    lefts = [
-        pl.BlockSpec((tokens, span), functools.partial(lambda n, p, s: (0, n * XS + s[0]), n))
-        for n in range(ZS)
-    ]
-    block = pl.BlockSpec((ZS * span, quarter), lambda p, s: (0, p))
+    operands, specs, width = [], [], 0
+    for rows, columns in factors:
+        m = columns.shape[1] // TS
+        operands += [rows.reshape(ZS, XS * span, tokens), columns]
+        specs += [
+            pl.BlockSpec((ZS, span, tokens), lambda n, s: (0, s[0, n], 0)),
+            pl.BlockSpec((tokens, m), lambda n, s: (0, s[1, n])),
+        ]
+        width += m
+    block = pl.BlockSpec((1, ZS * span, width), lambda n, s: (n, 0, 0))
     extra = [] if added is None else [added]
     return pl.pallas_call(
-        product_kernel,
-        out_shape=jax.ShapeDtypeStruct((ZS * span, parts * quarter), BF16),
+        functools.partial(product_kernel, len(factors), len(extra) == 1),
+        out_shape=jax.ShapeDtypeStruct((4, ZS * span, width), BF16),
         grid_spec=pltpu.PrefetchScalarGridSpec(
             num_scalar_prefetch=1,
-            grid=(parts,),
-            in_specs=lefts + [right] + [block] * len(extra),
+            grid=(4,),
+            in_specs=specs + [block] * len(extra),
             out_specs=block,
         ),
-        cost_estimate=pl.CostEstimate(
-            flops=2 * tokens * ZS * span * parts * quarter,
-            bytes_accessed=2 * (tokens + ZS * span) * (ZS * span + parts * quarter),
-            transcendentals=0,
-        ),
+        cost_estimate=BRIEF,
         compiler_params=pltpu.CompilerParams(vmem_limit_bytes=VMEM_LIMIT),
-    )(choice, *([rows] * ZS), columns, *extra)
-
-
-def scatter_sum(rows, columns, quarter, z, x, c, t):
-    def block(dx, dt, dh, added=None):
-        choice = jnp.stack([x ^ dx, (t ^ dt) * 2 + (c ^ dh)]).astype(jnp.int32)
-        return product(rows, columns, quarter, choice, added)
-
-    def on_chip(dx, dt, other_dx, other_dt):
-        return block(dx, dt, 0, send(block(other_dx, other_dt, 1), to_core))
-
-    flag = 1 - c
-    far_both = send(on_chip(1, 1, 1, 1), to_far)
-    far_one = send(on_chip(c, flag, flag, c), to_far)
-    near = on_chip(flag, c, c, flag).astype(F32) + far_both.astype(F32)
-    near = send(near.astype(BF16), to_near)
-    whole = on_chip(0, 0, 0, 0).astype(F32) + far_one.astype(F32) + near.astype(F32)
+    )(choice, *operands, *extra)
+
+
+def block_choice(core, where):
+    z, x, c, t = where
+    dx = jnp.stack([jnp.ones_like(core), core, 1 - core, jnp.zeros_like(core)])
+    dt = jnp.stack([jnp.ones_like(core), 1 - core, core, jnp.zeros_like(core)])
+    return jnp.stack([x ^ dx, t ^ dt]).astype(jnp.int32)
+
+
+def scatter_near(blocks, far):
+    return (blocks[2].astype(F32) + far[0].astype(F32)).astype(BF16)
+
+
+def scatter_z(blocks, far, near, where):
+    z = where[0]
+    whole = blocks[3].astype(F32) + far[1].astype(F32) + near.astype(F32)
     whole = whole.astype(BF16).reshape(ZS, CS, 64, whole.shape[-1])
-    total = pick(whole, z).astype(F32)
-    for k in range(1, ZS):
-        total = total + send(pick(whole, (z + k) % ZS), to_z(k)).astype(F32)
-    return pick(total, c), send(pick(total, 1 - c).astype(BF16), to_core).astype(F32)
+    return [pick(whole, (z + k) % ZS) for k in range(ZS)]
+
+
+def scatter_total(own, others, where):
+    c = where[2]
+    total = sum(term.astype(F32) for term in [own] + list(others))
+    return pick(total, c), pick(total, 1 - c).astype(BF16)
 
 
 def in_order(own, other, bit):
     return jnp.where(bit == 0, own, other), jnp.where(bit == 0, other, own)
 
 
-def whole_image(values, t):
-    own = pick(values, t)
-    other = send(pick(values, 1 - t).astype(BF16), to_t).astype(F32)
-    return jnp.concatenate(in_order(own, other, t), axis=0)
-
-
-def split_image(values, t):
+def join_image(values, other, t):
+    return jnp.concatenate(in_order(pick(values, t), other.astype(F32), t), axis=0)
+
+
+def own_and_other(values, t):
     half = values.shape[0] // 2
     own = lax.dynamic_slice_in_dim(values, t * half, half, axis=0)
     give = lax.dynamic_slice_in_dim(values, (1 - t) * half, half, axis=0)
-    other = send(give.astype(BF16), to_t).astype(F32)
-    return jnp.stack(in_order(own, other, t))
+    return own, give.astype(BF16)
+
+
+def two_images(own, other, t):
+    return jnp.stack(in_order(own, other.astype(F32), t))
 
 
 def unit_of(values, mask):
@@ -453,15 +439,16 @@
     return [(lane >= n * head_dim) & (lane < (n + 1) * head_dim) for n in range(2)]
 
 
-def attend_kernel(head_dim, scale_ref, row_ref, column_ref, q_ref, k_ref, v_ref, out_ref, bias_ref):
+def attend_kernel(head_dim, scale_ref, row_ref, column_ref, raw_ref, out_ref, bias_ref):
     pair = pl.program_id(0)
 
     @pl.when(pair == 0)
     def _():
         bias_ref[...] = jnp.where(row_ref[...] <= column_ref[...], 0.0, HIDDEN)
 
-    q, k = q_ref[...].astype(F32), k_ref[...].astype(F32)
-    v = v_ref[...]
+    lanes = 2 * head_dim
+    q, k = raw_ref[:, :lanes].astype(F32), raw_ref[:, lanes : 2 * lanes].astype(F32)
+    v = raw_ref[:, 2 * lanes :]
     values = jnp.concatenate([v, jnp.ones_like(v)], axis=1)
     masks = head_masks(q.shape, head_dim)
     k_hat = (unit_of(k, masks[0])[0] + unit_of(k, masks[1])[0]).astype(BF16)
@@ -483,9 +470,8 @@
     lanes = 2 * head_dim
     pairs = width // lanes
 
-    def block(part):
-        return pl.BlockSpec((tokens, lanes), lambda n: (0, part * pairs + n))
-
+    block = pl.BlockSpec((tokens, lanes), lambda n: (0, n))
+    triple = pl.BlockSpec((tokens, 3 * lanes), lambda n: (0, n))
     return pl.pallas_call(
         functools.partial(attend_kernel, head_dim),
         out_shape=jax.ShapeDtypeStruct((tokens, width), BF16),
@@ -494,19 +480,13 @@
             pl.BlockSpec(memory_space=pltpu.SMEM),
             pl.BlockSpec((1, tokens), lambda n: (0, 0)),
             pl.BlockSpec((tokens, 1), lambda n: (0, 0)),
-            block(0),
-            block(1),
-            block(2),
+            triple,
         ],
-        out_specs=pl.BlockSpec((tokens, lanes), lambda n: (0, n)),
+        out_specs=block,
         scratch_shapes=[pltpu.VMEM((tokens, tokens), F32)],
-        cost_estimate=pl.CostEstimate(
-            flops=4 * tokens * tokens * width,
-            bytes_accessed=8 * tokens * width,
-            transcendentals=tokens * tokens * all_scale.shape[0],
-        ),
+        cost_estimate=BRIEF,
         compiler_params=pltpu.CompilerParams(vmem_limit_bytes=VMEM_LIMIT),
-    )(all_scale, scale_row[None, :], scale_row[:, None], raw, raw, raw)
+    )(all_scale, scale_row[None, :], scale_row[:, None], raw)
 
 
 def attend_back_kernel(
@@ -514,9 +494,7 @@
     scale_ref,
     row_ref,
     column_ref,
-    q_ref,
-    k_ref,
-    v_ref,
+    raw_ref,
     mixed_ref,
     d_mixed_ref,
     out_ref,
@@ -529,8 +507,9 @@
     def _():
         bias_ref[...] = jnp.where(column_ref[...] <= row_ref[...], 0.0, HIDDEN)
 
-    q, k = q_ref[...].astype(F32), k_ref[...].astype(F32)
-    v, d_mixed = v_ref[...], d_mixed_ref[...]
+    lanes = 2 * head_dim
+    q, k = raw_ref[:, :lanes].astype(F32), raw_ref[:, lanes : 2 * lanes].astype(F32)
+    v, d_mixed = raw_ref[:, 2 * lanes :], d_mixed_ref[...]
     masks = head_masks(q.shape, head_dim)
     k_units = [unit_of(k, mask) for mask in masks]
     k_hat = (k_units[0][0] + k_units[1][0]).astype(BF16)
@@ -563,9 +542,9 @@
         else:
             d_q_all, d_k_all = d_q_all + d_q, d_k_all + d_k
             d_v_all, term_all = d_v_all + d_v, term_all + term_n
-    out_ref[0] = d_q_all.astype(out_ref.dtype)
-    out_ref[1] = d_k_all.astype(out_ref.dtype)
-    out_ref[2] = d_v_all.astype(out_ref.dtype)
+    out_ref[:, :lanes] = d_q_all.astype(out_ref.dtype)
+    out_ref[:, lanes : 2 * lanes] = d_k_all.astype(out_ref.dtype)
+    out_ref[:, 2 * lanes :] = d_v_all.astype(out_ref.dtype)
     term_ref[...] = jnp.broadcast_to(term_all, term_ref.shape)
 
 
@@ -576,13 +555,12 @@
     lanes = 2 * head_dim
     pairs = width // lanes
 
-    def block(part):
-        return pl.BlockSpec((tokens, lanes), lambda n: (0, part * pairs + n))
-
+    block = pl.BlockSpec((tokens, lanes), lambda n: (0, n))
+    triple = pl.BlockSpec((tokens, 3 * lanes), lambda n: (0, n))
     d_raw, terms = pl.pallas_call(
         functools.partial(attend_back_kernel, head_dim),
         out_shape=[
-            jax.ShapeDtypeStruct((3, tokens, width), BF16),
+            jax.ShapeDtypeStruct((tokens, 3 * width), BF16),
             jax.ShapeDtypeStruct((8, width), F32),
         ],
         grid=(pairs,),
@@ -590,24 +568,18 @@
             pl.BlockSpec(memory_space=pltpu.SMEM),
             pl.BlockSpec((1, tokens), lambda n: (0, 0)),
             pl.BlockSpec((tokens, 1), lambda n: (0, 0)),
-            block(0),
-            block(1),
-            block(2),
-            block(0),
-            block(0),
+            triple,
+            block,
+            block,
         ],
         out_specs=[
-            pl.BlockSpec((3, tokens, lanes), lambda n: (0, 0, n)),
+            triple,
             pl.BlockSpec((8, lanes), lambda n: (0, n)),
         ],
         scratch_shapes=[pltpu.VMEM((tokens, tokens), F32)],
-        cost_estimate=pl.CostEstimate(
-            flops=10 * tokens * tokens * width,
-            bytes_accessed=16 * tokens * width,
-            transcendentals=tokens * tokens * heads,
-        ),
+        cost_estimate=BRIEF,
         compiler_params=pltpu.CompilerParams(vmem_limit_bytes=VMEM_LIMIT),
-    )(all_scale, scale_row[None, :], scale_row[:, None], raw, raw, raw, mixed, d_mixed)
+    )(all_scale, scale_row[None, :], scale_row[:, None], raw, mixed, d_mixed)
     return d_raw, jnp.sum(terms[0].reshape(heads, head_dim), axis=1)
 
 
@@ -628,106 +600,204 @@
     z, x, c, t = place()
     position = jnp.stack([z, x, c, t]).astype(jnp.int32)
 
-    qkv_parts = [halves(w_qkv[:, n].astype(BF16), c, quarter) for n in range(3)]
-    proj_parts = halves(w_proj.astype(BF16).T, c, quarter)
-    fc1_parts = halves(w_fc1.astype(BF16), c, hidden_quarter)
-    fc2_parts = halves(w_fc2.astype(BF16).T, c, hidden_quarter)
-    pieces_qkv = gather_pieces(
-        *[jnp.concatenate([part[n] for part in qkv_parts], axis=1) for n in range(2)]
-    )
-    pieces_mid = gather_pieces(
-        *[jnp.concatenate([proj_parts[n], fc1_parts[n]], axis=1) for n in range(2)]
-    )
-    pieces_fc2 = gather_pieces(*fc2_parts)
-    (qkv_low,) = assemble(
-        pieces_qkv,
-        position,
-        [(0, n * width, 2 * quarter, quarter, n * quarter, quarter) for n in range(3)],
-        [3 * width],
-    )
-    proj_low, fc1_low = assemble(
-        pieces_mid,
-        position,
-        [
-            (0, 0, 2 * quarter, quarter, 0, quarter),
-            (1, 0, 2 * hidden_quarter, hidden_quarter, quarter, hidden_quarter),
-        ],
-        [width, 4 * hidden_quarter],
-    )
-    (fc2_low,) = assemble(
-        pieces_fc2,
-        position,
-        [(0, 0, 2 * hidden_quarter, hidden_quarter, 0, hidden_quarter)],
-        [4 * hidden_quarter],
-    )
-
+    where = (z, x, c, t)
+
+    pair = 2 * width // heads
+
+    choice_given, choice_kept = block_choice(1 - c, where), block_choice(c, where)
+
+    token_other = send(pick(inputs, 1 - t).astype(BF16), to_t)
     label_pair = jnp.stack(in_order(labels[0], labels[1], t)).astype(F32)
     label_tile = jnp.broadcast_to(label_pair[:, None], (2, 128))
-    all_labels = gather_near_first(label_tile)[:, 0].astype(jnp.int32)
+    label_z = send_z(label_tile)
+    scale_tile = jnp.broadcast_to(head_scale[None, :], (8, head_scale.shape[0]))
+    scale_other = send(scale_tile, to_t)
+    qkv_halves = []
+    for side in (c, 1 - c):
+        columns = [
+            lax.dynamic_slice_in_dim(w_qkv[:, n].astype(BF16), side * quarter + j * pair, pair, 1)
+            for j in range(quarter // pair)
+            for n in range(3)
+        ]
+        qkv_halves.append(jnp.concatenate(columns, axis=1))
+    keep_qkv, give_qkv = qkv_halves
+    keep_qkv, recv_qkv, label_z, scale_other, rest = hold(
+        keep_qkv,
+        send(give_qkv, to_core),
+        label_z,
+        scale_other,
+        (cotangent, w_ada, w_proj, w_fc1, w_fc2, table),
+    )
+    cotangent, w_ada, w_proj, w_fc1, w_fc2, table = rest
+    two_qkv = jnp.stack([keep_qkv, recv_qkv])
+    z_qkv = send_z(two_qkv)
+    scale_row = pick(scale_ids, t)
+    scales = jnp.concatenate(in_order(head_scale, scale_other[0], t)).reshape(TS, 2, -1)
+    scale_own, scale_oth = pick(scales, c, 1).reshape(-1), pick(scales, 1 - c, 1).reshape(-1)
+
+    label_rows = jnp.concatenate([label_tile] + label_z)
+    label_rows = jnp.concatenate([label_rows, send(label_rows, to_x)])
+    label_rows = jnp.concatenate([label_rows, send(label_rows, to_core)])
+    all_labels = label_rows[:, 0].astype(jnp.int32)
     one_hot = (all_labels[:, None] == jnp.arange(classes)[None, :]).astype(BF16)
     condition = matmul(one_hot, table.astype(BF16), NN)
     silu_low = jax.nn.silu(condition).astype(BF16)
     ada_low = w_ada.astype(BF16).reshape(rows, 6 * width)
     silu_own = silu_low.reshape(-1, TS, rows)[:, 0]
-    partial = matmul(silu_own, ada_low, NN).reshape(ZS, XS, CS, 6 * width)
-    modulation = reduce_near_first(partial).reshape(6, 1, width)
+    partial = matmul(silu_own, ada_low, NN).reshape(CS, XS, ZS, 6 * width)
+    partial = partial[0] + send(partial[1], to_core)
+    own_part, x_part = partial[0], send(partial[1], to_x)
+    w_fc1, w_proj_t, w_fc2_t = w_fc1.astype(BF16), w_proj.astype(BF16).T, w_fc2.astype(BF16).T
+    rest_halves = [halves(w_proj_t, c, quarter), halves(w_fc1, c, hidden_quarter)]
+    rest_halves.append(halves(w_fc2_t, c, hidden_quarter))
+    keep_rest, give_rest = [jnp.concatenate([part[n] for part in rest_halves], 1) for n in range(2)]
+    cotangent_other = send(pick(cotangent, 1 - t).astype(BF16), to_t)
+    z_qkv, own_part, x_part, token_other, recv_rest = hold(
+        z_qkv, own_part, x_part, token_other, send(give_rest, to_core)
+    )
+
+    partial = own_part + x_part
+    four_qkv = jnp.stack([two_qkv] + z_qkv)
+    near_qkv, far_qkv = send(four_qkv, to_near), send(four_qkv, to_far)
+    mod_z = send_terms_z([partial[ZS - k] for k in range(1, ZS)])
+    mod_z, keep_rest = hold(mod_z, keep_rest)
+    split = quarter + hidden_quarter
+    two_mid = jnp.stack([keep_rest[:, :split], recv_rest[:, :split]])
+    two_fc2 = jnp.stack([keep_rest[:, split:], recv_rest[:, split:]])
+    mid_2 = send(two_mid, to_z(2))
+    modulation = sum(mod_z, partial[0]).reshape(6, 1, width)
     gain_attn, gain_mlp, scale_attn, scale_mlp, shift_attn, shift_mlp = modulation
-
-    tokens_in = whole_image(inputs, t)
-    upstream = whole_image(cotangent, t)
-    scale_row = pick(scale_ids, t)
-    other_scale = send(jnp.broadcast_to(head_scale[None, :], (8, head_scale.shape[0])), to_t)[0]
-    all_scale = jnp.concatenate(in_order(head_scale, other_scale, t))
-
+    tokens_in = join_image(inputs, token_other, t)
+    near_qkv, far_qkv, mid_2, two_mid = hold(near_qkv, far_qkv, mid_2, two_mid)
+    last_qkv = send(near_qkv, to_far)
+    mid_1, mid_3 = send(two_mid, to_z(1)), send(two_mid, to_z(3))
     normed_one, inverse_one = layer_norm(tokens_in)
     hidden_one = (normed_one * (1.0 + scale_attn) + shift_attn).astype(BF16)
-    raw = matmul(hidden_one, qkv_low, NN).astype(BF16)
-    mixed = attend_whole(raw, scale_row, all_scale)
-    attended = matmul(mixed, proj_low, NT)
+    last_qkv, mid_1, mid_3, hidden_one, cotangent_other = hold(
+        last_qkv, mid_1, mid_3, hidden_one, cotangent_other
+    )
+    four_mid = jnp.stack([two_mid, mid_1, mid_2, mid_3])
+    near_mid, far_mid = send(four_mid, to_near), send(four_mid, to_far)
+    z_fc2 = send_z(two_fc2)
+    (qkv_own,) = assemble([four_qkv, near_qkv, far_qkv, last_qkv], position, [3 * quarter])
+    raw_own = matmul(hidden_one, qkv_own, NN).astype(BF16)
+    raw_own, qkv_oth = hold(raw_own, send(qkv_own, to_core))
+    raw_oth = matmul(hidden_one, qkv_oth, NN).astype(BF16)
+    mixed_own = attend_whole(raw_own, scale_row, scale_own)
+    mixed_own, near_mid, far_mid, z_fc2, raw_oth = hold(mixed_own, near_mid, far_mid, z_fc2, raw_oth)
+    last_mid = send(near_mid, to_far)
+    mixed_oth = attend_whole(raw_oth, scale_row, scale_oth)
+    mixed_oth, last_mid = hold(mixed_oth, last_mid)
+    four_fc2 = jnp.stack([two_fc2] + z_fc2)
+    near_fc2, far_fc2 = send(four_fc2, to_near), send(four_fc2, to_far)
+    proj_own, fc1_own = assemble(
+        [four_mid, near_mid, far_mid, last_mid], position, [quarter, hidden_quarter]
+    )
+    upstream = join_image(cotangent, cotangent_other, t)
+    d_branch = (gain_mlp * upstream).astype(BF16)
+    proj_oth, d_branch = hold(send(proj_own, to_core), d_branch)
+    fc1_oth = send(fc1_own, to_core)
+    attended = matmul(mixed_own, proj_own, NT) + matmul(mixed_oth, proj_oth, NT)
     middle = tokens_in + gain_attn * attended
     normed_two, inverse_two = layer_norm(middle)
     hidden_two = (normed_two * (1.0 + scale_mlp) + shift_mlp).astype(BF16)
-    before = matmul(hidden_two, fc1_low, NN)
-    gelu_fn = functools.partial(jax.nn.gelu, approximate=True)
-    active_f, gelu_pull = jax.vjp(gelu_fn, before)
-    active = active_f.astype(BF16)
-    slope = gelu_pull(jnp.ones_like(before))[0].astype(BF16)
-    branch = matmul(active, fc2_low, NT)
-    output = split_image(middle + gain_mlp * branch, t)
+    hidden_two, fc1_oth = hold(hidden_two, fc1_oth)
+
+    def activate(weights):
+        before = matmul(hidden_two, weights, NN)
+        active, pull = jax.vjp(functools.partial(jax.nn.gelu, approximate=True), before)
+        return active.astype(BF16), pull(jnp.ones_like(before))[0].astype(BF16)
+
+    active_oth, slope_oth = activate(fc1_oth)
+    active_oth, slope_oth, near_fc2, far_fc2 = hold(active_oth, slope_oth, near_fc2, far_fc2)
+    last_fc2 = send(near_fc2, to_far)
+    active_own, slope_own = activate(fc1_own)
+    d_branch_t = d_branch.T
+    given = products([(d_branch_t, active_oth)], choice_given)
+    given, active_own, slope_own, last_fc2 = hold(given, active_own, slope_own, last_fc2)
+    added = send(given, to_core)
+    (fc2_own,) = assemble([four_fc2, near_fc2, far_fc2, last_fc2], position, [hidden_quarter])
+    fc2_own, added = hold(fc2_own, added)
+    fc2_oth = send(fc2_own, to_core)
+    blocks_fc2 = products([(d_branch_t, active_own)], choice_kept, added)
+    blocks_fc2, fc2_oth = hold(blocks_fc2, fc2_oth)
+    far_fc2 = send(blocks_fc2[:2], to_far)
+    d_before_oth = (matmul(d_branch, fc2_oth, NN) * slope_oth.astype(F32)).astype(BF16)
+    d_before_own = (matmul(d_branch, fc2_own, NN) * slope_own.astype(F32)).astype(BF16)
+    branch = matmul(active_own, fc2_own, NT) + matmul(active_oth, fc2_oth, NT)
+    output_own, output_give = own_and_other(middle + gain_mlp * branch, t)
 
     d_gain_mlp = jnp.sum(upstream * branch, axis=0)
-    d_branch = (gain_mlp * upstream).astype(BF16)
-    grad_fc2 = scatter_sum(d_branch, active, hidden_quarter, z, x, c, t)
-    d_before = (matmul(d_branch, fc2_low, NN) * slope.astype(F32)).astype(BF16)
-    grad_fc1 = scatter_sum(hidden_two, d_before, hidden_quarter, z, x, c, t)
-    d_hidden_two = matmul(d_before, fc1_low, NT)
+    d_before_oth, d_before_own, output_give, far_fc2 = hold(
+        d_before_oth, d_before_own, output_give, far_fc2
+    )
+    near_fc2 = send(scatter_near(blocks_fc2, far_fc2), to_near)
+    d_hidden_two = matmul(d_before_own, fc1_own, NT) + matmul(d_before_oth, fc1_oth, NT)
     d_scale_mlp = jnp.sum(d_hidden_two * normed_two, axis=0)
     d_shift_mlp = jnp.sum(d_hidden_two, axis=0)
     d_middle = upstream + norm_back(d_hidden_two * (1.0 + scale_mlp), normed_two, inverse_two)
     d_gain_attn = jnp.sum(d_middle * attended, axis=0)
     d_attended = (gain_attn * d_middle).astype(BF16)
-    grad_proj = scatter_sum(d_attended, mixed, quarter, z, x, c, t)
-    d_mixed = matmul(d_attended, proj_low, NN).astype(BF16)
-    d_raw, scale_terms = attend_back_whole(raw, mixed, d_mixed, scale_row, all_scale)
-    grad_qkv = scatter_sum(hidden_one, d_raw, quarter, z, x, c, t)
-    d_hidden_one = sum(
-        matmul(d_raw[n], qkv_low[:, n * width : (n + 1) * width], NT) for n in range(3)
-    )
+    d_attended, near_fc2 = hold(d_attended, near_fc2)
+    z_fc2 = scatter_z(blocks_fc2, far_fc2, near_fc2, where)
+    own_fc2, others_fc2 = z_fc2[0], send_terms_z(z_fc2[1:])
+    hidden_two_t, d_attended_t = hidden_two.T, d_attended.T
+    given = products([(d_attended_t, mixed_oth), (hidden_two_t, d_before_oth)], choice_given)
+    given, d_attended = hold(given, d_attended)
+    d_mixed_oth = matmul(d_attended, proj_oth, NN).astype(BF16)
+    d_mixed_own = matmul(d_attended, proj_own, NN).astype(BF16)
+    d_mixed_oth, d_mixed_own, added = hold(d_mixed_oth, d_mixed_own, send(given, to_core))
+    blocks_mid = products(
+        [(d_attended_t, mixed_own), (hidden_two_t, d_before_own)], choice_kept, added
+    )
+    blocks_mid, d_mixed_oth, others_fc2 = hold(blocks_mid, d_mixed_oth, others_fc2)
+    far_mid = send(blocks_mid[:2], to_far)
+    d_raw_oth, terms_oth = attend_back_whole(raw_oth, mixed_oth, d_mixed_oth, scale_row, scale_oth)
+    hidden_one_t = hidden_one.T
+    given = products([(hidden_one_t, d_raw_oth)], choice_given)
+    given, far_mid, d_mixed_own = hold(given, far_mid, d_mixed_own)
+    near_mid = send(scatter_near(blocks_mid, far_mid), to_near)
+    added, output_other = send(given, to_core), send(output_give, to_t)
+    d_raw_own, terms_own = attend_back_whole(raw_own, mixed_own, d_mixed_own, scale_row, scale_own)
+    d_raw_own, near_mid, added = hold(d_raw_own, near_mid, added)
+    z_mid = scatter_z(blocks_mid, far_mid, near_mid, where)
+    own_mid, others_mid = z_mid[0], send_terms_z(z_mid[1:])
+    blocks_qkv = products([(hidden_one_t, d_raw_own)], choice_kept, added)
+    blocks_qkv, d_raw_own = hold(blocks_qkv, d_raw_own)
+    far_qkv = send(blocks_qkv[:2], to_far)
+    d_hidden_one = matmul(d_raw_own, qkv_own, NT) + matmul(d_raw_oth, qkv_oth, NT)
     d_scale_attn = jnp.sum(d_hidden_one * normed_one, axis=0)
     d_shift_attn = jnp.sum(d_hidden_one, axis=0)
-    d_inputs = d_middle + norm_back(d_hidden_one * (1.0 + scale_attn), normed_one, inverse_one)
-    d_inputs = split_image(d_inputs, t)
-
     d_modulation = jnp.concatenate(
         [d_gain_attn, d_gain_mlp, d_scale_attn, d_scale_mlp, d_shift_attn, d_shift_mlp]
     )
+    terms = in_order(terms_own.reshape(TS, -1), terms_oth.reshape(TS, -1), c)
+    scale_terms = jnp.concatenate(terms, axis=1).reshape(-1)
     scale_high = lax.reduce_precision(scale_terms, 8, 7)
     row = jnp.concatenate(
         [d_modulation, scale_high, scale_terms - scale_high, jnp.zeros((128 - 2 * heads,), F32)]
     ).astype(BF16)[None, :]
-    everything = gather_near_first(jnp.concatenate([row, send(row, to_t)]))
-    d_mod_all = everything[:, : 6 * width]
-    scale_sum = jnp.sum(everything[:, 6 * width : 6 * width + 2 * heads].astype(F32), axis=0)
+    d_inputs = d_middle + norm_back(d_hidden_one * (1.0 + scale_attn), normed_one, inverse_one)
+    inputs_own, inputs_give = own_and_other(d_inputs, t)
+    row_other = send(row, to_t)
+    far_qkv, inputs_give, row_other, output_other, others_mid = hold(
+        far_qkv, inputs_give, row_other, output_other, others_mid
+    )
+    near_qkv = send(scatter_near(blocks_qkv, far_qkv), to_near)
+    inputs_other = send(inputs_give, to_t)
+    mod_rows = jnp.concatenate([row, row_other])
+    half_fc2, other_fc2 = scatter_total(own_fc2, others_fc2, where)
+    half_mid, other_mid = scatter_total(own_mid, others_mid, where)
+    other_rest = jnp.concatenate([other_mid, other_fc2], axis=1)
+    near_qkv, mod_z, other_rest = hold(near_qkv, send_z(mod_rows), send(other_rest, to_core))
+    z_qkv = scatter_z(blocks_qkv, far_qkv, near_qkv, where)
+    own_qkv, others_qkv = z_qkv[0], send_terms_z(z_qkv[1:])
+    mod_rows = jnp.concatenate([mod_rows] + mod_z)
+    mod_rows = jnp.concatenate([mod_rows, send(mod_rows, to_x)])
+    mod_rows = jnp.concatenate([mod_rows, send(mod_rows, to_core)])
+
+    d_mod_all = mod_rows[:, : 6 * width]
+    scale_sum = jnp.sum(mod_rows[:, 6 * width : 6 * width + 2 * heads].astype(F32), axis=0)
     scale_sum = (scale_sum[:heads] + scale_sum[heads:]).reshape(TS, heads // TS)
     grad_scale = pick(scale_sum, t)
     grad_ada = matmul(silu_low, d_mod_all, TN).reshape(rows, 6, width)
@@ -736,31 +806,34 @@
     d_condition = silu_pull(d_silu)[0]
     grad_table = jnp.dot(one_hot.astype(F32).T, d_condition, precision=HIGHEST)
 
-    own_qkv, other_qkv = grad_qkv
-    grad_qkv = jnp.stack(
-        [
-            jnp.concatenate(
-                in_order(
-                    own_qkv[:, n * quarter : (n + 1) * quarter],
-                    other_qkv[:, n * quarter : (n + 1) * quarter],
-                    c,
-                ),
-                axis=1,
-            )
-            for n in range(3)
-        ],
-        axis=1,
-    )
+    def joined(own, other):
+        return jnp.concatenate(in_order(own, other.astype(F32), c), axis=1)
+
+    grad_proj = joined(half_mid[:, :quarter], other_rest[:, :quarter]).T
+    grad_fc1 = joined(half_mid[:, quarter:], other_rest[:, quarter:split])
+    grad_fc2 = joined(half_fc2, other_rest[:, split:]).T
+    others_qkv, others = hold(
+        others_qkv, (grad_ada, grad_table, grad_scale, inputs_other, grad_proj, grad_fc1, grad_fc2)
+    )
+    grad_ada, grad_table, grad_scale, inputs_other, grad_proj, grad_fc1, grad_fc2 = others
+    half_qkv, other_qkv = scatter_total(own_qkv, others_qkv, where)
+    other_qkv = send(other_qkv, to_core)
+
+    def part_of(values, n):
+        starts = range(n * pair, 3 * quarter, 3 * pair)
+        return jnp.concatenate([values[:, start : start + pair] for start in starts], axis=1)
+
+    grad_qkv = [joined(part_of(half_qkv, n), part_of(other_qkv, n)) for n in range(3)]
     return (
-        output,
-        d_inputs,
+        two_images(output_own, output_other, t),
+        two_images(inputs_own, inputs_other, t),
         grad_table,
         grad_ada,
-        grad_qkv,
+        jnp.stack(grad_qkv, axis=1),
         grad_scale,
-        jnp.concatenate(in_order(*grad_proj, c), axis=1).T,
-        jnp.concatenate(in_order(*grad_fc1, c), axis=1),
-        jnp.concatenate(in_order(*grad_fc2, c), axis=1).T,
+        grad_proj,
+        grad_fc1,
+        grad_fc2,
     )
 
 

time: 712 us -> 532 us (0.75)
  Pallas kernels: 208 us -> 122 us
  waiting for transfers between devices: 175 us -> 99.3 us
  starting transfers between devices: 104 us -> 62.3 us
  local copies, waits for them, and re-layouts: 50.1 us -> 80.1 us
  other arithmetic: 62.5 us -> 53.1 us
    pallas_call x35 -> x9, Pallas kernels: 159 us -> 69.2 us  [the longest x6 54.5 us: products(): pl.pallas_call(functools.partial(product_kernel, len(factors), len(extra)...]
    ppermute x98 -> x65, waiting for transfers between devices: 175 us -> 99.3 us  [send(): return lax.ppermute(values, BOTH, perm_of(step))]
    ppermute x98 -> x65, starting transfers between devices: 104 us -> 62.3 us  [send(): return lax.ppermute(values, BOTH, perm_of(step))]
    unnamed x165 -> x170, local copies, waits for them, and re-layouts: 16.1 us -> 28.3 us
    transpose x0 -> x4, local copies, waits for them, and re-layouts: none -> 10.2 us  [the longest x2 5.13 us: on_device_whole(): hidden_two_t, d_attended_t = (hidden_two.T, d_attended.T)]
    another operation x25 -> x17, other arithmetic: 22.6 us -> 13.9 us  [the longest x4 3.75 us: two_images(): return jnp.stack(in_order(own, other.astype(F32), t))]
    slice x2 -> x8, local copies, waits for them, and re-layouts: 0.09 us -> 7.22 us  [the longest x1 3.42 us: on_device_whole(): far_mid = send(blocks_mid[:2], to_far)]
    dot_general x14 -> x20, matrix products: 94.9 us -> 102 us  [matmul(): return lax.dot_general(left, right, dims, preferred_element_type=F32)]
  transfers between devices with their start and end apart: 98 -> 65, of which waited for: 26 -> 27; matrix products, arithmetic and copies ran while one was open for 18% -> 38% of each run, Pallas kernels for 16% -> 19%
where the time goes in v2:
time: 532 us; the launch traced here: 524 us
  Pallas kernels  122 us (23%)
  matrix products  103 us (19%)
  waiting for transfers between devices  99.3 us (19%)
  local copies, waits for them, and re-layouts  80.1 us (15%)
  starting transfers between devices  62.3 us (12%)
  other arithmetic  53.1 us (10%)
    dot_general x20, matrix products, matmul(): return lax.dot_general(left, right, dims, preferred_element_type=F32)  102 us
    ppermute x65, waiting for transfers between devices, send(): return lax.ppermute(values, BOTH, perm_of(step))  99.3 us
    ppermute x65, starting transfers between devices, send(): return lax.ppermute(values, BOTH, perm_of(step))  62.3 us
    pallas_call x6, Pallas kernels, products(): pl.pallas_call(functools.partial(product_kernel, len(factors), len(extra)...  54.5 us
    pallas_call x2, Pallas kernels, attend_back_whole(): pl.pallas_call(functools.partial(attend_back_kernel, head_dim), out_shape...  36.3 us
    unnamed x170, local copies, waits for them, and re-layouts  28.3 us
    pallas_call x2, Pallas kernels, attend_whole(): pl.pallas_call(functools.partial(attend_kernel, head_dim), out_shape=jax....  16.5 us
    pallas_call x3, Pallas kernels, assemble(): pl.pallas_call(functools.partial(assemble_kernel, widths), out_shape=[jax...  14.8 us
  transfers between devices with their start and end apart: 65, of which 27 were waited for; matrix products, arithmetic and copies ran while one was open for 38% of the time, Pallas kernels for 19%

profile of v2, /device:TPU:9, one launch (start us, length us, event | category | flops | bytes accessed | tf_op | source)
XLA Modules:
  0.0 524.0 jit_solution(15203269401299287519)
XLA Ops:
  64.4 13.8 %collective-permute-done.19 = bf16[2,64,1280]{2,1,0:T(8,128)(2,1)S(1)} collective-permute-done((bf16[2,64,1280]{2,1,0:T(8,128)(2,1)S(1)}, bf16[2,64,1280]{2,1,0:T(8,128)(2,1)S(1)}, u32[]{:S(2)}, u32[]{:S(2)}) %collective-permute-start.19) | collective-permute-done | bytes 327712 | tf_op jit(solution)/shard_map/ppermute | solution.py:255
  91.5 11.0 %collective-permute-done.22 = bf16[2,64,1280]{2,1,0:T(8,128)(2,1)S(1)} collective-permute-done((bf16[2,64,1280]{2,1,0:T(8,128)(2,1)S(1)}, bf16[2,64,1280]{2,1,0:T(8,128)(2,1)S(1)}, u32[]{:S(2)}, u32[]{:S(2)}) %collective-permute-start.22) | collective-permute-done | bytes 327712 | tf_op jit(solution)/shard_map/ppermute | solution.py:255
  130.7 8.2 %shard_map.179.refs_2_.mixed_ref = bf16[680,512]{1,0:T(8,128)(2,1)} custom-call(f32[8]{0:T(128)} %reshape.550.scale_ref, s32[1,680]{1,0:T(1,128)} %constant_dynamic-slice_fusion.2.row_ref, s32[680,1]{1,0:T(8,128)} %copy.85.column_ref, bf16[680,1536]{1,0:T(8,128)(2,1)} %convolution_convert_fusion.1.raw_ref), custom_call_target="tpu_custom_call" | custom-call | tf_op jit(solution)/shard_map/pallas_call | solution.py:475
  147.2 8.3 %shard_map.180.refs_2_.mixed_ref = bf16[680,512]{1,0:T(8,128)(2,1)} custom-call(f32[8]{0:T(128)} %reshape.551.scale_ref, s32[1,680]{1,0:T(1,128)} %constant_dynamic-slice_fusion.2.row_ref, s32[680,1]{1,0:T(8,128)} %copy.85.column_ref, bf16[680,1536]{1,0:T(8,128)(2,1)} %convolution_convert_fusion.raw_ref), custom_call_target="tpu_custom_call" | custom-call | tf_op jit(solution)/shard_map/pallas_call | solution.py:475
  155.4 7.5 %collective-permute-done.30.refs_3_ = bf16[4,2,64,1280]{3,2,1,0:T(8,128)(2,1)} collective-permute-done((bf16[4,2,64,1280]{3,2,1,0:T(8,128)(2,1)}, bf16[4,2,64,1280]{3,2,1,0:T(8,128)(2,1)}, u32[]{:S(2)}, u32[]{:S(2)}) %collective-permute-start.30) | collective-permute-done | bytes 1310752 | tf_op jit(solution)/shard_map/ppermute | solution.py:255
  162.9 5.6 %shard_map.181 = (bf16[1024,512]{1,0:T(8,128)(2,1)}, bf16[1024,2048]{1,0:T(8,128)(2,1)}) custom-call(s32[4]{0:T(128)} %pad_add_fusion.6.where_ref, bf16[4,2,64,1280]{3,2,1,0:T(8,128)(2,1)} %pad_maximum_fusion.4.refs_0_, bf16[4,2,64,1280]{3,2,1,0:T(8,128)(2,1)} %collective-permute-done.25.refs_1_, bf16[4,2,64,1280]{3,2,1,0:T(8,128)(2,1)} %collective-permute-done.26.refs_2_, ...), custom_call_target="tpu_custom_call" | custom-call | tf_op jit(solution)/shard_map/pallas_call | solution.py:334
  187.3 10.7 %fusion.6 = (bf16[680,2048]{1,0:T(8,128)(2,1)}, bf16[680,2048]{1,0:T(8,128)(2,1)}) fusion(bf16[680,1024]{1,0:T(8,128)(2,1)S(1)} %add_convert_fusion, bf16[1024,2048]{1,0:T(8,128)(2,1)} %collective-permute-done.32), kind=kOutput, calls=%fused_computation.10 | convolution fusion | flops 2879979520 | bytes 11157504 | tf_op jit(solution)/shard_map/dot_general | solution.py:293
  202.5 8.3 %shard_map.182 = bf16[4,512,1024]{2,1,0:T(8,128)(2,1)} custom-call(s32[2,4]{1,0:T(2,128)} %pad_add_fusion.refs_0_, bf16[4,256,680]{2,1,0:T(8,128)(2,1)} %bitcast.229, bf16[680,2048]{1,0:T(8,128)(2,1)} %get-tuple-element.169.refs_2_), custom_call_target="tpu_custom_call" | custom-call | tf_op jit(solution)/shard_map/pallas_call | solution.py:374
  210.8 17.8 %fusion.13 = (bf16[680,2048]{1,0:T(8,128)(2,1)}, bf16[680,2048]{1,0:T(8,128)(2,1)}) fusion(bf16[680,1024]{1,0:T(8,128)(2,1)} %copy-done.21, bf16[1024,2048]{1,0:T(8,128)(2,1)} %get-tuple-element.163), kind=kOutput, calls=%fused_computation.17 | convolution fusion | flops 2879979520 | bytes 11157504 | tf_op jit(solution)/shard_map/dot_general | solution.py:293
  240.2 9.2 %shard_map.184 = bf16[4,512,1024]{2,1,0:T(8,128)(2,1)} custom-call(s32[2,4]{1,0:T(2,128)} %pad_add_fusion.1.refs_0_, bf16[4,256,680]{2,1,0:T(8,128)(2,1)} %bitcast.230, bf16[680,2048]{1,0:T(8,128)(2,1)} %get-tuple-element.171.refs_2_, bf16[4,512,1024]{2,1,0:T(8,128)(2,1)} %collective-permute-done.36.refs_3_), custom_call_target="tpu_custom_call" | custom-call | tf_op jit(solution)/shard_map/pallas_call | solution.py:374
  249.5 6.7 %multiply_convert_fusion.refs_4_ = bf16[680,2048]{1,0:T(8,128)(2,1)S(1)} fusion(bf16[680,2048]{1,0:T(8,128)(2,1)} %get-tuple-element.179, bf16[680,1024]{1,0:T(8,128)(2,1)} %multiply_convert_fusion.5, bf16[1024,2048]{1,0:T(8,128)(2,1)} %shard_map.183), kind=kOutput, calls=%fused_computation.18 | convolution fusion | flops 2856304640 | bytes 11157504 | tf_op jit(solution)/shard_map/dot_general | solution.py:293
  258.9 7.5 %fusion.72 = f32[680,1024]{1,0:T(8,128)} fusion(bf16[680,2048]{1,0:T(8,128)(2,1)S(1)} %copy-done.30, bf16[1024,2048]{1,0:T(8,128)(2,1)} %collective-permute-done.37), kind=kOutput, calls=%fused_computation.256 | convolution fusion | flops 2852126720 | bytes 9764864 | tf_op jit(solution)/shard_map/dot_general | solution.py:293
  266.5 5.9 %multiply_add_fusion.2 = (f32[680,1024]{1,0:T(8,128)}, f32[680,1024]{1,0:T(8,128)S(1)}) fusion(f32[680,1024]{1,0:T(8,128)S(1)} %copy-done.3, f32[1024]{0:T(1024)S(1)} %get-tuple-element.377, f32[680,1024]{1,0:T(8,128)} %fusion.72, bf16[680,2048]{1,0:T(8,128)(2,1)S(1)} %copy-done.28, bf16[1024,2048]{1,0:T(8,128)(2,1)S(1)} %copy-done.23), kind=kOutput, calls=%fused_computation.37 | convolution fusion | flops 2854215680 | bytes 18124800 | tf_op jit(solution)/shard_map/dot_general | solution.py:293
  274.9 6.1 %multiply_convert_fusion.1.refs_4_ = bf16[680,2048]{1,0:T(8,128)(2,1)S(1)} fusion(bf16[680,2048]{1,0:T(8,128)(2,1)} %get-tuple-element.178, bf16[680,1024]{1,0:T(8,128)(2,1)S(1)} %copy-done.19, bf16[1024,2048]{1,0:T(8,128)(2,1)} %collective-permute-done.37), kind=kOutput, calls=%fused_computation.19 | convolution fusion | flops 2856304640 | bytes 11157504 | tf_op jit(solution)/shard_map/dot_general | solution.py:293
  288.8 6.1 %multiply_reduce_fusion = (bf16[1024]{0:T(1024)(128)(2,1)S(1)}, f32[680]{0:T(1024)S(1)}, f32[680]{0:T(1024)S(1)}, bf16[1024]{0:T(1024)(128)(2,1)S(1)}, f32[680,1024]{1,0:T(8,128)S(1)}) fusion(f32[680,1024]{1,0:T(8,128)S(1)} %copy-done.3, f32[680]{0:T(1024)S(1)} %add_rsqrt_fusion, f32[680]{0:T(1024)S(1)} %broadcast_multiply_fusion.4, ...), kind=kOutput, calls=%fused_computation.28 | convolution fusion | flops 2859086336 | bytes 15354496 | tf_op jit(solution)/shard_map/dot_general | solution.py:293
  302.0 7.4 %collective-permute-done.39 = bf16[512,1024]{1,0:T(8,128)(2,1)S(1)} collective-permute-done((bf16[512,1024]{1,0:T(8,128)(2,1)S(1)}, bf16[512,1024]{1,0:T(8,128)(2,1)S(1)}, u32[]{:S(2)}, u32[]{:S(2)}) %collective-permute-start.39) | collective-permute-done | bytes 1048608 | tf_op jit(solution)/shard_map/ppermute | solution.py:255
  312.9 10.3 %shard_map.185 = bf16[4,512,1280]{2,1,0:T(8,128)(2,1)} custom-call(s32[2,4]{1,0:T(2,128)} %pad_add_fusion.refs_0_, bf16[4,256,680]{2,1,0:T(8,128)(2,1)} %bitcast.235, bf16[680,512]{1,0:T(8,128)(2,1)} %shard_map.180.refs_2_.mixed_ref, bf16[4,256,680]{2,1,0:T(8,128)(2,1)} %bitcast.233, bf16[680,2048]{1,0:T(8,128)(2,1)} %copy-done.29), custom_call_target="tpu_custom_call" | custom-call | tf_op jit(solution)/shard_map/pallas_call | solution.py:374
  333.8 11.5 %shard_map.186 = bf16[4,512,1280]{2,1,0:T(8,128)(2,1)} custom-call(s32[2,4]{1,0:T(2,128)} %pad_add_fusion.1.refs_0_, bf16[4,256,680]{2,1,0:T(8,128)(2,1)} %bitcast.236, bf16[680,512]{1,0:T(8,128)(2,1)} %shard_map.179.refs_2_.mixed_ref, bf16[4,256,680]{2,1,0:T(8,128)(2,1)} %bitcast.234, bf16[680,2048]{1,0:T(8,128)(2,1)} %copy-done.31, ...), custom_call_target="tpu_custom_call" | custom-call | tf_op jit(solution)/shard_map/pallas_call | solution.py:374
  359.4 18.1 %shard_map.187 = (bf16[680,1536]{1,0:T(8,128)(2,1)}, f32[8,512]{1,0:T(8,128)}) custom-call(f32[8]{0:T(128)} %reshape.551.scale_ref, s32[1,680]{1,0:T(1,128)} %constant_dynamic-slice_fusion.2.row_ref, s32[680,1]{1,0:T(8,128)} %copy.85.column_ref, bf16[680,1536]{1,0:T(8,128)(2,1)} %convolution_convert_fusion.raw_ref, ...), custom_call_target="tpu_custom_call" | custom-call | tf_op jit(solution)/shard_map/pallas_call | solution.py:560
  377.5 7.2 %shard_map.188 = bf16[4,512,768]{2,1,0:T(8,128)(2,1)} custom-call(s32[2,4]{1,0:T(2,128)} %pad_add_fusion.refs_0_, bf16[4,256,680]{2,1,0:T(8,128)(2,1)} %bitcast.231, bf16[680,1536]{1,0:T(8,128)(2,1)} %get-tuple-element.191.refs_2_), custom_call_target="tpu_custom_call" | custom-call | tf_op jit(solution)/shard_map/pallas_call | solution.py:374
  395.6 6.4 %fusion.74 = f32[680,1024]{1,0:T(8,128)} fusion(bf16[680,1536]{1,0:T(8,128)(2,1)} %get-tuple-element.191.refs_2_, bf16[1024,1536]{1,0:T(8,128)(2,1)} %collective-permute-done.24), kind=kOutput, calls=%fused_computation.258 | convolution fusion | flops 2139095040 | bytes 8019968 | tf_op jit(solution)/shard_map/dot_general | solution.py:293
  402.0 18.2 %shard_map.189 = (bf16[680,1536]{1,0:T(8,128)(2,1)}, f32[8,512]{1,0:T(8,128)}) custom-call(f32[8]{0:T(128)} %reshape.550.scale_ref, s32[1,680]{1,0:T(1,128)} %constant_dynamic-slice_fusion.2.row_ref, s32[680,1]{1,0:T(8,128)} %copy.85.column_ref, bf16[680,1536]{1,0:T(8,128)(2,1)} %convolution_convert_fusion.1.raw_ref, ...), custom_call_target="tpu_custom_call" | custom-call | tf_op jit(solution)/shard_map/pallas_call | solution.py:560
  421.5 8.0 %shard_map.190 = bf16[4,512,768]{2,1,0:T(8,128)(2,1)} custom-call(s32[2,4]{1,0:T(2,128)} %pad_add_fusion.1.refs_0_, bf16[4,256,680]{2,1,0:T(8,128)(2,1)} %bitcast.232, bf16[680,1536]{1,0:T(8,128)(2,1)} %get-tuple-element.201.refs_2_, bf16[4,512,768]{2,1,0:T(8,128)(2,1)} %collective-permute-done.46.refs_3_), custom_call_target="tpu_custom_call" | custom-call | tf_op jit(solution)/shard_map/pallas_call | solution.py:374
  450.1 19.2 %collective-permute-done.51 = bf16[2,64,1280]{2,1,0:T(8,128)(2,1)} collective-permute-done((bf16[2,64,1280]{2,1,0:T(8,128)(2,1)}, bf16[2,64,1280]{2,1,0:T(8,128)(2,1)}, u32[]{:S(2)}, u32[]{:S(2)}) %collective-permute-start.51) | collective-permute-done | bytes 327712 | tf_op jit(solution)/shard_map/ppermute | solution.py:255
  (462 shorter events, 280.5 us)
Async XLA Ops:
  25.2 27.3 %collective-permute-start.12 = (bf16[340,1024]{1,0:T(8,128)(2,1)}, bf16[340,1024]{1,0:T(8,128)(2,1)}, u32[]{:S(2)}, u32[]{:S(2)}) collective-permute-start(bf16[340,1024]{1,0:T(8,128)(2,1)} %bitcast.227), channel_id=1, source_target_pairs={{0,1},{1,0},{2,3},{3,2},{4,5},{5,4},{6,7},{7,6},{8,9},{9,8},{10,11... | collective-permute-start | bytes 2088968 | tf_op jit(solution)/shard_map/ppermute | solution.py:255
  49.4 38.2 %collective-permute-start.23 = (bf16[340,1024]{1,0:T(8,128)(2,1)S(1)}, bf16[340,1024]{1,0:T(8,128)(2,1)S(1)}, u32[]{:S(2)}, u32[]{:S(2)}) collective-permute-start(bf16[340,1024]{1,0:T(8,128)(2,1)S(1)} %fusion.24), channel_id=1, source_target_pairs={{0,1},{1,0},{2,3},{3,2},{4,5},{5,4},{6,7},{7,6},{8,9},{9,8},{10,11... | collective-permute-start | bytes 2088968 | tf_op jit(solution)/shard_map/ppermute | solution.py:255
  53.6 29.6 %collective-permute-start.17 = (bf16[4,2,64,768]{3,2,1,0:T(8,128)(2,1)S(1)}, bf16[4,2,64,768]{3,2,1,0:T(8,128)(2,1)S(1)}, u32[]{:S(2)}, u32[]{:S(2)}) collective-permute-start(bf16[4,2,64,768]{3,2,1,0:T(8,128)(2,1)S(1)} %pad_maximum_fusion.6.refs_0_), channel_id=1, source_target_pairs={{0,4},{1,5},{2,3},{3,2},{4,0},{5,1},{6,7},{7,6},{8,12},{9,13},{10,... | collective-permute-start | bytes 2359304 | tf_op jit(solution)/shard_map/ppermute | solution.py:255
  60.3 22.9 %collective-permute-start.18 = (bf16[4,2,64,768]{3,2,1,0:T(8,128)(2,1)S(1)}, bf16[4,2,64,768]{3,2,1,0:T(8,128)(2,1)S(1)}, u32[]{:S(2)}, u32[]{:S(2)}) collective-permute-start(bf16[4,2,64,768]{3,2,1,0:T(8,128)(2,1)S(1)} %pad_maximum_fusion.6.refs_0_), channel_id=1, source_target_pairs={{0,1},{1,0},{2,6},{3,7},{4,5},{5,4},{6,2},{7,3},{8,9},{9,8},{10,14... | collective-permute-start | bytes 2359304 | tf_op jit(solution)/shard_map/ppermute | solution.py:255
  114.5 29.6 %collective-permute-start.25 = (bf16[4,2,64,1280]{3,2,1,0:T(8,128)(2,1)}, bf16[4,2,64,1280]{3,2,1,0:T(8,128)(2,1)}, u32[]{:S(2)}, u32[]{:S(2)}) collective-permute-start(bf16[4,2,64,1280]{3,2,1,0:T(8,128)(2,1)} %pad_maximum_fusion.4.refs_0_), channel_id=1, source_target_pairs={{0,4},{1,5},{2,3},{3,2},{4,0},{5,1},{6,7},{7,6},{8,12},{9,13},{10,... | collective-permute-start | bytes 3932168 | tf_op jit(solution)/shard_map/ppermute | solution.py:255
  115.8 30.1 %collective-permute-start.26 = (bf16[4,2,64,1280]{3,2,1,0:T(8,128)(2,1)}, bf16[4,2,64,1280]{3,2,1,0:T(8,128)(2,1)}, u32[]{:S(2)}, u32[]{:S(2)}) collective-permute-start(bf16[4,2,64,1280]{3,2,1,0:T(8,128)(2,1)} %pad_maximum_fusion.4.refs_0_), channel_id=1, source_target_pairs={{0,1},{1,0},{2,6},{3,7},{4,5},{5,4},{6,2},{7,3},{8,9},{9,8},{10,14... | collective-permute-start | bytes 3932168 | tf_op jit(solution)/shard_map/ppermute | solution.py:255
  117.2 21.7 %collective-permute-start.27 = (bf16[2,64,1024]{2,1,0:T(8,128)(2,1)S(1)}, bf16[2,64,1024]{2,1,0:T(8,128)(2,1)S(1)}, u32[]{:S(2)}, u32[]{:S(2)}) collective-permute-start(bf16[2,64,1024]{2,1,0:T(8,128)(2,1)S(1)} %get-tuple-element.327), channel_id=1, source_target_pairs={{0,8},{1,9},{2,10},{3,11},{4,12},{5,13},{6,14},{7,15},{8,16},{9,17... | collective-permute-start | bytes 786440 | tf_op jit(solution)/shard_map/ppermute | solution.py:255
  118.1 21.9 %collective-permute-start.28 = (bf16[2,64,1024]{2,1,0:T(8,128)(2,1)S(1)}, bf16[2,64,1024]{2,1,0:T(8,128)(2,1)S(1)}, u32[]{:S(2)}, u32[]{:S(2)}) collective-permute-start(bf16[2,64,1024]{2,1,0:T(8,128)(2,1)S(1)} %get-tuple-element.327), channel_id=1, source_target_pairs={{0,16},{1,17},{2,18},{3,19},{4,20},{5,21},{6,22},{7,23},{8,24},{9,... | collective-permute-start | bytes 786440 | tf_op jit(solution)/shard_map/ppermute | solution.py:255
  175.7 23.6 %collective-permute-start.33 = (bf16[4,2,64,1024]{3,2,1,0:T(8,128)(2,1)}, bf16[4,2,64,1024]{3,2,1,0:T(8,128)(2,1)}, u32[]{:S(2)}, u32[]{:S(2)}) collective-permute-start(bf16[4,2,64,1024]{3,2,1,0:T(8,128)(2,1)} %pad_maximum_fusion.5.refs_0_), channel_id=1, source_target_pairs={{0,4},{1,5},{2,3},{3,2},{4,0},{5,1},{6,7},{7,6},{8,12},{9,13},{10,... | collective-permute-start | bytes 3145736 | tf_op jit(solution)/shard_map/ppermute | solution.py:255
  177.2 24.6 %collective-permute-start.34 = (bf16[4,2,64,1024]{3,2,1,0:T(8,128)(2,1)}, bf16[4,2,64,1024]{3,2,1,0:T(8,128)(2,1)}, u32[]{:S(2)}, u32[]{:S(2)}) collective-permute-start(bf16[4,2,64,1024]{3,2,1,0:T(8,128)(2,1)} %pad_maximum_fusion.5.refs_0_), channel_id=1, source_target_pairs={{0,1},{1,0},{2,6},{3,7},{4,5},{5,4},{6,2},{7,3},{8,9},{9,8},{10,14... | collective-permute-start | bytes 3145736 | tf_op jit(solution)/shard_map/ppermute | solution.py:255
  201.8 26.7 %collective-permute-start.35 = (bf16[4,2,64,1024]{3,2,1,0:T(8,128)(2,1)}, bf16[4,2,64,1024]{3,2,1,0:T(8,128)(2,1)}, u32[]{:S(2)}, u32[]{:S(2)}) collective-permute-start(bf16[4,2,64,1024]{3,2,1,0:T(8,128)(2,1)} %collective-permute-done.33.refs_1_), channel_id=1, source_target_pairs={{0,1},{1,0},{2,6},{3,7},{4,5},{5,4},{6,2},{7,3},{8,9},{9,8},{10,14... | collective-permute-start | bytes 3145736 | tf_op jit(solution)/shard_map/ppermute | solution.py:255
  256.4 25.2 %collective-permute-start.38 = (bf16[2,512,1024]{2,1,0:T(8,128)(2,1)S(1)}, bf16[2,512,1024]{2,1,0:T(8,128)(2,1)S(1)}, u32[]{:S(2)}, u32[]{:S(2)}) collective-permute-start(bf16[2,512,1024]{2,1,0:T(8,128)(2,1)S(1)} %slice.230), channel_id=1, source_target_pairs={{0,1},{1,0},{2,6},{3,7},{4,5},{5,4},{6,2},{7,3},{8,9},{9,8},{10,14... | collective-permute-start | bytes 6291464 | tf_op jit(solution)/shard_map/ppermute | solution.py:255
  327.6 22.6 %collective-permute-start.42 = (bf16[2,64,1024]{2,1,0:T(8,128)(2,1)S(1)}, bf16[2,64,1024]{2,1,0:T(8,128)(2,1)}, u32[]{:S(2)}, u32[]{:S(2)}) collective-permute-start(bf16[2,64,1024]{2,1,0:T(8,128)(2,1)S(1)} %get-tuple-element.311), channel_id=1, source_target_pairs={{0,16},{1,17},{2,18},{3,19},{4,20},{5,21},{6,22},{7,23},{8,24},{9,... | collective-permute-start | bytes 786440 | tf_op jit(solution)/shard_map/ppermute | solution.py:255
  329.0 23.8 %collective-permute-start.43 = (bf16[2,64,1024]{2,1,0:T(8,128)(2,1)S(1)}, bf16[2,64,1024]{2,1,0:T(8,128)(2,1)}, u32[]{:S(2)}, u32[]{:S(2)}) collective-permute-start(bf16[2,64,1024]{2,1,0:T(8,128)(2,1)S(1)} %get-tuple-element.310), channel_id=1, source_target_pairs={{0,24},{1,25},{2,26},{3,27},{4,28},{5,29},{6,30},{7,31},{8,0},{9,1... | collective-permute-start | bytes 786440 | tf_op jit(solution)/shard_map/ppermute | solution.py:255
  356.2 31.1 %collective-permute-start.44 = (bf16[2,512,1280]{2,1,0:T(8,128)(2,1)}, bf16[2,512,1280]{2,1,0:T(8,128)(2,1)}, u32[]{:S(2)}, u32[]{:S(2)}) collective-permute-start(bf16[2,512,1280]{2,1,0:T(8,128)(2,1)} %slice.235), channel_id=1, source_target_pairs={{0,1},{1,0},{2,6},{3,7},{4,5},{5,4},{6,2},{7,3},{8,9},{9,8},{10,14... | collective-permute-start | bytes 7864328 | tf_op jit(solution)/shard_map/ppermute | solution.py:255
  387.3 34.2 %collective-permute-start.46 = (bf16[4,512,768]{2,1,0:T(8,128)(2,1)}, bf16[4,512,768]{2,1,0:T(8,128)(2,1)}, u32[]{:S(2)}, u32[]{:S(2)}) collective-permute-start(bf16[4,512,768]{2,1,0:T(8,128)(2,1)} %shard_map.188), channel_id=1, source_target_pairs={{0,2},{1,3},{2,0},{3,1},{4,6},{5,7},{6,4},{7,5},{8,10},{9,11},{10,... | collective-permute-start | bytes 9437192 | tf_op jit(solution)/shard_map/ppermute | solution.py:255
  388.7 57.9 %collective-permute-start.49 = (bf16[340,1024]{1,0:T(8,128)(2,1)}, bf16[340,1024]{1,0:T(8,128)(2,1)}, u32[]{:S(2)}, u32[]{:S(2)}) collective-permute-start(bf16[340,1024]{1,0:T(8,128)(2,1)} %dynamic-slice_convert_fusion.1), channel_id=1, source_target_pairs={{0,1},{1,0},{2,3},{3,2},{4,5},{5,4},{6,7},{7,6},{8,9},{9,8},{10,11... | collective-permute-start | bytes 2088968 | tf_op jit(solution)/shard_map/ppermute | solution.py:255
  393.5 28.0 %collective-permute-start.45 = (bf16[512,1280]{1,0:T(8,128)(2,1)}, bf16[512,1280]{1,0:T(8,128)(2,1)}, u32[]{:S(2)}, u32[]{:S(2)}) collective-permute-start(bf16[512,1280]{1,0:T(8,128)(2,1)} %fusion.21), channel_id=1, source_target_pairs={{0,4},{1,5},{2,3},{3,2},{4,0},{5,1},{6,7},{7,6},{8,12},{9,13},{10,... | collective-permute-start | bytes 3932168 | tf_op jit(solution)/shard_map/ppermute | solution.py:255
  432.3 39.5 %collective-permute-start.47 = (bf16[2,512,768]{2,1,0:T(8,128)(2,1)}, bf16[2,512,768]{2,1,0:T(8,128)(2,1)}, u32[]{:S(2)}, u32[]{:S(2)}) collective-permute-start(bf16[2,512,768]{2,1,0:T(8,128)(2,1)} %slice.238), channel_id=1, source_target_pairs={{0,1},{1,0},{2,6},{3,7},{4,5},{5,4},{6,2},{7,3},{8,9},{9,8},{10,14... | collective-permute-start | bytes 4718600 | tf_op jit(solution)/shard_map/ppermute | solution.py:255
  441.2 28.1 %collective-permute-start.51 = (bf16[2,64,1280]{2,1,0:T(8,128)(2,1)}, bf16[2,64,1280]{2,1,0:T(8,128)(2,1)}, u32[]{:S(2)}, u32[]{:S(2)}) collective-permute-start(bf16[2,64,1280]{2,1,0:T(8,128)(2,1)} %get-tuple-element.308), channel_id=1, source_target_pairs={{0,16},{1,17},{2,18},{3,19},{4,20},{5,21},{6,22},{7,23},{8,24},{9,... | collective-permute-start | bytes 983048 | tf_op jit(solution)/shard_map/ppermute | solution.py:255
  442.2 29.5 %collective-permute-start.52 = (bf16[2,64,1280]{2,1,0:T(8,128)(2,1)}, bf16[2,64,1280]{2,1,0:T(8,128)(2,1)}, u32[]{:S(2)}, u32[]{:S(2)}) collective-permute-start(bf16[2,64,1280]{2,1,0:T(8,128)(2,1)} %get-tuple-element.307), channel_id=1, source_target_pairs={{0,24},{1,25},{2,26},{3,27},{4,28},{5,29},{6,30},{7,31},{8,0},{9,1... | collective-permute-start | bytes 983048 | tf_op jit(solution)/shard_map/ppermute | solution.py:255
  486.2 27.2 %collective-permute-start.63 = (bf16[340,1024]{1,0:T(8,128)(2,1)}, bf16[340,1024]{1,0:T(8,128)(2,1)}, u32[]{:S(2)}, u32[]{:S(2)}) collective-permute-start(bf16[340,1024]{1,0:T(8,128)(2,1)} %dynamic-slice_convert_fusion), channel_id=1, source_target_pairs={{0,1},{1,0},{2,3},{3,2},{4,5},{5,4},{6,7},{7,6},{8,9},{9,8},{10,11... | collective-permute-start | bytes 2088968 | tf_op jit(solution)/shard_map/ppermute | solution.py:255
  490.5 22.9 %collective-permute-start.58 = (bf16[2,64,768]{2,1,0:T(8,128)(2,1)}, bf16[2,64,768]{2,1,0:T(8,128)(2,1)}, u32[]{:S(2)}, u32[]{:S(2)}) collective-permute-start(bf16[2,64,768]{2,1,0:T(8,128)(2,1)} %get-tuple-element.317), channel_id=1, source_target_pairs={{0,8},{1,9},{2,10},{3,11},{4,12},{5,13},{6,14},{7,15},{8,16},{9,17... | collective-permute-start | bytes 589832 | tf_op jit(solution)/shard_map/ppermute | solution.py:255
  491.0 22.4 %collective-permute-start.59 = (bf16[2,64,768]{2,1,0:T(8,128)(2,1)}, bf16[2,64,768]{2,1,0:T(8,128)(2,1)}, u32[]{:S(2)}, u32[]{:S(2)}) collective-permute-start(bf16[2,64,768]{2,1,0:T(8,128)(2,1)} %get-tuple-element.316), channel_id=1, source_target_pairs={{0,16},{1,17},{2,18},{3,19},{4,20},{5,21},{6,22},{7,23},{8,24},{9,... | collective-permute-start | bytes 589832 | tf_op jit(solution)/shard_map/ppermute | solution.py:255
  (121 other events, 1094.4 us)

commit v3 on v2

--- a/solution.py
+++ b/solution.py
@@ -1,4 +1,5 @@
 import functools
+import math
 
 import jax
 import jax.numpy as jnp
@@ -343,62 +344,37 @@
     )(position, *pieces)
 
 
-def product_kernel(count, with_added, *refs):
-    out, start = refs[-1], 0
-    for n in range(count):
-        left = refs[1 + 2 * n][...]
-        left = left.reshape(left.shape[0] * left.shape[1], left.shape[2])
-        right = refs[2 + 2 * n][...]
-        total = matmul(left, right, NN)
-        columns = pl.ds(start, right.shape[1])
-        if with_added:
-            total = total + refs[1 + 2 * count][0, :, columns].astype(F32)
-        out[0, :, columns] = total.astype(out.dtype)
-        start += right.shape[1]
-
-
-def products(factors, choice, added=None):
-    tokens = factors[0][0].shape[1]
-    span = CS * 64
-    operands, specs, width = [], [], 0
-    for rows, columns in factors:
-        m = columns.shape[1] // TS
-        operands += [rows.reshape(ZS, XS * span, tokens), columns]
-        specs += [
-            pl.BlockSpec((ZS, span, tokens), lambda n, s: (0, s[0, n], 0)),
-            pl.BlockSpec((tokens, m), lambda n, s: (0, s[1, n])),
-        ]
-        width += m
-    block = pl.BlockSpec((1, ZS * span, width), lambda n, s: (n, 0, 0))
-    extra = [] if added is None else [added]
-    return pl.pallas_call(
-        functools.partial(product_kernel, len(factors), len(extra) == 1),
-        out_shape=jax.ShapeDtypeStruct((4, ZS * span, width), BF16),
-        grid_spec=pltpu.PrefetchScalarGridSpec(
-            num_scalar_prefetch=1,
-            grid=(4,),
-            in_specs=specs + [block] * len(extra),
-            out_specs=block,
-        ),
-        cost_estimate=BRIEF,
-        compiler_params=pltpu.CompilerParams(vmem_limit_bytes=VMEM_LIMIT),
-    )(choice, *operands, *extra)
-
-
-def block_choice(core, where):
+def products(factors, added=None):
+    terms = [matmul(rows, columns, TN) for rows, columns in factors]
+    if added is not None:
+        terms = [term + other.astype(F32) for term, other in zip(terms, added)]
+    return [term.astype(BF16) for term in terms]
+
+
+def block(blocks, dx, dt, where):
     z, x, c, t = where
-    dx = jnp.stack([jnp.ones_like(core), core, 1 - core, jnp.zeros_like(core)])
-    dt = jnp.stack([jnp.ones_like(core), 1 - core, core, jnp.zeros_like(core)])
-    return jnp.stack([x ^ dx, t ^ dt]).astype(jnp.int32)
-
-
-def scatter_near(blocks, far):
-    return (blocks[2].astype(F32) + far[0].astype(F32)).astype(BF16)
+    parts = []
+    for values in blocks:
+        m = values.shape[1] // TS
+        values = lax.dynamic_slice_in_dim(values, (t ^ dt) * m, m, 1)
+        values = pick(values.reshape(ZS, XS, CS * 64, m), x ^ dx, 1)
+        parts.append(values.reshape(ZS * CS * 64, m))
+    return parts[0] if len(parts) == 1 else jnp.concatenate(parts, axis=1)
+
+
+def scatter_far(blocks, where):
+    c = where[2]
+    return jnp.stack([block(blocks, 1, 1, where), block(blocks, c, 1 - c, where)])
+
+
+def scatter_near(blocks, far, where):
+    c = where[2]
+    return (block(blocks, 1 - c, c, where).astype(F32) + far[0].astype(F32)).astype(BF16)
 
 
 def scatter_z(blocks, far, near, where):
     z = where[0]
-    whole = blocks[3].astype(F32) + far[1].astype(F32) + near.astype(F32)
+    whole = block(blocks, 0, 0, where).astype(F32) + far[1].astype(F32) + near.astype(F32)
     whole = whole.astype(BF16).reshape(ZS, CS, 64, whole.shape[-1])
     return [pick(whole, (z + k) % ZS) for k in range(ZS)]
 
@@ -604,14 +580,10 @@
 
     pair = 2 * width // heads
 
-    choice_given, choice_kept = block_choice(1 - c, where), block_choice(c, where)
-
-    token_other = send(pick(inputs, 1 - t).astype(BF16), to_t)
+
     label_pair = jnp.stack(in_order(labels[0], labels[1], t)).astype(F32)
     label_tile = jnp.broadcast_to(label_pair[:, None], (2, 128))
-    label_z = send_z(label_tile)
     scale_tile = jnp.broadcast_to(head_scale[None, :], (8, head_scale.shape[0]))
-    scale_other = send(scale_tile, to_t)
     qkv_halves = []
     for side in (c, 1 - c):
         columns = [
@@ -620,20 +592,23 @@
             for n in range(3)
         ]
         qkv_halves.append(jnp.concatenate(columns, axis=1))
-    keep_qkv, give_qkv = qkv_halves
-    keep_qkv, recv_qkv, label_z, scale_other, rest = hold(
-        keep_qkv,
-        send(give_qkv, to_core),
+    keep_qkv, give_qkv, label_tile, scale_tile, inputs = hold(
+        *qkv_halves, label_tile, scale_tile, inputs
+    )
+    recv_qkv, label_z = send(give_qkv, to_core), send_z(label_tile)
+    keep_qkv, recv_qkv, label_z = hold(keep_qkv, recv_qkv, label_z)
+    two_qkv = jnp.stack([keep_qkv, recv_qkv])
+    two_qkv, label_z, inputs, scale_tile, rest = hold(
+        two_qkv,
         label_z,
-        scale_other,
-        (cotangent, w_ada, w_proj, w_fc1, w_fc2, table),
-    )
-    cotangent, w_ada, w_proj, w_fc1, w_fc2, table = rest
-    two_qkv = jnp.stack([keep_qkv, recv_qkv])
+        inputs,
+        scale_tile,
+        (cotangent, w_ada, w_proj, w_fc1, w_fc2, table, scale_ids),
+    )
+    cotangent, w_ada, w_proj, w_fc1, w_fc2, table, scale_ids = rest
     z_qkv = send_z(two_qkv)
+    token_other = send(pick(inputs, 1 - t).astype(BF16), to_t)
     scale_row = pick(scale_ids, t)
-    scales = jnp.concatenate(in_order(head_scale, scale_other[0], t)).reshape(TS, 2, -1)
-    scale_own, scale_oth = pick(scales, c, 1).reshape(-1), pick(scales, 1 - c, 1).reshape(-1)
 
     label_rows = jnp.concatenate([label_tile] + label_z)
     label_rows = jnp.concatenate([label_rows, send(label_rows, to_x)])
@@ -651,32 +626,40 @@
     rest_halves = [halves(w_proj_t, c, quarter), halves(w_fc1, c, hidden_quarter)]
     rest_halves.append(halves(w_fc2_t, c, hidden_quarter))
     keep_rest, give_rest = [jnp.concatenate([part[n] for part in rest_halves], 1) for n in range(2)]
-    cotangent_other = send(pick(cotangent, 1 - t).astype(BF16), to_t)
+    split = quarter + hidden_quarter
     z_qkv, own_part, x_part, token_other, recv_rest = hold(
         z_qkv, own_part, x_part, token_other, send(give_rest, to_core)
     )
 
+    four_qkv = jnp.stack([two_qkv] + z_qkv)
     partial = own_part + x_part
-    four_qkv = jnp.stack([two_qkv] + z_qkv)
+    four_qkv, partial, recv_rest, token_other = hold(four_qkv, partial, recv_rest, token_other)
     near_qkv, far_qkv = send(four_qkv, to_near), send(four_qkv, to_far)
     mod_z = send_terms_z([partial[ZS - k] for k in range(1, ZS)])
-    mod_z, keep_rest = hold(mod_z, keep_rest)
-    split = quarter + hidden_quarter
     two_mid = jnp.stack([keep_rest[:, :split], recv_rest[:, :split]])
     two_fc2 = jnp.stack([keep_rest[:, split:], recv_rest[:, split:]])
+    mod_z, two_mid, two_fc2 = hold(mod_z, two_mid, two_fc2)
     mid_2 = send(two_mid, to_z(2))
     modulation = sum(mod_z, partial[0]).reshape(6, 1, width)
     gain_attn, gain_mlp, scale_attn, scale_mlp, shift_attn, shift_mlp = modulation
     tokens_in = join_image(inputs, token_other, t)
-    near_qkv, far_qkv, mid_2, two_mid = hold(near_qkv, far_qkv, mid_2, two_mid)
+    cotangent_give = pick(cotangent, 1 - t).astype(BF16)
+    near_qkv, far_qkv, mid_2, two_mid, cotangent_give, scale_tile = hold(
+        near_qkv, far_qkv, mid_2, two_mid, cotangent_give, scale_tile
+    )
     last_qkv = send(near_qkv, to_far)
     mid_1, mid_3 = send(two_mid, to_z(1)), send(two_mid, to_z(3))
+    scale_other = send(scale_tile, to_t)
+    cotangent_other = send(cotangent_give, to_t)
     normed_one, inverse_one = layer_norm(tokens_in)
     hidden_one = (normed_one * (1.0 + scale_attn) + shift_attn).astype(BF16)
-    last_qkv, mid_1, mid_3, hidden_one, cotangent_other = hold(
-        last_qkv, mid_1, mid_3, hidden_one, cotangent_other
-    )
+    last_qkv, mid_1, mid_3, hidden_one, scale_other, cotangent_other = hold(
+        last_qkv, mid_1, mid_3, hidden_one, scale_other, cotangent_other
+    )
+    scales = jnp.concatenate(in_order(head_scale, scale_other[0], t)).reshape(TS, 2, -1)
+    scale_own, scale_oth = pick(scales, c, 1).reshape(-1), pick(scales, 1 - c, 1).reshape(-1)
     four_mid = jnp.stack([two_mid, mid_1, mid_2, mid_3])
+    four_mid, last_qkv, two_fc2, hidden_one = hold(four_mid, last_qkv, two_fc2, hidden_one)
     near_mid, far_mid = send(four_mid, to_near), send(four_mid, to_far)
     z_fc2 = send_z(two_fc2)
     (qkv_own,) = assemble([four_qkv, near_qkv, far_qkv, last_qkv], position, [3 * quarter])
@@ -684,11 +667,13 @@
     raw_own, qkv_oth = hold(raw_own, send(qkv_own, to_core))
     raw_oth = matmul(hidden_one, qkv_oth, NN).astype(BF16)
     mixed_own = attend_whole(raw_own, scale_row, scale_own)
-    mixed_own, near_mid, far_mid, z_fc2, raw_oth = hold(mixed_own, near_mid, far_mid, z_fc2, raw_oth)
+    mixed_own, near_mid, far_mid, z_fc2, raw_oth = hold(
+        mixed_own, near_mid, far_mid, z_fc2, raw_oth
+    )
     last_mid = send(near_mid, to_far)
     mixed_oth = attend_whole(raw_oth, scale_row, scale_oth)
-    mixed_oth, last_mid = hold(mixed_oth, last_mid)
     four_fc2 = jnp.stack([two_fc2] + z_fc2)
+    mixed_oth, last_mid, four_fc2 = hold(mixed_oth, last_mid, four_fc2)
     near_fc2, far_fc2 = send(four_fc2, to_near), send(four_fc2, to_far)
     proj_own, fc1_own = assemble(
         [four_mid, near_mid, far_mid, last_mid], position, [quarter, hidden_quarter]
@@ -704,24 +689,27 @@
     hidden_two, fc1_oth = hold(hidden_two, fc1_oth)
 
     def activate(weights):
+        first = (2.0 / jnp.pi) ** 0.5
         before = matmul(hidden_two, weights, NN)
-        active, pull = jax.vjp(functools.partial(jax.nn.gelu, approximate=True), before)
-        return active.astype(BF16), pull(jnp.ones_like(before))[0].astype(BF16)
+        square = before * before
+        gate = 0.5 + 0.5 * jnp.tanh(before * (first + (first * 0.044715) * square))
+        active = before * gate
+        steep = 2.0 * first + (6.0 * first * 0.044715) * square
+        return active.astype(BF16), (gate + active * (1.0 - gate) * steep).astype(BF16)
 
     active_oth, slope_oth = activate(fc1_oth)
     active_oth, slope_oth, near_fc2, far_fc2 = hold(active_oth, slope_oth, near_fc2, far_fc2)
     last_fc2 = send(near_fc2, to_far)
     active_own, slope_own = activate(fc1_own)
-    d_branch_t = d_branch.T
-    given = products([(d_branch_t, active_oth)], choice_given)
+    given = products([(d_branch, active_oth)])
     given, active_own, slope_own, last_fc2 = hold(given, active_own, slope_own, last_fc2)
-    added = send(given, to_core)
+    added = [send(part, to_core) for part in given]
     (fc2_own,) = assemble([four_fc2, near_fc2, far_fc2, last_fc2], position, [hidden_quarter])
     fc2_own, added = hold(fc2_own, added)
     fc2_oth = send(fc2_own, to_core)
-    blocks_fc2 = products([(d_branch_t, active_own)], choice_kept, added)
+    blocks_fc2 = products([(d_branch, active_own)], added)
     blocks_fc2, fc2_oth = hold(blocks_fc2, fc2_oth)
-    far_fc2 = send(blocks_fc2[:2], to_far)
+    far_fc2 = send(scatter_far(blocks_fc2, where), to_far)
     d_before_oth = (matmul(d_branch, fc2_oth, NN) * slope_oth.astype(F32)).astype(BF16)
     d_before_own = (matmul(d_branch, fc2_own, NN) * slope_own.astype(F32)).astype(BF16)
     branch = matmul(active_own, fc2_own, NT) + matmul(active_oth, fc2_oth, NT)
@@ -731,40 +719,36 @@
     d_before_oth, d_before_own, output_give, far_fc2 = hold(
         d_before_oth, d_before_own, output_give, far_fc2
     )
-    near_fc2 = send(scatter_near(blocks_fc2, far_fc2), to_near)
+    near_fc2 = send(scatter_near(blocks_fc2, far_fc2, where), to_near)
     d_hidden_two = matmul(d_before_own, fc1_own, NT) + matmul(d_before_oth, fc1_oth, NT)
     d_scale_mlp = jnp.sum(d_hidden_two * normed_two, axis=0)
     d_shift_mlp = jnp.sum(d_hidden_two, axis=0)
     d_middle = upstream + norm_back(d_hidden_two * (1.0 + scale_mlp), normed_two, inverse_two)
     d_gain_attn = jnp.sum(d_middle * attended, axis=0)
     d_attended = (gain_attn * d_middle).astype(BF16)
-    d_attended, near_fc2 = hold(d_attended, near_fc2)
+    given = products([(d_attended, mixed_oth), (hidden_two, d_before_oth)])
+    given, d_attended, near_fc2 = hold(given, d_attended, near_fc2)
     z_fc2 = scatter_z(blocks_fc2, far_fc2, near_fc2, where)
     own_fc2, others_fc2 = z_fc2[0], send_terms_z(z_fc2[1:])
-    hidden_two_t, d_attended_t = hidden_two.T, d_attended.T
-    given = products([(d_attended_t, mixed_oth), (hidden_two_t, d_before_oth)], choice_given)
-    given, d_attended = hold(given, d_attended)
     d_mixed_oth = matmul(d_attended, proj_oth, NN).astype(BF16)
     d_mixed_own = matmul(d_attended, proj_own, NN).astype(BF16)
-    d_mixed_oth, d_mixed_own, added = hold(d_mixed_oth, d_mixed_own, send(given, to_core))
-    blocks_mid = products(
-        [(d_attended_t, mixed_own), (hidden_two_t, d_before_own)], choice_kept, added
-    )
+    d_mixed_oth, d_mixed_own, added = hold(d_mixed_oth, d_mixed_own, [send(part, to_core) for part in given])
+    blocks_mid = products([(d_attended, mixed_own), (hidden_two, d_before_own)], added)
     blocks_mid, d_mixed_oth, others_fc2 = hold(blocks_mid, d_mixed_oth, others_fc2)
-    far_mid = send(blocks_mid[:2], to_far)
+    far_mid = send(scatter_far(blocks_mid, where), to_far)
     d_raw_oth, terms_oth = attend_back_whole(raw_oth, mixed_oth, d_mixed_oth, scale_row, scale_oth)
-    hidden_one_t = hidden_one.T
-    given = products([(hidden_one_t, d_raw_oth)], choice_given)
+    given = products([(hidden_one, d_raw_oth)])
     given, far_mid, d_mixed_own = hold(given, far_mid, d_mixed_own)
-    near_mid = send(scatter_near(blocks_mid, far_mid), to_near)
-    added, output_other = send(given, to_core), send(output_give, to_t)
+    near_mid = send(scatter_near(blocks_mid, far_mid, where), to_near)
+    added = [send(part, to_core) for part in given]
+    output_other = send(output_give, to_t)
     d_raw_own, terms_own = attend_back_whole(raw_own, mixed_own, d_mixed_own, scale_row, scale_own)
     d_raw_own, near_mid, added = hold(d_raw_own, near_mid, added)
     z_mid = scatter_z(blocks_mid, far_mid, near_mid, where)
     own_mid, others_mid = z_mid[0], send_terms_z(z_mid[1:])
-    blocks_qkv = products([(hidden_one_t, d_raw_own)], choice_kept, added)
+    blocks_qkv = products([(hidden_one, d_raw_own)], added)
     blocks_qkv, d_raw_own = hold(blocks_qkv, d_raw_own)
-    far_qkv = send(blocks_qkv[:2], to_far)
+    far_qkv = send(scatter_far(blocks_qkv, where), to_far)
     d_hidden_one = matmul(d_raw_own, qkv_own, NT) + matmul(d_raw_oth, qkv_oth, NT)
     d_scale_attn = jnp.sum(d_hidden_one * normed_one, axis=0)
     d_shift_attn = jnp.sum(d_hidden_one, axis=0)
@@ -780,18 +764,22 @@
     d_inputs = d_middle + norm_back(d_hidden_one * (1.0 + scale_attn), normed_one, inverse_one)
     inputs_own, inputs_give = own_and_other(d_inputs, t)
     row_other = send(row, to_t)
-    far_qkv, inputs_give, row_other, output_other, others_mid = hold(
-        far_qkv, inputs_give, row_other, output_other, others_mid
-    )
-    near_qkv = send(scatter_near(blocks_qkv, far_qkv), to_near)
+    far_qkv, inputs_give, row_other, output_other = hold(
+        far_qkv, inputs_give, row_other, output_other
+    )
+    near_give, inputs_give, row_other = hold(
+        scatter_near(blocks_qkv, far_qkv, where), inputs_give, row_other
+    )
+    near_qkv = send(near_give, to_near)
     inputs_other = send(inputs_give, to_t)
     mod_rows = jnp.concatenate([row, row_other])
+    near_qkv, mod_z, others_mid = hold(near_qkv, send_z(mod_rows), others_mid)
+    z_qkv = scatter_z(blocks_qkv, far_qkv, near_qkv, where)
+    z_qkv, mod_z, mod_rows = hold(z_qkv, mod_z, mod_rows)
+    own_qkv, others_qkv = z_qkv[0], send_terms_z(z_qkv[1:])
     half_fc2, other_fc2 = scatter_total(own_fc2, others_fc2, where)
     half_mid, other_mid = scatter_total(own_mid, others_mid, where)
-    other_rest = jnp.concatenate([other_mid, other_fc2], axis=1)
-    near_qkv, mod_z, other_rest = hold(near_qkv, send_z(mod_rows), send(other_rest, to_core))
-    z_qkv = scatter_z(blocks_qkv, far_qkv, near_qkv, where)
-    own_qkv, others_qkv = z_qkv[0], send_terms_z(z_qkv[1:])
+    other_rest = send(jnp.concatenate([other_mid, other_fc2], axis=1), to_core)
     mod_rows = jnp.concatenate([mod_rows] + mod_z)
     mod_rows = jnp.concatenate([mod_rows, send(mod_rows, to_x)])
     mod_rows = jnp.concatenate([mod_rows, send(mod_rows, to_core)])

time: 532 us -> 491 us (0.923)
  Pallas kernels: 122 us -> 68.5 us
  local copies, waits for them, and re-layouts: 80.1 us -> 62.2 us
  waiting for transfers between devices: 99.3 us -> 112 us
  matrix products: 103 us -> 115 us
  starting transfers between devices: 62.3 us -> 72.5 us
  other arithmetic: 53.1 us -> 44.9 us
    pallas_call x6 -> x0, Pallas kernels: 54.5 us -> none  [products(): pl.pallas_call(functools.partial(product_kernel, len(factors), len(extra)...]
    ppermute x65 -> x66, waiting for transfers between devices: 99.3 us -> 112 us  [send(): return lax.ppermute(values, BOTH, perm_of(step))]
    dot_general x20 -> x28, matrix products: 102 us -> 114 us  [matmul(): return lax.dot_general(left, right, dims, preferred_element_type=F32)]
    transpose x4 -> x0, local copies, waits for them, and re-layouts: 10.2 us -> none  [the longest x2 5.13 us: on_device_whole(): hidden_two_t, d_attended_t = (hidden_two.T, d_attended.T)]
    ppermute x65 -> x66, starting transfers between devices: 62.3 us -> 72.5 us  [send(): return lax.ppermute(values, BOTH, perm_of(step))]
    dynamic_slice x0 -> x4, local copies, waits for them, and re-layouts: none -> 6.91 us  [block(): values = lax.dynamic_slice_in_dim(values, (t ^ dt) * m, m, 1)]
    slice x3 -> x0, local copies, waits for them, and re-layouts: 6.39 us -> none  [the longest x1 3.42 us: on_device_whole(): far_mid = send(blocks_mid[:2], to_far)]
    unnamed x170 -> x209, local copies, waits for them, and re-layouts: 28.3 us -> 26.9 us
  transfers between devices with their start and end apart: 65 -> 66, of which waited for: 27 -> 27; matrix products, arithmetic and copies ran while one was open for 38% -> 37% of each run, Pallas kernels for 19% -> 12%
where the time goes in v3:
time: 491 us; the launch traced here: 481 us
  matrix products  115 us (23%)
  waiting for transfers between devices  112 us (23%)
  starting transfers between devices  72.5 us (15%)
  Pallas kernels  68.5 us (14%)
  local copies, waits for them, and re-layouts  62.2 us (13%)
  other arithmetic  44.9 us (9%)
  between operations  5.32 us (1%)
    dot_general x28, matrix products, matmul(): return lax.dot_general(left, right, dims, preferred_element_type=F32)  114 us
    ppermute x66, waiting for transfers between devices, send(): return lax.ppermute(values, BOTH, perm_of(step))  112 us
    ppermute x66, starting transfers between devices, send(): return lax.ppermute(values, BOTH, perm_of(step))  72.5 us
    pallas_call x2, Pallas kernels, attend_back_whole(): pl.pallas_call(functools.partial(attend_back_kernel, head_dim), out_shape...  36.4 us
    unnamed x209, local copies, waits for them, and re-layouts  26.9 us
    pallas_call x2, Pallas kernels, attend_whole(): pl.pallas_call(functools.partial(attend_kernel, head_dim), out_shape=jax....  17 us
    pallas_call x3, Pallas kernels, assemble(): pl.pallas_call(functools.partial(assemble_kernel, widths), out_shape=[jax...  15.1 us
  transfers between devices with their start and end apart: 66, of which 27 were waited for; matrix products, arithmetic and copies ran while one was open for 37% of the time, Pallas kernels for 12%

profile of v3, /device:TPU:9, one launch (start us, length us, event | category | flops | bytes accessed | tf_op | source)
XLA Modules:
  0.0 481.3 jit_solution(18177922884664283533)
XLA Ops:
  55.0 13.7 %collective-permute-done.18 = bf16[2,64,1280]{2,1,0:T(8,128)(2,1)S(1)} collective-permute-done((bf16[2,64,1280]{2,1,0:T(8,128)(2,1)S(1)}, bf16[2,64,1280]{2,1,0:T(8,128)(2,1)S(1)}, u32[]{:S(2)}, u32[]{:S(2)}) %collective-permute-start.18) | collective-permute-done | bytes 327712 | tf_op jit(solution)/shard_map/ppermute | solution.py:256
  75.5 12.4 %collective-permute-done.22 = f32[8,8]{1,0:T(8,128)S(1)} collective-permute-done((f32[8,8]{1,0:T(8,128)S(1)}, f32[8,8]{1,0:T(8,128)S(1)}, u32[]{:S(2)}, u32[]{:S(2)}) %collective-permute-start.22) | collective-permute-done | bytes 288 | tf_op jit(solution)/shard_map/ppermute | solution.py:256
  96.4 7.0 %collective-permute-start.24 = (bf16[1024,1536]{1,0:T(8,128)(2,1)}, bf16[1024,1536]{1,0:T(8,128)(2,1)}, u32[]{:S(2)}, u32[]{:S(2)}) collective-permute-start(bf16[1024,1536]{1,0:T(8,128)(2,1)} %shard_map.178), channel_id=1, source_target_pairs={{0,2},{1,3},{2,0},{3,1},{4,6},{5,7},{6,4},{7,5},{8,10},{9,11},{10,... | collective-permute-start | bytes 9437192 | tf_op jit(solution)/shard_map/ppermute | solution.py:256
  111.8 6.0 %convolution_convert_fusion.4.raw_ref = bf16[680,1536]{1,0:T(8,128)(2,1)} fusion(bf16[680,1024]{1,0:T(8,128)(2,1)} %add_convert_fusion.6, bf16[1024,1536]{1,0:T(8,128)(2,1)} %shard_map.178), kind=kOutput, calls=%fused_computation.17 | convolution fusion | flops 2140139520 | bytes 6627328 | tf_op jit(solution)/shard_map/dot_general | solution.py:294
  118.1 5.6 %convolution_convert_fusion.3.raw_ref = bf16[680,1536]{1,0:T(8,128)(2,1)} fusion(bf16[680,1024]{1,0:T(8,128)(2,1)S(1)} %copy-done.44, bf16[1024,1536]{1,0:T(8,128)(2,1)} %collective-permute-done.24), kind=kOutput, calls=%fused_computation.16 | convolution fusion | flops 2140139520 | bytes 6627328 | tf_op jit(solution)/shard_map/dot_general | solution.py:294
  123.7 8.7 %shard_map.179.mixed_ref = bf16[680,512]{1,0:T(8,128)(2,1)} custom-call(f32[8]{0:T(128)} %reshape.419.scale_ref, s32[1,680]{1,0:T(1,128)} %constant_dynamic-slice_fusion.34.row_ref, s32[680,1]{1,0:T(8,128)} %copy.69.column_ref, bf16[680,1536]{1,0:T(8,128)(2,1)} %convolution_convert_fusion.4.raw_ref), custom_call_target="tpu_custom_call" | custom-call | tf_op jit(solution)/shard_map/pallas_call | solution.py:451
  137.4 8.3 %shard_map.180.mixed_ref = bf16[680,512]{1,0:T(8,128)(2,1)} custom-call(f32[8]{0:T(128)} %reshape.420.scale_ref, s32[1,680]{1,0:T(1,128)} %constant_dynamic-slice_fusion.34.row_ref, s32[680,1]{1,0:T(8,128)} %copy.69.column_ref, bf16[680,1536]{1,0:T(8,128)(2,1)} %convolution_convert_fusion.3.raw_ref), custom_call_target="tpu_custom_call" | custom-call | tf_op jit(solution)/shard_map/pallas_call | solution.py:451
  147.8 5.5 %collective-permute-done.30.refs_3_ = bf16[4,2,64,1280]{3,2,1,0:T(8,128)(2,1)} collective-permute-done((bf16[4,2,64,1280]{3,2,1,0:T(8,128)(2,1)}, bf16[4,2,64,1280]{3,2,1,0:T(8,128)(2,1)}, u32[]{:S(2)}, u32[]{:S(2)}) %collective-permute-start.30) | collective-permute-done | bytes 1310752 | tf_op jit(solution)/shard_map/ppermute | solution.py:256
  153.3 5.7 %shard_map.181 = (bf16[1024,512]{1,0:T(8,128)(2,1)}, bf16[1024,2048]{1,0:T(8,128)(2,1)}) custom-call(s32[4]{0:T(128)} %pad_add_fusion.where_ref, bf16[4,2,64,1280]{3,2,1,0:T(8,128)(2,1)} %pad_maximum_fusion.7.refs_0_, bf16[4,2,64,1280]{3,2,1,0:T(8,128)(2,1)} %collective-permute-done.25.refs_1_, bf16[4,2,64,1280]{3,2,1,0:T(8,128)(2,1)} %collective-permute-done.26.refs_2_, ...), custom_call_target="tpu_custom_call" | custom-call | tf_op jit(solution)/shard_map/pallas_call | solution.py:335
  173.8 6.4 %add_convert_fusion.4 = (bf16[680,2048]{1,0:T(8,128)(2,1)}, bf16[680,2048]{1,0:T(8,128)(2,1)S(1)}) fusion(bf16[680,1024]{1,0:T(8,128)(2,1)S(1)} %add_convert_fusion.5, bf16[1024,2048]{1,0:T(8,128)(2,1)S(1)} %collective-permute-done.32), kind=kOutput, calls=%fused_computation.9 | convolution fusion | flops 2873016320 | bytes 11157504 | tf_op jit(solution)/shard_map/dot_general | solution.py:294
  180.2 7.2 %collective-permute-done.33.refs_1_ = bf16[4,2,64,1024]{3,2,1,0:T(8,128)(2,1)S(1)} collective-permute-done((bf16[4,2,64,1024]{3,2,1,0:T(8,128)(2,1)S(1)}, bf16[4,2,64,1024]{3,2,1,0:T(8,128)(2,1)S(1)}, u32[]{:S(2)}, u32[]{:S(2)}) %collective-permute-start.33) | collective-permute-done | bytes 1048608 | tf_op jit(solution)/shard_map/ppermute | solution.py:256
  195.3 7.0 %add_convert_fusion.3 = (bf16[680,2048]{1,0:T(8,128)(2,1)}, bf16[680,2048]{1,0:T(8,128)(2,1)}) fusion(bf16[680,1024]{1,0:T(8,128)(2,1)S(1)} %add_convert_fusion.5, bf16[1024,2048]{1,0:T(8,128)(2,1)S(1)} %copy-done.86), kind=kOutput, calls=%fused_computation.5 | convolution fusion | flops 2873016320 | bytes 11157504 | tf_op jit(solution)/shard_map/dot_general | solution.py:294
  212.3 7.1 %multiply_convert_fusion = bf16[680,2048]{1,0:T(8,128)(2,1)} fusion(bf16[680,2048]{1,0:T(8,128)(2,1)} %get-tuple-element.239, bf16[680,1024]{1,0:T(8,128)(2,1)S(1)} %copy-done.42, bf16[1024,2048]{1,0:T(8,128)(2,1)} %shard_map.182), kind=kOutput, calls=%fused_computation.3 | convolution fusion | flops 2856304640 | bytes 11157504 | tf_op jit(solution)/shard_map/dot_general | solution.py:294
  227.9 5.8 %fusion.71 = f32[680,1024]{1,0:T(8,128)S(1)} fusion(bf16[680,2048]{1,0:T(8,128)(2,1)S(1)} %copy-done.99, bf16[1024,2048]{1,0:T(8,128)(2,1)} %collective-permute-done.37), kind=kOutput, calls=%fused_computation.297 | convolution fusion | flops 2852126720 | bytes 9764864 | tf_op jit(solution)/shard_map/dot_general | solution.py:294
  239.3 6.3 %multiply_convert_fusion.1 = bf16[680,2048]{1,0:T(8,128)(2,1)S(1)} fusion(bf16[680,2048]{1,0:T(8,128)(2,1)} %get-tuple-element.238, bf16[680,1024]{1,0:T(8,128)(2,1)S(1)} %copy-done.43, bf16[1024,2048]{1,0:T(8,128)(2,1)} %collective-permute-done.37), kind=kOutput, calls=%fused_computation.4 | convolution fusion | flops 2856304640 | bytes 11157504 | tf_op jit(solution)/shard_map/dot_general | solution.py:294
  245.6 6.1 %collective-permute-done.38 = bf16[2,512,1024]{2,1,0:T(8,128)(2,1)S(1)} collective-permute-done((bf16[2,512,1024]{2,1,0:T(8,128)(2,1)S(1)}, bf16[2,512,1024]{2,1,0:T(8,128)(2,1)S(1)}, u32[]{:S(2)}, u32[]{:S(2)}) %collective-permute-start.38) | collective-permute-done | bytes 2097184 | tf_op jit(solution)/shard_map/ppermute | solution.py:256
  294.5 7.8 %collective-permute-done.43 = bf16[2,64,1024]{2,1,0:T(8,128)(2,1)S(1)} collective-permute-done((bf16[2,64,1024]{2,1,0:T(8,128)(2,1)S(1)}, bf16[2,64,1024]{2,1,0:T(8,128)(2,1)S(1)}, u32[]{:S(2)}, u32[]{:S(2)}) %collective-permute-start.43) | collective-permute-done | bytes 262176 | tf_op jit(solution)/shard_map/ppermute | solution.py:256
  312.4 18.2 %shard_map.183 = (bf16[680,1536]{1,0:T(8,128)(2,1)}, f32[8,512]{1,0:T(8,128)}) custom-call(f32[8]{0:T(128)} %reshape.420.scale_ref, s32[1,680]{1,0:T(1,128)} %constant_dynamic-slice_fusion.34.row_ref, s32[680,1]{1,0:T(8,128)} %copy.69.column_ref, bf16[680,1536]{1,0:T(8,128)(2,1)} %convolution_convert_fusion.3.raw_ref, ...), custom_call_target="tpu_custom_call" | custom-call | tf_op jit(solution)/shard_map/pallas_call | solution.py:536
  330.6 6.4 %convolution_convert_fusion = bf16[1024,1536]{1,0:T(8,128)(2,1)} fusion(bf16[680,1024]{1,0:T(8,128)(2,1)} %add_convert_fusion.6, bf16[680,1536]{1,0:T(8,128)(2,1)} %get-tuple-element.252), kind=kOutput, calls=%fused_computation.13 | convolution fusion | flops 2140667904 | bytes 6627328 | tf_op jit(solution)/shard_map/dot_general | solution.py:294
  336.9 6.0 %collective-permute-done.45 = bf16[2,512,1280]{2,1,0:T(8,128)(2,1)} collective-permute-done((bf16[2,512,1280]{2,1,0:T(8,128)(2,1)}, bf16[2,512,1280]{2,1,0:T(8,128)(2,1)}, u32[]{:S(2)}, u32[]{:S(2)}) %collective-permute-start.45) | collective-permute-done | bytes 2621472 | tf_op jit(solution)/shard_map/ppermute | solution.py:256
  354.5 6.5 %fusion.73 = f32[680,1024]{1,0:T(8,128)} fusion(bf16[680,1536]{1,0:T(8,128)(2,1)} %get-tuple-element.252, bf16[1024,1536]{1,0:T(8,128)(2,1)} %collective-permute-done.24), kind=kOutput, calls=%fused_computation.299 | convolution fusion | flops 2139095040 | bytes 8019968 | tf_op jit(solution)/shard_map/dot_general | solution.py:294
  361.0 18.2 %shard_map.184 = (bf16[680,1536]{1,0:T(8,128)(2,1)}, f32[8,512]{1,0:T(8,128)}) custom-call(f32[8]{0:T(128)} %reshape.419.scale_ref, s32[1,680]{1,0:T(1,128)} %constant_dynamic-slice_fusion.34.row_ref, s32[680,1]{1,0:T(8,128)} %copy.69.column_ref, bf16[680,1536]{1,0:T(8,128)(2,1)} %convolution_convert_fusion.4.raw_ref, ...), custom_call_target="tpu_custom_call" | custom-call | tf_op jit(solution)/shard_map/pallas_call | solution.py:536
  380.5 5.6 %add_convert_fusion.2 = bf16[1024,1536]{1,0:T(8,128)(2,1)S(1)} fusion(bf16[1024,1536]{1,0:T(8,128)(2,1)} %collective-permute-done.47, bf16[680,1024]{1,0:T(8,128)(2,1)S(1)} %copy-done.45, bf16[680,1536]{1,0:T(8,128)(2,1)} %get-tuple-element.263), kind=kOutput, calls=%fused_computation.2 | convolution fusion | flops 2143813632 | bytes 9773056 | tf_op jit(solution)/shard_map/dot_general | solution.py:294
  414.6 19.7 %collective-permute-done.56 = bf16[2,64,1280]{2,1,0:T(8,128)(2,1)S(1)} collective-permute-done((bf16[2,64,1280]{2,1,0:T(8,128)(2,1)S(1)}, bf16[2,64,1280]{2,1,0:T(8,128)(2,1)S(1)}, u32[]{:S(2)}, u32[]{:S(2)}) %collective-permute-start.56) | collective-permute-done | bytes 327712 | tf_op jit(solution)/shard_map/ppermute | solution.py:256
  (515 shorter events, 268.9 us)
Async XLA Ops:
  12.9 28.1 %collective-permute-start.4 = (bf16[2,64,768]{2,1,0:T(8,128)(2,1)S(1)}, bf16[2,64,768]{2,1,0:T(8,128)(2,1)}, u32[]{:S(2)}, u32[]{:S(2)}) collective-permute-start(bf16[2,64,768]{2,1,0:T(8,128)(2,1)S(1)} %pad_maximum_fusion.16), channel_id=1, source_target_pairs={{0,8},{1,9},{2,10},{3,11},{4,12},{5,13},{6,14},{7,15},{8,16},{9,17... | collective-permute-start | bytes 589832 | tf_op jit(solution)/shard_map/ppermute | solution.py:256
  13.0 28.4 %collective-permute-start.5 = (bf16[2,64,768]{2,1,0:T(8,128)(2,1)S(1)}, bf16[2,64,768]{2,1,0:T(8,128)(2,1)}, u32[]{:S(2)}, u32[]{:S(2)}) collective-permute-start(bf16[2,64,768]{2,1,0:T(8,128)(2,1)S(1)} %pad_maximum_fusion.16), channel_id=1, source_target_pairs={{0,16},{1,17},{2,18},{3,19},{4,20},{5,21},{6,22},{7,23},{8,24},{9,... | collective-permute-start | bytes 589832 | tf_op jit(solution)/shard_map/ppermute | solution.py:256
  16.1 25.3 %collective-permute-start.6 = (bf16[2,64,768]{2,1,0:T(8,128)(2,1)S(1)}, bf16[2,64,768]{2,1,0:T(8,128)(2,1)}, u32[]{:S(2)}, u32[]{:S(2)}) collective-permute-start(bf16[2,64,768]{2,1,0:T(8,128)(2,1)S(1)} %pad_maximum_fusion.16), channel_id=1, source_target_pairs={{0,24},{1,25},{2,26},{3,27},{4,28},{5,29},{6,30},{7,31},{8,0},{9,1... | collective-permute-start | bytes 589832 | tf_op jit(solution)/shard_map/ppermute | solution.py:256
  22.7 22.6 %collective-permute-start.11 = (bf16[340,1024]{1,0:T(8,128)(2,1)}, bf16[340,1024]{1,0:T(8,128)(2,1)}, u32[]{:S(2)}, u32[]{:S(2)}) collective-permute-start(bf16[340,1024]{1,0:T(8,128)(2,1)} %fusion.17), channel_id=1, source_target_pairs={{0,1},{1,0},{2,3},{3,2},{4,5},{5,4},{6,7},{7,6},{8,9},{9,8},{10,11... | collective-permute-start | bytes 2088968 | tf_op jit(solution)/shard_map/ppermute | solution.py:256
  46.5 22.2 %collective-permute-start.16 = (bf16[4,2,64,768]{3,2,1,0:T(8,128)(2,1)S(1)}, bf16[4,2,64,768]{3,2,1,0:T(8,128)(2,1)S(1)}, u32[]{:S(2)}, u32[]{:S(2)}) collective-permute-start(bf16[4,2,64,768]{3,2,1,0:T(8,128)(2,1)S(1)} %pad_maximum_fusion.9.refs_0_), channel_id=1, source_target_pairs={{0,4},{1,5},{2,3},{3,2},{4,0},{5,1},{6,7},{7,6},{8,12},{9,13},{10,... | collective-permute-start | bytes 2359304 | tf_op jit(solution)/shard_map/ppermute | solution.py:256
  46.8 21.9 %collective-permute-start.17 = (bf16[4,2,64,768]{3,2,1,0:T(8,128)(2,1)S(1)}, bf16[4,2,64,768]{3,2,1,0:T(8,128)(2,1)S(1)}, u32[]{:S(2)}, u32[]{:S(2)}) collective-permute-start(bf16[4,2,64,768]{3,2,1,0:T(8,128)(2,1)S(1)} %pad_maximum_fusion.9.refs_0_), channel_id=1, source_target_pairs={{0,1},{1,0},{2,6},{3,7},{4,5},{5,4},{6,2},{7,3},{8,9},{9,8},{10,14... | collective-permute-start | bytes 2359304 | tf_op jit(solution)/shard_map/ppermute | solution.py:256
  104.9 29.8 %collective-permute-start.25 = (bf16[4,2,64,1280]{3,2,1,0:T(8,128)(2,1)}, bf16[4,2,64,1280]{3,2,1,0:T(8,128)(2,1)}, u32[]{:S(2)}, u32[]{:S(2)}) collective-permute-start(bf16[4,2,64,1280]{3,2,1,0:T(8,128)(2,1)} %pad_maximum_fusion.7.refs_0_), channel_id=1, source_target_pairs={{0,4},{1,5},{2,3},{3,2},{4,0},{5,1},{6,7},{7,6},{8,12},{9,13},{10,... | collective-permute-start | bytes 3932168 | tf_op jit(solution)/shard_map/ppermute | solution.py:256
  106.2 30.1 %collective-permute-start.26 = (bf16[4,2,64,1280]{3,2,1,0:T(8,128)(2,1)}, bf16[4,2,64,1280]{3,2,1,0:T(8,128)(2,1)}, u32[]{:S(2)}, u32[]{:S(2)}) collective-permute-start(bf16[4,2,64,1280]{3,2,1,0:T(8,128)(2,1)} %pad_maximum_fusion.7.refs_0_), channel_id=1, source_target_pairs={{0,1},{1,0},{2,6},{3,7},{4,5},{5,4},{6,2},{7,3},{8,9},{9,8},{10,14... | collective-permute-start | bytes 3932168 | tf_op jit(solution)/shard_map/ppermute | solution.py:256
  106.7 25.7 %collective-permute-start.27 = (bf16[2,64,1024]{2,1,0:T(8,128)(2,1)S(1)}, bf16[2,64,1024]{2,1,0:T(8,128)(2,1)S(1)}, u32[]{:S(2)}, u32[]{:S(2)}) collective-permute-start(bf16[2,64,1024]{2,1,0:T(8,128)(2,1)S(1)} %copy-done.58), channel_id=1, source_target_pairs={{0,8},{1,9},{2,10},{3,11},{4,12},{5,13},{6,14},{7,15},{8,16},{9,17... | collective-permute-start | bytes 786440 | tf_op jit(solution)/shard_map/ppermute | solution.py:256
  107.0 25.4 %collective-permute-start.28 = (bf16[2,64,1024]{2,1,0:T(8,128)(2,1)S(1)}, bf16[2,64,1024]{2,1,0:T(8,128)(2,1)}, u32[]{:S(2)}, u32[]{:S(2)}) collective-permute-start(bf16[2,64,1024]{2,1,0:T(8,128)(2,1)S(1)} %copy-done.58), channel_id=1, source_target_pairs={{0,16},{1,17},{2,18},{3,19},{4,20},{5,21},{6,22},{7,23},{8,24},{9,... | collective-permute-start | bytes 786440 | tf_op jit(solution)/shard_map/ppermute | solution.py:256
  163.9 23.4 %collective-permute-start.33 = (bf16[4,2,64,1024]{3,2,1,0:T(8,128)(2,1)S(1)}, bf16[4,2,64,1024]{3,2,1,0:T(8,128)(2,1)S(1)}, u32[]{:S(2)}, u32[]{:S(2)}) collective-permute-start(bf16[4,2,64,1024]{3,2,1,0:T(8,128)(2,1)S(1)} %copy-done.25), channel_id=1, source_target_pairs={{0,4},{1,5},{2,3},{3,2},{4,0},{5,1},{6,7},{7,6},{8,12},{9,13},{10,... | collective-permute-start | bytes 3145736 | tf_op jit(solution)/shard_map/ppermute | solution.py:256
  165.4 24.3 %collective-permute-start.34 = (bf16[4,2,64,1024]{3,2,1,0:T(8,128)(2,1)S(1)}, bf16[4,2,64,1024]{3,2,1,0:T(8,128)(2,1)S(1)}, u32[]{:S(2)}, u32[]{:S(2)}) collective-permute-start(bf16[4,2,64,1024]{3,2,1,0:T(8,128)(2,1)S(1)} %copy-done.25), channel_id=1, source_target_pairs={{0,1},{1,0},{2,6},{3,7},{4,5},{5,4},{6,2},{7,3},{8,9},{9,8},{10,14... | collective-permute-start | bytes 3145736 | tf_op jit(solution)/shard_map/ppermute | solution.py:256
  226.5 25.2 %collective-permute-start.38 = (bf16[2,512,1024]{2,1,0:T(8,128)(2,1)S(1)}, bf16[2,512,1024]{2,1,0:T(8,128)(2,1)S(1)}, u32[]{:S(2)}, u32[]{:S(2)}) collective-permute-start(bf16[2,512,1024]{2,1,0:T(8,128)(2,1)S(1)} %pad_maximum_fusion.5), channel_id=1, source_target_pairs={{0,1},{1,0},{2,6},{3,7},{4,5},{5,4},{6,2},{7,3},{8,9},{9,8},{10,14... | collective-permute-start | bytes 6291464 | tf_op jit(solution)/shard_map/ppermute | solution.py:256
  279.7 22.6 %collective-permute-start.43 = (bf16[2,64,1024]{2,1,0:T(8,128)(2,1)S(1)}, bf16[2,64,1024]{2,1,0:T(8,128)(2,1)S(1)}, u32[]{:S(2)}, u32[]{:S(2)}) collective-permute-start(bf16[2,64,1024]{2,1,0:T(8,128)(2,1)S(1)} %get-tuple-element.395), channel_id=1, source_target_pairs={{0,16},{1,17},{2,18},{3,19},{4,20},{5,21},{6,22},{7,23},{8,24},{9,... | collective-permute-start | bytes 786440 | tf_op jit(solution)/shard_map/ppermute | solution.py:256
  283.7 22.5 %collective-permute-start.44 = (bf16[2,64,1024]{2,1,0:T(8,128)(2,1)S(1)}, bf16[2,64,1024]{2,1,0:T(8,128)(2,1)S(1)}, u32[]{:S(2)}, u32[]{:S(2)}) collective-permute-start(bf16[2,64,1024]{2,1,0:T(8,128)(2,1)S(1)} %get-tuple-element.394), channel_id=1, source_target_pairs={{0,24},{1,25},{2,26},{3,27},{4,28},{5,29},{6,30},{7,31},{8,0},{9,1... | collective-permute-start | bytes 786440 | tf_op jit(solution)/shard_map/ppermute | solution.py:256
  311.8 31.1 %collective-permute-start.45 = (bf16[2,512,1280]{2,1,0:T(8,128)(2,1)}, bf16[2,512,1280]{2,1,0:T(8,128)(2,1)}, u32[]{:S(2)}, u32[]{:S(2)}) collective-permute-start(bf16[2,512,1280]{2,1,0:T(8,128)(2,1)} %pad_maximum_fusion.4), channel_id=1, source_target_pairs={{0,1},{1,0},{2,6},{3,7},{4,5},{5,4},{6,2},{7,3},{8,9},{9,8},{10,14... | collective-permute-start | bytes 7864328 | tf_op jit(solution)/shard_map/ppermute | solution.py:256
  342.9 37.6 %collective-permute-start.47 = (bf16[1024,1536]{1,0:T(8,128)(2,1)}, bf16[1024,1536]{1,0:T(8,128)(2,1)}, u32[]{:S(2)}, u32[]{:S(2)}) collective-permute-start(bf16[1024,1536]{1,0:T(8,128)(2,1)} %convolution_convert_fusion), channel_id=1, source_target_pairs={{0,2},{1,3},{2,0},{3,1},{4,6},{5,7},{6,4},{7,5},{8,10},{9,11},{10,... | collective-permute-start | bytes 9437192 | tf_op jit(solution)/shard_map/ppermute | solution.py:256
  344.6 60.8 %collective-permute-start.50 = (bf16[340,1024]{1,0:T(8,128)(2,1)}, bf16[340,1024]{1,0:T(8,128)(2,1)}, u32[]{:S(2)}, u32[]{:S(2)}) collective-permute-start(bf16[340,1024]{1,0:T(8,128)(2,1)} %dynamic-slice_convert_fusion.1), channel_id=1, source_target_pairs={{0,1},{1,0},{2,3},{3,2},{4,5},{5,4},{6,7},{7,6},{8,9},{9,8},{10,11... | collective-permute-start | bytes 2088968 | tf_op jit(solution)/shard_map/ppermute | solution.py:256
  353.1 27.4 %collective-permute-start.46 = (bf16[512,1280]{1,0:T(8,128)(2,1)}, bf16[512,1280]{1,0:T(8,128)(2,1)S(1)}, u32[]{:S(2)}, u32[]{:S(2)}) collective-permute-start(bf16[512,1280]{1,0:T(8,128)(2,1)} %fusion.6), channel_id=1, source_target_pairs={{0,4},{1,5},{2,3},{3,2},{4,0},{5,1},{6,7},{7,6},{8,12},{9,13},{10,... | collective-permute-start | bytes 3932168 | tf_op jit(solution)/shard_map/ppermute | solution.py:256
  405.4 28.9 %collective-permute-start.56 = (bf16[2,64,1280]{2,1,0:T(8,128)(2,1)S(1)}, bf16[2,64,1280]{2,1,0:T(8,128)(2,1)S(1)}, u32[]{:S(2)}, u32[]{:S(2)}) collective-permute-start(bf16[2,64,1280]{2,1,0:T(8,128)(2,1)S(1)} %get-tuple-element.388), channel_id=1, source_target_pairs={{0,16},{1,17},{2,18},{3,19},{4,20},{5,21},{6,22},{7,23},{8,24},{9,... | collective-permute-start | bytes 983048 | tf_op jit(solution)/shard_map/ppermute | solution.py:256
  405.4 29.6 %collective-permute-start.57 = (bf16[2,64,1280]{2,1,0:T(8,128)(2,1)S(1)}, bf16[2,64,1280]{2,1,0:T(8,128)(2,1)S(1)}, u32[]{:S(2)}, u32[]{:S(2)}) collective-permute-start(bf16[2,64,1280]{2,1,0:T(8,128)(2,1)S(1)} %get-tuple-element.387), channel_id=1, source_target_pairs={{0,24},{1,25},{2,26},{3,27},{4,28},{5,29},{6,30},{7,31},{8,0},{9,1... | collective-permute-start | bytes 983048 | tf_op jit(solution)/shard_map/ppermute | solution.py:256
  411.0 26.0 %collective-permute-start.51 = (bf16[512,768]{1,0:T(8,128)(2,1)S(1)}, bf16[512,768]{1,0:T(8,128)(2,1)S(1)}, u32[]{:S(2)}, u32[]{:S(2)}) collective-permute-start(bf16[512,768]{1,0:T(8,128)(2,1)S(1)} %fusion.10), channel_id=1, source_target_pairs={{0,4},{1,5},{2,3},{3,2},{4,0},{5,1},{6,7},{7,6},{8,12},{9,13},{10,... | collective-permute-start | bytes 2359304 | tf_op jit(solution)/shard_map/ppermute | solution.py:256
  412.1 23.4 %collective-permute-start.52 = (bf16[2,6272]{1,0:T(2,128)(2,1)S(1)}, bf16[2,6272]{1,0:T(2,128)(2,1)S(1)}, u32[]{:S(2)}, u32[]{:S(2)}) collective-permute-start(bf16[2,6272]{1,0:T(2,128)(2,1)S(1)} %pad_maximum_fusion.24), channel_id=1, source_target_pairs={{0,8},{1,9},{2,10},{3,11},{4,12},{5,13},{6,14},{7,15},{8,16},{9,17... | collective-permute-start | bytes 75272 | tf_op jit(solution)/shard_map/ppermute | solution.py:256
  435.0 26.8 %collective-permute-start.63 = (bf16[340,1024]{1,0:T(8,128)(2,1)}, bf16[340,1024]{1,0:T(8,128)(2,1)}, u32[]{:S(2)}, u32[]{:S(2)}) collective-permute-start(bf16[340,1024]{1,0:T(8,128)(2,1)} %dynamic-slice_convert_fusion), channel_id=1, source_target_pairs={{0,1},{1,0},{2,3},{3,2},{4,5},{5,4},{6,7},{7,6},{8,9},{9,8},{10,11... | collective-permute-start | bytes 2088968 | tf_op jit(solution)/shard_map/ppermute | solution.py:256
  (142 other events, 1505.0 us)

commit v4 on v3

--- a/solution.py
+++ b/solution.py
@@ -235,7 +235,7 @@
 NT = (((1,), (1,)), ((), ()))
 TN = (((0,), (0,)), ((), ()))
 HIDDEN = -1e30
-VMEM_LIMIT = 60 * 1024 * 1024
+MIB = 1024 * 1024
 BRIEF = pl.CostEstimate(flops=0, bytes_accessed=0, transcendentals=0)
 
 
@@ -306,11 +306,12 @@
     return [send(terms[k - 1], to_z(k)) for k in range(1, ZS)]
 
 
-def assemble_kernel(widths, where_ref, *refs):
+def assemble_kernel(widths, crossed, where_ref, *refs):
     pieces, outs, sem = refs[:4], refs[4:-1], refs[-1]
     z, x, c, t = where_ref[0], where_ref[1], where_ref[2], where_ref[3]
     for slot, piece in enumerate(pieces):
-        dx, dt = [(0, 0), (1 - c, c), (c, 1 - c), (1, 1)][slot]
+        near = (1 - c, c) if crossed else (0, 1)
+        dx, dt = [(0, 0), near, (1 - near[0], 1 - near[1]), (1, 1)][slot]
         sx, st = x ^ dx, t ^ dt
         for dz in range(ZS):
             for dc in range(CS):
@@ -330,17 +331,17 @@
         pltpu.make_async_copy(out, out, sem.at[which]).wait()
 
 
-def assemble(pieces, position, widths):
+def assemble(pieces, position, widths, crossed=True):
     rows = ZS * XS * CS * 64
     return pl.pallas_call(
-        functools.partial(assemble_kernel, widths),
+        functools.partial(assemble_kernel, widths, crossed),
         out_shape=[jax.ShapeDtypeStruct((rows, TS * width), BF16) for width in widths],
         in_specs=[pl.BlockSpec(memory_space=pltpu.SMEM)]
         + [pl.BlockSpec(memory_space=pl.ANY)] * 4,
         out_specs=[pl.BlockSpec(memory_space=pltpu.VMEM)] * len(widths),
         scratch_shapes=[pltpu.SemaphoreType.DMA((len(widths),))],
         cost_estimate=BRIEF,
-        compiler_params=pltpu.CompilerParams(vmem_limit_bytes=VMEM_LIMIT),
+        compiler_params=pltpu.CompilerParams(vmem_limit_bytes=8 * MIB),
     )(position, *pieces)
 
 
@@ -461,7 +462,7 @@
         out_specs=block,
         scratch_shapes=[pltpu.VMEM((tokens, tokens), F32)],
         cost_estimate=BRIEF,
-        compiler_params=pltpu.CompilerParams(vmem_limit_bytes=VMEM_LIMIT),
+        compiler_params=pltpu.CompilerParams(vmem_limit_bytes=16 * MIB),
     )(all_scale, scale_row[None, :], scale_row[:, None], raw)
 
 
@@ -554,7 +555,7 @@
         ],
         scratch_shapes=[pltpu.VMEM((tokens, tokens), F32)],
         cost_estimate=BRIEF,
-        compiler_params=pltpu.CompilerParams(vmem_limit_bytes=VMEM_LIMIT),
+        compiler_params=pltpu.CompilerParams(vmem_limit_bytes=20 * MIB),
     )(all_scale, scale_row[None, :], scale_row[:, None], raw, mixed, d_mixed)
     return d_raw, jnp.sum(terms[0].reshape(heads, head_dim), axis=1)
 
@@ -596,13 +597,13 @@
         *qkv_halves, label_tile, scale_tile, inputs
     )
     recv_qkv, label_z = send(give_qkv, to_core), send_z(label_tile)
-    keep_qkv, recv_qkv, label_z = hold(keep_qkv, recv_qkv, label_z)
+    scale_other = send(scale_tile, to_t)
+    keep_qkv, recv_qkv, label_z, scale_other = hold(keep_qkv, recv_qkv, label_z, scale_other)
     two_qkv = jnp.stack([keep_qkv, recv_qkv])
-    two_qkv, label_z, inputs, scale_tile, rest = hold(
+    two_qkv, label_z, inputs, rest = hold(
         two_qkv,
         label_z,
         inputs,
-        scale_tile,
         (cotangent, w_ada, w_proj, w_fc1, w_fc2, table, scale_ids),
     )
     cotangent, w_ada, w_proj, w_fc1, w_fc2, table, scale_ids = rest
@@ -634,7 +635,7 @@
     four_qkv = jnp.stack([two_qkv] + z_qkv)
     partial = own_part + x_part
     four_qkv, partial, recv_rest, token_other = hold(four_qkv, partial, recv_rest, token_other)
-    near_qkv, far_qkv = send(four_qkv, to_near), send(four_qkv, to_far)
+    near_qkv, far_qkv = send(four_qkv, to_t), send(four_qkv, to_x)
     mod_z = send_terms_z([partial[ZS - k] for k in range(1, ZS)])
     two_mid = jnp.stack([keep_rest[:, :split], recv_rest[:, :split]])
     two_fc2 = jnp.stack([keep_rest[:, split:], recv_rest[:, split:]])
@@ -644,17 +645,16 @@
     gain_attn, gain_mlp, scale_attn, scale_mlp, shift_attn, shift_mlp = modulation
     tokens_in = join_image(inputs, token_other, t)
     cotangent_give = pick(cotangent, 1 - t).astype(BF16)
-    near_qkv, far_qkv, mid_2, two_mid, cotangent_give, scale_tile = hold(
-        near_qkv, far_qkv, mid_2, two_mid, cotangent_give, scale_tile
-    )
-    last_qkv = send(near_qkv, to_far)
+    near_qkv, far_qkv, mid_2, two_mid, cotangent_give = hold(
+        near_qkv, far_qkv, mid_2, two_mid, cotangent_give
+    )
+    last_qkv = send(near_qkv, to_x)
     mid_1, mid_3 = send(two_mid, to_z(1)), send(two_mid, to_z(3))
-    scale_other = send(scale_tile, to_t)
     cotangent_other = send(cotangent_give, to_t)
     normed_one, inverse_one = layer_norm(tokens_in)
     hidden_one = (normed_one * (1.0 + scale_attn) + shift_attn).astype(BF16)
-    last_qkv, mid_1, mid_3, hidden_one, scale_other, cotangent_other = hold(
-        last_qkv, mid_1, mid_3, hidden_one, scale_other, cotangent_other
+    last_qkv, mid_1, mid_3, hidden_one, cotangent_other = hold(
+        last_qkv, mid_1, mid_3, hidden_one, cotangent_other
     )
     scales = jnp.concatenate(in_order(head_scale, scale_other[0], t)).reshape(TS, 2, -1)
     scale_own, scale_oth = pick(scales, c, 1).reshape(-1), pick(scales, 1 - c, 1).reshape(-1)
@@ -662,7 +662,9 @@
     four_mid, last_qkv, two_fc2, hidden_one = hold(four_mid, last_qkv, two_fc2, hidden_one)
     near_mid, far_mid = send(four_mid, to_near), send(four_mid, to_far)
     z_fc2 = send_z(two_fc2)
-    (qkv_own,) = assemble([four_qkv, near_qkv, far_qkv, last_qkv], position, [3 * quarter])
+    (qkv_own,) = assemble(
+        [four_qkv, near_qkv, far_qkv, last_qkv], position, [3 * quarter], crossed=False
+    )
     raw_own = matmul(hidden_one, qkv_own, NN).astype(BF16)
     raw_own, qkv_oth = hold(raw_own, send(qkv_own, to_core))
     raw_oth = matmul(hidden_one, qkv_oth, NN).astype(BF16)
@@ -734,11 +736,14 @@
     d_mixed_own = matmul(d_attended, proj_own, NN).astype(BF16)
     d_mixed_oth, d_mixed_own, added = hold(d_mixed_oth, d_mixed_own, [send(part, to_core) for part in given])
     blocks_mid = products([(d_attended, mixed_own), (hidden_two, d_before_own)], added)
-    blocks_mid, d_mixed_oth, others_fc2 = hold(blocks_mid, d_mixed_oth, others_fc2)
+    blocks_mid, d_mixed_oth = hold(blocks_mid, d_mixed_oth)
     far_mid = send(scatter_far(blocks_mid, where), to_far)
     d_raw_oth, terms_oth = attend_back_whole(raw_oth, mixed_oth, d_mixed_oth, scale_row, scale_oth)
     given = products([(hidden_one, d_raw_oth)])
-    given, far_mid, d_mixed_own = hold(given, far_mid, d_mixed_own)
+    d_hidden_oth = matmul(d_raw_oth, qkv_oth, NT)
+    given, far_mid, d_mixed_own, d_hidden_oth, others_fc2 = hold(
+        given, far_mid, d_mixed_own, d_hidden_oth, others_fc2
+    )
     near_mid = send(scatter_near(blocks_mid, far_mid, where), to_near)
     added = [send(part, to_core) for part in given]
     output_other = send(output_give, to_t)
@@ -749,7 +754,7 @@
     blocks_qkv = products([(hidden_one, d_raw_own)], added)
     blocks_qkv, d_raw_own = hold(blocks_qkv, d_raw_own)
     far_qkv = send(scatter_far(blocks_qkv, where), to_far)
-    d_hidden_one = matmul(d_raw_own, qkv_own, NT) + matmul(d_raw_oth, qkv_oth, NT)
+    d_hidden_one = matmul(d_raw_own, qkv_own, NT) + d_hidden_oth
     d_scale_attn = jnp.sum(d_hidden_one * normed_one, axis=0)
     d_shift_attn = jnp.sum(d_hidden_one, axis=0)
     d_modulation = jnp.concatenate(
@@ -788,7 +793,10 @@
     scale_sum = jnp.sum(mod_rows[:, 6 * width : 6 * width + 2 * heads].astype(F32), axis=0)
     scale_sum = (scale_sum[:heads] + scale_sum[heads:]).reshape(TS, heads // TS)
     grad_scale = pick(scale_sum, t)
-    grad_ada = matmul(silu_low, d_mod_all, TN).reshape(rows, 6, width)
+    grad_ada = [
+        matmul(silu_low, d_mod_all[:, n * width : (n + 1) * width], TN) for n in range(6)
+    ]
+    grad_ada = jnp.stack(grad_ada).transpose(1, 0, 2)
     d_silu = matmul(d_mod_all, ada_low, NT)
     _, silu_pull = jax.vjp(jax.nn.silu, condition)
     d_condition = silu_pull(d_silu)[0]

time: 491 us -> 467 us (0.951)
  waiting for transfers between devices: 112 us -> 98.4 us
  Pallas kernels: 68.5 us -> 58.1 us
  matrix products: 115 us -> 124 us
  local copies, waits for them, and re-layouts: 62.2 us -> 56.7 us
    ppermute x66, waiting for transfers between devices: 112 us -> 98.4 us  [send(): return lax.ppermute(values, BOTH, perm_of(step))]
    dot_general x28 -> x33, matrix products: 114 us -> 123 us  [matmul(): return lax.dot_general(left, right, dims, preferred_element_type=F32)]
    pallas_call x3, Pallas kernels: 15.1 us -> 9.48 us  [assemble(): pl.pallas_call(functools.partial(assemble_kernel, widths, crossed), out_s...]
    unnamed x209 -> x202, local copies, waits for them, and re-layouts: 26.9 us -> 23.7 us
  transfers between devices with their start and end apart: 66 -> 66, of which waited for: 27 -> 26; matrix products, arithmetic and copies ran while one was open for 37% -> 37% of each run, Pallas kernels for 12% -> 11%
where the time goes in v4:
time: 467 us; the launch traced here: 457 us
  matrix products  124 us (27%)
  waiting for transfers between devices  98.4 us (21%)
  starting transfers between devices  72.6 us (16%)
  Pallas kernels  58.1 us (12%)
  local copies, waits for them, and re-layouts  56.7 us (12%)
  other arithmetic  42.5 us (9%)
  between operations  5.17 us (1%)
    dot_general x33, matrix products, matmul(): return lax.dot_general(left, right, dims, preferred_element_type=F32)  123 us
    ppermute x66, waiting for transfers between devices, send(): return lax.ppermute(values, BOTH, perm_of(step))  98.4 us
    ppermute x66, starting transfers between devices, send(): return lax.ppermute(values, BOTH, perm_of(step))  72.6 us
    pallas_call x2, Pallas kernels, attend_back_whole(): pl.pallas_call(functools.partial(attend_back_kernel, head_dim), out_shape...  34.2 us
    unnamed x202, local copies, waits for them, and re-layouts  23.7 us
    pallas_call x2, Pallas kernels, attend_whole(): pl.pallas_call(functools.partial(attend_kernel, head_dim), out_shape=jax....  14.4 us
    pallas_call x3, Pallas kernels, assemble(): pl.pallas_call(functools.partial(assemble_kernel, widths, crossed), out_s...  9.48 us
  transfers between devices with their start and end apart: 66, of which 26 were waited for; matrix products, arithmetic and copies ran while one was open for 37% of the time, Pallas kernels for 11%

profile of v4, /device:TPU:9, one launch (start us, length us, event | category | flops | bytes accessed | tf_op | source)
XLA Modules:
  0.0 457.4 jit_solution(9922085311072431096)
XLA Ops:
  54.5 13.2 %collective-permute-done.19 = bf16[2,64,1280]{2,1,0:T(8,128)(2,1)S(1)} collective-permute-done((bf16[2,64,1280]{2,1,0:T(8,128)(2,1)S(1)}, bf16[2,64,1280]{2,1,0:T(8,128)(2,1)S(1)}, u32[]{:S(2)}, u32[]{:S(2)}) %collective-permute-start.19) | collective-permute-done | bytes 327712 | tf_op jit(solution)/shard_map/ppermute | solution.py:256
  74.3 4.9 %collective-permute-done.21 = bf16[2,64,1280]{2,1,0:T(8,128)(2,1)S(1)} collective-permute-done((bf16[2,64,1280]{2,1,0:T(8,128)(2,1)S(1)}, bf16[2,64,1280]{2,1,0:T(8,128)(2,1)S(1)}, u32[]{:S(2)}, u32[]{:S(2)}) %collective-permute-start.21) | collective-permute-done | bytes 327712 | tf_op jit(solution)/shard_map/ppermute | solution.py:256
  79.3 8.5 %collective-permute-done.22 = bf16[2,64,1280]{2,1,0:T(8,128)(2,1)S(1)} collective-permute-done((bf16[2,64,1280]{2,1,0:T(8,128)(2,1)S(1)}, bf16[2,64,1280]{2,1,0:T(8,128)(2,1)S(1)}, u32[]{:S(2)}, u32[]{:S(2)}) %collective-permute-start.22) | collective-permute-done | bytes 327712 | tf_op jit(solution)/shard_map/ppermute | solution.py:256
  104.3 5.6 %convolution_convert_fusion.3.raw_ref = bf16[680,1536]{1,0:T(8,128)(2,1)} fusion(bf16[680,1024]{1,0:T(8,128)(2,1)S(1)} %copy-done.48, bf16[1024,1536]{1,0:T(8,128)(2,1)} %collective-permute-done.24), kind=kOutput, calls=%fused_computation.16 | convolution fusion | flops 2140139520 | bytes 6627328 | tf_op jit(solution)/shard_map/dot_general | solution.py:294
  109.9 7.3 %shard_map.179.mixed_ref = bf16[680,512]{1,0:T(8,128)(2,1)S(1)} custom-call(f32[8]{0:T(128)S(1)} %reshape.416.scale_ref, s32[1,680]{1,0:T(1,128)S(1)} %constant_dynamic-slice_fusion.34.row_ref, s32[680,1]{1,0:T(8,128)S(1)} %copy.65.column_ref, bf16[680,1536]{1,0:T(8,128)(2,1)S(1)} %convolution_convert_fusion.4.raw_ref), custom_call_target="tpu_custom_call" | custom-call | tf_op jit(solution)/shard_map/pallas_call | solution.py:452
  127.4 7.1 %shard_map.180.mixed_ref = bf16[680,512]{1,0:T(8,128)(2,1)S(1)} custom-call(f32[8]{0:T(128)S(1)} %reshape.417.scale_ref, s32[1,680]{1,0:T(1,128)S(1)} %constant_dynamic-slice_fusion.34.row_ref, s32[680,1]{1,0:T(8,128)S(1)} %copy.65.column_ref, bf16[680,1536]{1,0:T(8,128)(2,1)S(1)} %copy-done.2), custom_call_target="tpu_custom_call" | custom-call | tf_op jit(solution)/shard_map/pallas_call | solution.py:452
  134.7 7.3 %collective-permute-done.30.refs_3_ = bf16[4,2,64,1280]{3,2,1,0:T(8,128)(2,1)} collective-permute-done((bf16[4,2,64,1280]{3,2,1,0:T(8,128)(2,1)}, bf16[4,2,64,1280]{3,2,1,0:T(8,128)(2,1)}, u32[]{:S(2)}, u32[]{:S(2)}) %collective-permute-start.30) | collective-permute-done | bytes 1310752 | tf_op jit(solution)/shard_map/ppermute | solution.py:256
  149.5 5.6 %collective-permute-done.31 = bf16[1024,512]{1,0:T(8,128)(2,1)S(1)} collective-permute-done((bf16[1024,512]{1,0:T(8,128)(2,1)S(1)}, bf16[1024,512]{1,0:T(8,128)(2,1)S(1)}, u32[]{:S(2)}, u32[]{:S(2)}) %collective-permute-start.31) | collective-permute-done | bytes 1048608 | tf_op jit(solution)/shard_map/ppermute | solution.py:256
  160.3 6.4 %add_convert_fusion.4 = (bf16[680,2048]{1,0:T(8,128)(2,1)}, bf16[680,2048]{1,0:T(8,128)(2,1)S(1)}) fusion(bf16[680,1024]{1,0:T(8,128)(2,1)S(1)} %add_convert_fusion.5, bf16[1024,2048]{1,0:T(8,128)(2,1)S(1)} %collective-permute-done.32), kind=kOutput, calls=%fused_computation.9 | convolution fusion | flops 2873016320 | bytes 11157504 | tf_op jit(solution)/shard_map/dot_general | solution.py:294
  166.6 5.1 %collective-permute-done.33.refs_1_ = bf16[4,2,64,1024]{3,2,1,0:T(8,128)(2,1)S(1)} collective-permute-done((bf16[4,2,64,1024]{3,2,1,0:T(8,128)(2,1)S(1)}, bf16[4,2,64,1024]{3,2,1,0:T(8,128)(2,1)S(1)}, u32[]{:S(2)}, u32[]{:S(2)}) %collective-permute-start.33) | collective-permute-done | bytes 1048608 | tf_op jit(solution)/shard_map/ppermute | solution.py:256
  177.4 7.1 %add_convert_fusion.3 = (bf16[680,2048]{1,0:T(8,128)(2,1)}, bf16[680,2048]{1,0:T(8,128)(2,1)}) fusion(bf16[680,1024]{1,0:T(8,128)(2,1)S(1)} %add_convert_fusion.5, bf16[1024,2048]{1,0:T(8,128)(2,1)S(1)} %get-tuple-element.222), kind=kOutput, calls=%fused_computation.5 | convolution fusion | flops 2873016320 | bytes 11157504 | tf_op jit(solution)/shard_map/dot_general | solution.py:294
  196.7 6.7 %multiply_convert_fusion = bf16[680,2048]{1,0:T(8,128)(2,1)S(1)} fusion(bf16[680,2048]{1,0:T(8,128)(2,1)} %get-tuple-element.236, bf16[680,1024]{1,0:T(8,128)(2,1)} %copy-done.44, bf16[1024,2048]{1,0:T(8,128)(2,1)} %shard_map.182), kind=kOutput, calls=%fused_computation.3 | convolution fusion | flops 2856304640 | bytes 11157504 | tf_op jit(solution)/shard_map/dot_general | solution.py:294
  203.4 6.7 %add_convert_fusion.1 = bf16[1024,2048]{1,0:T(8,128)(2,1)S(1)} fusion(bf16[1024,2048]{1,0:T(8,128)(2,1)} %collective-permute-done.36, bf16[680,1024]{1,0:T(8,128)(2,1)S(1)} %copy-done.45, bf16[680,2048]{1,0:T(8,128)(2,1)S(1)} %copy-done.90), kind=kOutput, calls=%fused_computation.1 | convolution fusion | flops 2858418176 | bytes 12566528 | tf_op jit(solution)/shard_map/dot_general | solution.py:294
  214.4 7.6 %fusion.81 = f32[680,1024]{1,0:T(8,128)} fusion(bf16[680,2048]{1,0:T(8,128)(2,1)S(1)} %copy-done.96, bf16[1024,2048]{1,0:T(8,128)(2,1)} %collective-permute-done.37), kind=kOutput, calls=%fused_computation.313 | convolution fusion | flops 2852126720 | bytes 9764864 | tf_op jit(solution)/shard_map/dot_general | solution.py:294
  222.0 6.2 %multiply_add_fusion.4 = (f32[680,1024]{1,0:T(8,128)S(1)}, f32[680,1024]{1,0:T(8,128)S(1)}) fusion(f32[680,1024]{1,0:T(8,128)S(1)} %copy-done.22, f32[1024]{0:T(1024)S(1)} %get-tuple-element.456, f32[680,1024]{1,0:T(8,128)} %fusion.81, bf16[680,2048]{1,0:T(8,128)(2,1)S(1)} %copy-done.91, bf16[1024,2048]{1,0:T(8,128)(2,1)} %shard_map.182), kind=kOutput, calls=%fused_computation.31 | convolution fusion | flops 2854215680 | bytes 18124800 | tf_op jit(solution)/shard_map/dot_general | solution.py:294
  231.3 5.8 %multiply_convert_fusion.1 = bf16[680,2048]{1,0:T(8,128)(2,1)S(1)} fusion(bf16[680,2048]{1,0:T(8,128)(2,1)S(1)} %copy-done.92, bf16[680,1024]{1,0:T(8,128)(2,1)S(1)} %copy-done.45, bf16[1024,2048]{1,0:T(8,128)(2,1)} %collective-permute-done.37), kind=kOutput, calls=%fused_computation.4 | convolution fusion | flops 2856304640 | bytes 11157504 | tf_op jit(solution)/shard_map/dot_general | solution.py:294
  254.2 5.3 %convolution_convert_fusion.1 = bf16[1024,2048]{1,0:T(8,128)(2,1)} fusion(bf16[680,1024]{1,0:T(8,128)(2,1)S(1)} %copy-done.51, bf16[680,2048]{1,0:T(8,128)(2,1)S(1)} %copy-done.94), kind=kOutput, calls=%fused_computation.14 | convolution fusion | flops 2854223872 | bytes 8372224 | tf_op jit(solution)/shard_map/dot_general | solution.py:294
  273.6 5.3 %add_convert_fusion = bf16[1024,2048]{1,0:T(8,128)(2,1)S(1)} fusion(bf16[1024,2048]{1,0:T(8,128)(2,1)} %collective-permute-done.41, bf16[680,1024]{1,0:T(8,128)(2,1)S(1)} %copy-done.52, bf16[680,2048]{1,0:T(8,128)(2,1)S(1)} %copy-done.89), kind=kOutput, calls=%fused_computation | convolution fusion | flops 2858418176 | bytes 12566528 | tf_op jit(solution)/shard_map/dot_general | solution.py:294
  293.8 17.2 %shard_map.183 = (bf16[680,1536]{1,0:T(8,128)(2,1)S(1)}, f32[8,512]{1,0:T(8,128)S(1)}) custom-call(f32[8]{0:T(128)S(1)} %reshape.417.scale_ref, s32[1,680]{1,0:T(1,128)S(1)} %constant_dynamic-slice_fusion.34.row_ref, s32[680,1]{1,0:T(8,128)S(1)} %copy.65.column_ref, bf16[680,1536]{1,0:T(8,128)(2,1)S(1)} %copy-done.3, bf16[680,512]{1,0:T(8,128)(2,1)S(1)} %copy-done.6, ...), custom_call_target="tpu_custom_call" | custom-call | tf_op jit(solution)/shard_map/pallas_call | solution.py:537
  311.1 6.0 %fusion.83 = f32[680,1024]{1,0:T(8,128)} fusion(bf16[680,1536]{1,0:T(8,128)(2,1)S(1)} %get-tuple-element.248, bf16[1024,1536]{1,0:T(8,128)(2,1)} %collective-permute-done.24), kind=kOutput, calls=%fused_computation.315 | convolution fusion | flops 2139095040 | bytes 8019968 | tf_op jit(solution)/shard_map/dot_general | solution.py:294
  334.3 17.0 %shard_map.184 = (bf16[680,1536]{1,0:T(8,128)(2,1)S(1)}, f32[8,512]{1,0:T(8,128)S(1)}) custom-call(f32[8]{0:T(128)S(1)} %reshape.416.scale_ref, s32[1,680]{1,0:T(1,128)S(1)} %constant_dynamic-slice_fusion.34.row_ref, s32[680,1]{1,0:T(8,128)S(1)} %copy.65.column_ref, bf16[680,1536]{1,0:T(8,128)(2,1)S(1)} %convolution_convert_fusion.4.raw_ref, ...), custom_call_target="tpu_custom_call" | custom-call | tf_op jit(solution)/shard_map/pallas_call | solution.py:537
  355.4 5.6 %add_convert_fusion.2 = bf16[1024,1536]{1,0:T(8,128)(2,1)S(1)} fusion(bf16[1024,1536]{1,0:T(8,128)(2,1)} %collective-permute-done.47, bf16[680,1024]{1,0:T(8,128)(2,1)} %add_convert_fusion.6, bf16[680,1536]{1,0:T(8,128)(2,1)} %copy-done.13), kind=kOutput, calls=%fused_computation.2 | convolution fusion | flops 2143813632 | bytes 9773056 | tf_op jit(solution)/shard_map/dot_general | solution.py:294
  366.3 6.5 %multiply_reduce_fusion.1 = (bf16[1024]{0:T(1024)(128)(2,1)S(1)}, f32[680]{0:T(1024)S(1)}, f32[680]{0:T(1024)S(1)}, bf16[1024]{0:T(1024)(128)(2,1)S(1)}, f32[680,1024]{1,0:T(8,128)}) fusion(f32[680]{0:T(1024)S(1)} %copy-done.81, f32[680]{0:T(1024)S(1)} %copy-done.76, f32[340,1024]{1,0:T(8,128)S(1)} %copy-done.20, f32[340,1024]{1,0:T(8,128)S(1)} %copy-done.17, ...), kind=kOutput, calls=%fused_computation.23 | convolution fusion | flops 2146751232 | bytes 13609600 | tf_op jit(solution)/shard_map/dot_general | solution.py:294
  391.8 18.5 %collective-permute-done.56 = bf16[2,64,1280]{2,1,0:T(8,128)(2,1)S(1)} collective-permute-done((bf16[2,64,1280]{2,1,0:T(8,128)(2,1)S(1)}, bf16[2,64,1280]{2,1,0:T(8,128)(2,1)S(1)}, u32[]{:S(2)}, u32[]{:S(2)}) %collective-permute-start.56) | collective-permute-done | bytes 327712 | tf_op jit(solution)/shard_map/ppermute | solution.py:256
  (512 shorter events, 259.8 us)
Async XLA Ops:
  14.4 24.7 %collective-permute-start.5 = (bf16[2,64,768]{2,1,0:T(8,128)(2,1)S(1)}, bf16[2,64,768]{2,1,0:T(8,128)(2,1)}, u32[]{:S(2)}, u32[]{:S(2)}) collective-permute-start(bf16[2,64,768]{2,1,0:T(8,128)(2,1)S(1)} %pad_maximum_fusion.16), channel_id=1, source_target_pairs={{0,8},{1,9},{2,10},{3,11},{4,12},{5,13},{6,14},{7,15},{8,16},{9,17... | collective-permute-start | bytes 589832 | tf_op jit(solution)/shard_map/ppermute | solution.py:256
  14.5 25.1 %collective-permute-start.6 = (bf16[2,64,768]{2,1,0:T(8,128)(2,1)S(1)}, bf16[2,64,768]{2,1,0:T(8,128)(2,1)}, u32[]{:S(2)}, u32[]{:S(2)}) collective-permute-start(bf16[2,64,768]{2,1,0:T(8,128)(2,1)S(1)} %pad_maximum_fusion.16), channel_id=1, source_target_pairs={{0,16},{1,17},{2,18},{3,19},{4,20},{5,21},{6,22},{7,23},{8,24},{9,... | collective-permute-start | bytes 589832 | tf_op jit(solution)/shard_map/ppermute | solution.py:256
  17.6 21.9 %collective-permute-start.7 = (bf16[2,64,768]{2,1,0:T(8,128)(2,1)S(1)}, bf16[2,64,768]{2,1,0:T(8,128)(2,1)}, u32[]{:S(2)}, u32[]{:S(2)}) collective-permute-start(bf16[2,64,768]{2,1,0:T(8,128)(2,1)S(1)} %pad_maximum_fusion.16), channel_id=1, source_target_pairs={{0,24},{1,25},{2,26},{3,27},{4,28},{5,29},{6,30},{7,31},{8,0},{9,1... | collective-permute-start | bytes 589832 | tf_op jit(solution)/shard_map/ppermute | solution.py:256
  44.7 23.0 %collective-permute-start.17 = (bf16[4,2,64,768]{3,2,1,0:T(8,128)(2,1)S(1)}, bf16[4,2,64,768]{3,2,1,0:T(8,128)(2,1)S(1)}, u32[]{:S(2)}, u32[]{:S(2)}) collective-permute-start(bf16[4,2,64,768]{3,2,1,0:T(8,128)(2,1)S(1)} %pad_maximum_fusion.9.refs_0_), channel_id=1, source_target_pairs={{0,1},{1,0},{2,3},{3,2},{4,5},{5,4},{6,7},{7,6},{8,9},{9,8},{10,11... | collective-permute-start | bytes 2359304 | tf_op jit(solution)/shard_map/ppermute | solution.py:256
  45.0 22.7 %collective-permute-start.18 = (bf16[4,2,64,768]{3,2,1,0:T(8,128)(2,1)S(1)}, bf16[4,2,64,768]{3,2,1,0:T(8,128)(2,1)S(1)}, u32[]{:S(2)}, u32[]{:S(2)}) collective-permute-start(bf16[4,2,64,768]{3,2,1,0:T(8,128)(2,1)S(1)} %pad_maximum_fusion.9.refs_0_), channel_id=1, source_target_pairs={{0,4},{1,5},{2,6},{3,7},{4,0},{5,1},{6,2},{7,3},{8,12},{9,13},{10,... | collective-permute-start | bytes 2359304 | tf_op jit(solution)/shard_map/ppermute | solution.py:256
  93.8 30.1 %collective-permute-start.25 = (bf16[4,2,64,1280]{3,2,1,0:T(8,128)(2,1)}, bf16[4,2,64,1280]{3,2,1,0:T(8,128)(2,1)}, u32[]{:S(2)}, u32[]{:S(2)}) collective-permute-start(bf16[4,2,64,1280]{3,2,1,0:T(8,128)(2,1)} %pad_maximum_fusion.7.refs_0_), channel_id=1, source_target_pairs={{0,4},{1,5},{2,3},{3,2},{4,0},{5,1},{6,7},{7,6},{8,12},{9,13},{10,... | collective-permute-start | bytes 3932168 | tf_op jit(solution)/shard_map/ppermute | solution.py:256
  94.1 30.8 %collective-permute-start.26 = (bf16[4,2,64,1280]{3,2,1,0:T(8,128)(2,1)}, bf16[4,2,64,1280]{3,2,1,0:T(8,128)(2,1)}, u32[]{:S(2)}, u32[]{:S(2)}) collective-permute-start(bf16[4,2,64,1280]{3,2,1,0:T(8,128)(2,1)} %pad_maximum_fusion.7.refs_0_), channel_id=1, source_target_pairs={{0,1},{1,0},{2,6},{3,7},{4,5},{5,4},{6,2},{7,3},{8,9},{9,8},{10,14... | collective-permute-start | bytes 3932168 | tf_op jit(solution)/shard_map/ppermute | solution.py:256
  94.9 22.2 %collective-permute-start.27 = (bf16[2,64,1024]{2,1,0:T(8,128)(2,1)S(1)}, bf16[2,64,1024]{2,1,0:T(8,128)(2,1)S(1)}, u32[]{:S(2)}, u32[]{:S(2)}) collective-permute-start(bf16[2,64,1024]{2,1,0:T(8,128)(2,1)S(1)} %pad_maximum_fusion.15), channel_id=1, source_target_pairs={{0,8},{1,9},{2,10},{3,11},{4,12},{5,13},{6,14},{7,15},{8,16},{9,17... | collective-permute-start | bytes 786440 | tf_op jit(solution)/shard_map/ppermute | solution.py:256
  148.7 23.1 %collective-permute-start.33 = (bf16[4,2,64,1024]{3,2,1,0:T(8,128)(2,1)S(1)}, bf16[4,2,64,1024]{3,2,1,0:T(8,128)(2,1)S(1)}, u32[]{:S(2)}, u32[]{:S(2)}) collective-permute-start(bf16[4,2,64,1024]{3,2,1,0:T(8,128)(2,1)S(1)} %pad_maximum_fusion.8.refs_0_), channel_id=1, source_target_pairs={{0,4},{1,5},{2,3},{3,2},{4,0},{5,1},{6,7},{7,6},{8,12},{9,13},{10,... | collective-permute-start | bytes 3145736 | tf_op jit(solution)/shard_map/ppermute | solution.py:256
  149.0 24.1 %collective-permute-start.34 = (bf16[4,2,64,1024]{3,2,1,0:T(8,128)(2,1)S(1)}, bf16[4,2,64,1024]{3,2,1,0:T(8,128)(2,1)S(1)}, u32[]{:S(2)}, u32[]{:S(2)}) collective-permute-start(bf16[4,2,64,1024]{3,2,1,0:T(8,128)(2,1)S(1)} %pad_maximum_fusion.8.refs_0_), channel_id=1, source_target_pairs={{0,1},{1,0},{2,6},{3,7},{4,5},{5,4},{6,2},{7,3},{8,9},{9,8},{10,14... | collective-permute-start | bytes 3145736 | tf_op jit(solution)/shard_map/ppermute | solution.py:256
  212.9 25.2 %collective-permute-start.38 = (bf16[2,512,1024]{2,1,0:T(8,128)(2,1)S(1)}, bf16[2,512,1024]{2,1,0:T(8,128)(2,1)S(1)}, u32[]{:S(2)}, u32[]{:S(2)}) collective-permute-start(bf16[2,512,1024]{2,1,0:T(8,128)(2,1)S(1)} %pad_maximum_fusion.5), channel_id=1, source_target_pairs={{0,1},{1,0},{2,6},{3,7},{4,5},{5,4},{6,2},{7,3},{8,9},{9,8},{10,14... | collective-permute-start | bytes 6291464 | tf_op jit(solution)/shard_map/ppermute | solution.py:256
  285.1 36.8 %collective-permute-start.42 = (bf16[2,512,1280]{2,1,0:T(8,128)(2,1)}, bf16[2,512,1280]{2,1,0:T(8,128)(2,1)}, u32[]{:S(2)}, u32[]{:S(2)}) collective-permute-start(bf16[2,512,1280]{2,1,0:T(8,128)(2,1)} %pad_maximum_fusion.4), channel_id=1, source_target_pairs={{0,1},{1,0},{2,6},{3,7},{4,5},{5,4},{6,2},{7,3},{8,9},{9,8},{10,14... | collective-permute-start | bytes 7864328 | tf_op jit(solution)/shard_map/ppermute | solution.py:256
  289.5 31.7 %collective-permute-start.43 = (bf16[2,64,1024]{2,1,0:T(8,128)(2,1)S(1)}, bf16[2,64,1024]{2,1,0:T(8,128)(2,1)S(1)}, u32[]{:S(2)}, u32[]{:S(2)}) collective-permute-start(bf16[2,64,1024]{2,1,0:T(8,128)(2,1)S(1)} %get-tuple-element.394), channel_id=1, source_target_pairs={{0,8},{1,9},{2,10},{3,11},{4,12},{5,13},{6,14},{7,15},{8,16},{9,17... | collective-permute-start | bytes 786440 | tf_op jit(solution)/shard_map/ppermute | solution.py:256
  290.6 30.6 %collective-permute-start.44 = (bf16[2,64,1024]{2,1,0:T(8,128)(2,1)S(1)}, bf16[2,64,1024]{2,1,0:T(8,128)(2,1)S(1)}, u32[]{:S(2)}, u32[]{:S(2)}) collective-permute-start(bf16[2,64,1024]{2,1,0:T(8,128)(2,1)S(1)} %get-tuple-element.393), channel_id=1, source_target_pairs={{0,16},{1,17},{2,18},{3,19},{4,20},{5,21},{6,22},{7,23},{8,24},{9,... | collective-permute-start | bytes 786440 | tf_op jit(solution)/shard_map/ppermute | solution.py:256
  293.6 27.6 %collective-permute-start.45 = (bf16[2,64,1024]{2,1,0:T(8,128)(2,1)S(1)}, bf16[2,64,1024]{2,1,0:T(8,128)(2,1)S(1)}, u32[]{:S(2)}, u32[]{:S(2)}) collective-permute-start(bf16[2,64,1024]{2,1,0:T(8,128)(2,1)S(1)} %get-tuple-element.392), channel_id=1, source_target_pairs={{0,24},{1,25},{2,26},{3,27},{4,28},{5,29},{6,30},{7,31},{8,0},{9,1... | collective-permute-start | bytes 786440 | tf_op jit(solution)/shard_map/ppermute | solution.py:256
  322.6 32.8 %collective-permute-start.47 = (bf16[1024,1536]{1,0:T(8,128)(2,1)}, bf16[1024,1536]{1,0:T(8,128)(2,1)}, u32[]{:S(2)}, u32[]{:S(2)}) collective-permute-start(bf16[1024,1536]{1,0:T(8,128)(2,1)} %convolution_convert_fusion), channel_id=1, source_target_pairs={{0,2},{1,3},{2,0},{3,1},{4,6},{5,7},{6,4},{7,5},{8,10},{9,11},{10,... | collective-permute-start | bytes 9437192 | tf_op jit(solution)/shard_map/ppermute | solution.py:256
  323.5 61.5 %collective-permute-start.50 = (bf16[340,1024]{1,0:T(8,128)(2,1)}, bf16[340,1024]{1,0:T(8,128)(2,1)}, u32[]{:S(2)}, u32[]{:S(2)}) collective-permute-start(bf16[340,1024]{1,0:T(8,128)(2,1)} %dynamic-slice_convert_fusion.1), channel_id=1, source_target_pairs={{0,1},{1,0},{2,3},{3,2},{4,5},{5,4},{6,7},{7,6},{8,9},{9,8},{10,11... | collective-permute-start | bytes 2088968 | tf_op jit(solution)/shard_map/ppermute | solution.py:256
  329.4 26.0 %collective-permute-start.46 = (bf16[512,1280]{1,0:T(8,128)(2,1)}, bf16[512,1280]{1,0:T(8,128)(2,1)}, u32[]{:S(2)}, u32[]{:S(2)}) collective-permute-start(bf16[512,1280]{1,0:T(8,128)(2,1)} %fusion.6), channel_id=1, source_target_pairs={{0,4},{1,5},{2,3},{3,2},{4,0},{5,1},{6,7},{7,6},{8,12},{9,13},{10,... | collective-permute-start | bytes 3932168 | tf_op jit(solution)/shard_map/ppermute | solution.py:256
  382.9 27.5 %collective-permute-start.56 = (bf16[2,64,1280]{2,1,0:T(8,128)(2,1)S(1)}, bf16[2,64,1280]{2,1,0:T(8,128)(2,1)S(1)}, u32[]{:S(2)}, u32[]{:S(2)}) collective-permute-start(bf16[2,64,1280]{2,1,0:T(8,128)(2,1)S(1)} %get-tuple-element.386), channel_id=1, source_target_pairs={{0,16},{1,17},{2,18},{3,19},{4,20},{5,21},{6,22},{7,23},{8,24},{9,... | collective-permute-start | bytes 983048 | tf_op jit(solution)/shard_map/ppermute | solution.py:256
  384.9 28.8 %collective-permute-start.57 = (bf16[2,64,1280]{2,1,0:T(8,128)(2,1)S(1)}, bf16[2,64,1280]{2,1,0:T(8,128)(2,1)S(1)}, u32[]{:S(2)}, u32[]{:S(2)}) collective-permute-start(bf16[2,64,1280]{2,1,0:T(8,128)(2,1)S(1)} %get-tuple-element.385), channel_id=1, source_target_pairs={{0,24},{1,25},{2,26},{3,27},{4,28},{5,29},{6,30},{7,31},{8,0},{9,1... | collective-permute-start | bytes 983048 | tf_op jit(solution)/shard_map/ppermute | solution.py:256
  386.3 28.5 %collective-permute-start.51 = (bf16[512,768]{1,0:T(8,128)(2,1)S(1)}, bf16[512,768]{1,0:T(8,128)(2,1)S(1)}, u32[]{:S(2)}, u32[]{:S(2)}) collective-permute-start(bf16[512,768]{1,0:T(8,128)(2,1)S(1)} %fusion.10), channel_id=1, source_target_pairs={{0,4},{1,5},{2,3},{3,2},{4,0},{5,1},{6,7},{7,6},{8,12},{9,13},{10,... | collective-permute-start | bytes 2359304 | tf_op jit(solution)/shard_map/ppermute | solution.py:256
  387.4 27.1 %collective-permute-start.52 = (bf16[2,6272]{1,0:T(2,128)(2,1)S(1)}, bf16[2,6272]{1,0:T(2,128)(2,1)S(1)}, u32[]{:S(2)}, u32[]{:S(2)}) collective-permute-start(bf16[2,6272]{1,0:T(2,128)(2,1)S(1)} %pad_maximum_fusion.24), channel_id=1, source_target_pairs={{0,8},{1,9},{2,10},{3,11},{4,12},{5,13},{6,14},{7,15},{8,16},{9,17... | collective-permute-start | bytes 75272 | tf_op jit(solution)/shard_map/ppermute | solution.py:256
  389.9 24.7 %collective-permute-start.53 = (bf16[2,6272]{1,0:T(2,128)(2,1)S(1)}, bf16[2,6272]{1,0:T(2,128)(2,1)S(1)}, u32[]{:S(2)}, u32[]{:S(2)}) collective-permute-start(bf16[2,6272]{1,0:T(2,128)(2,1)S(1)} %pad_maximum_fusion.24), channel_id=1, source_target_pairs={{0,16},{1,17},{2,18},{3,19},{4,20},{5,21},{6,22},{7,23},{8,24},{9,... | collective-permute-start | bytes 75272 | tf_op jit(solution)/shard_map/ppermute | solution.py:256
  413.7 26.2 %collective-permute-start.63 = (bf16[340,1024]{1,0:T(8,128)(2,1)}, bf16[340,1024]{1,0:T(8,128)(2,1)}, u32[]{:S(2)}, u32[]{:S(2)}) collective-permute-start(bf16[340,1024]{1,0:T(8,128)(2,1)} %dynamic-slice_convert_fusion), channel_id=1, source_target_pairs={{0,1},{1,0},{2,3},{3,2},{4,5},{5,4},{6,7},{7,6},{8,9},{9,8},{10,11... | collective-permute-start | bytes 2088968 | tf_op jit(solution)/shard_map/ppermute | solution.py:256
  (139 other events, 1294.2 us)
